TPU v7x, 512 devices: a whole 4x8x8 slice. The times are simulated.
512 devices in a mesh: seq: 64 (over x, z, core), head: 8 (over y).
Axes of the slice: x: 4, y: 8, z: 8, core: 2. Of those that a mesh axis runs over, the one named last changes fastest.
Arguments:
- query_tokens: bfloat16 [2, 32768, 4096], P(None, 'seq', 'head'), may hold values from -6 to 6
- key_tokens: bfloat16 [2, 32768, 4096], P(None, 'seq', 'head'), may hold values from -16 to 16
- value_tokens: bfloat16 [2, 32768, 4096], P(None, 'seq', 'head'), may hold values from -16 to 16
- token_rates: float32 [3, 2, 16, 32768], P(None, None, 'head', 'seq'), may hold values from 0.1 to 1
- fast_init: bfloat16 [3, 16, 256, 256], P(None, 'head'), may hold values from -0.375 to 0.375
Outputs:
- mixer_out: bfloat16 [2, 32768, 4096], P(None, ('seq', 'head'))
All inputs are finite; a program needn't handle non-finite values.
Results may differ from a plain program's by a relative error of at most 0.017.
Values may be sent and summed in bfloat16 or wider, within the bound.
No kernel may reach another device: no remote copies, remote signals or barrier semaphores. Data moves between devices by JAX's collectives and lax.ppermute only.
A program may use at most 64 MiB of HBM per device.

v0:
```python
import jax
import jax.numpy as jnp
from jax import lax
from jax.sharding import PartitionSpec as P

step_size = 0.05
eps_grad = 1e-05
eps_row = 1e-06


def gradients(current, keys_now, values_now, rate_block):
    rate_cols = jnp.transpose(rate_block, (0, 2, 1))
    gate_proj = jnp.einsum("thd,hde->the", keys_now, current[0], preferred_element_type=jnp.float32)
    up_proj = jnp.einsum("thd,hde->the", keys_now, current[1], preferred_element_type=jnp.float32)
    sigmoid_gate = jax.nn.sigmoid(gate_proj)
    silu_gate = gate_proj * sigmoid_gate
    hidden = (silu_gate * up_proj).astype(jnp.bfloat16)
    scaled_hidden = (hidden.astype(jnp.float32) * rate_cols[2][:, :, None]).astype(jnp.bfloat16)
    grad_down = -jnp.einsum(
        "the,thf->hef", scaled_hidden, values_now, preferred_element_type=jnp.float32
    )
    hidden_grad = -jnp.einsum(
        "thf,hef->the", values_now, current[2], preferred_element_type=jnp.float32
    )
    gate_grad = hidden_grad * up_proj * sigmoid_gate * (1.0 + gate_proj * (1.0 - sigmoid_gate))
    up_grad = hidden_grad * silu_gate
    gate_scaled = (gate_grad * rate_cols[0][:, :, None]).astype(jnp.bfloat16)
    up_scaled = (up_grad * rate_cols[1][:, :, None]).astype(jnp.bfloat16)
    grad_gate = jnp.einsum(
        "thd,the->hde", keys_now, gate_scaled, preferred_element_type=jnp.float32
    )
    grad_up = jnp.einsum("thd,the->hde", keys_now, up_scaled, preferred_element_type=jnp.float32)
    return jnp.stack([grad_gate, grad_up, grad_down])


def renorm(stepped, target):
    return (
        stepped * target * lax.rsqrt(jnp.mean(stepped * stepped, axis=-1, keepdims=True) + eps_row)
    )


def apply_weights(applied, query_now):
    gate_query = jnp.einsum(
        "thd,hde->the", query_now, applied[0], preferred_element_type=jnp.float32
    )
    up_query = jnp.einsum("thd,hde->the", query_now, applied[1], preferred_element_type=jnp.float32)
    hidden_query = (gate_query * jax.nn.sigmoid(gate_query) * up_query).astype(jnp.bfloat16)
    result = jnp.einsum(
        "the,hef->thf", hidden_query, applied[2], preferred_element_type=jnp.float32
    )
    return result.astype(jnp.bfloat16).reshape(result.shape[0], -1)


def body(query_tokens, key_tokens, value_tokens, token_rates, fast_init):
    head_count = fast_init.shape[1]
    head_width = fast_init.shape[2]
    block_count = query_tokens.shape[0]
    tok_rows = query_tokens.shape[1]
    initial = fast_init.astype(jnp.float32)
    target = jnp.sqrt(jnp.mean(initial * initial, axis=-1, keepdims=True))
    fast_state = initial
    current = fast_init
    outputs = []
    for block_index in range(block_count):
        keys_now = key_tokens[block_index].reshape(tok_rows, head_count, head_width)
        values_now = value_tokens[block_index].reshape(tok_rows, head_count, head_width)
        query_now = query_tokens[block_index].reshape(tok_rows, head_count, head_width)
        gradients_now = gradients(current, keys_now, values_now, token_rates[:, block_index])
        summed = lax.psum(gradients_now, "seq")
        grad_rms = jnp.sqrt(jnp.mean(summed * summed, axis=(2, 3), keepdims=True) + eps_grad)
        stepped = fast_state - step_size * summed / grad_rms
        fast_state = renorm(stepped, target)
        current = fast_state.astype(jnp.bfloat16)
        result = apply_weights(current, query_now)
        outputs.append(result)
    return lax.all_to_all(jnp.stack(outputs), "head", split_axis=1, concat_axis=2, tiled=True)


def solution(mesh):
    return jax.shard_map(
        body,
        mesh=mesh,
        in_specs=(
            P(None, "seq", "head"),
            P(None, "seq", "head"),
            P(None, "seq", "head"),
            P(None, None, "head", "seq"),
            P(None, "head", None, None),
        ),
        out_specs=P(None, ("seq", "head"), None),
        check_vma=False,
    )
```

profile of v0, /device:TPU:1, one launch (start us, length us, event | category | flops | bytes accessed | tf_op | source)
XLA Modules:
  0.0 478.3 jit_solution(11405979511401446143)
XLA Ops:
  6.5 1.5 copy.78
  8.0 0.1 fusion.43
  8.1 0.2 copy.134
  8.4 1.3 convolution_bitcast_fusion.6
  9.6 1.3 convolution_bitcast_fusion.7
  11.0 0.2 copy.133
  11.2 1.3 fusion.5
  12.6 1.9 fusion.9
  14.5 0.6 convolution_bitcast_fusion.11
  15.1 0.5 convolution_bitcast_fusion.10
  15.6 1.3 pad_maximum_fusion
  16.9 0.2 all-reduce.5.cloned.1.call-start
  17.1 0.2 copy.136
  17.3 0.2 copy.137
  17.6 204.5 %all-reduce.3.cloned.1.call-done = f32[3,2,256,256]{2,3,1,0:T(8,128)} async-done(((f32[3,2,256,256]{2,3,1,0:T(8,128)}), f32[3,2,256,256]{2,3,1,0:T(8,128)}) %all-reduce.3.cloned.1.call-update) | async-done | bytes 1572880 | tf_op jit(solution)/shard_map/psum | solution.py:69
  222.0 1.8 multiply_reduce_fusion.3
  223.8 0.1 copy-done
  223.9 0.5 fusion
  224.4 0.5 fusion.1
  224.9 0.3 convolution_bitcast_fusion.2
  225.2 0.3 convolution_bitcast_fusion.3
  225.5 0.3 copy-done.2
  225.7 0.3 fusion.3
  226.1 0.5 convolution_bitcast_fusion.8
  226.6 0.6 convolution_bitcast_fusion.9
  227.2 0.5 fusion.8
  227.7 1.3 pad_maximum_fusion.1
  229.0 1.2 copy-done.11
  230.2 1.0 fusion.42
  231.2 2.1 copy.135
  233.4 2.0 copy.138
  235.4 2.3 convolution_bitcast_fusion.5
  237.7 2.8 convolution_convert_fusion.1
  240.6 2.4 copy.108
  243.0 185.5 %all-reduce.5.cloned.1.call-done = f32[3,2,256,256]{2,3,1,0:T(8,128)} async-done(((f32[3,2,256,256]{2,3,1,0:T(8,128)}), f32[3,2,256,256]{2,3,1,0:T(8,128)}) %all-reduce.5.cloned.1.call-update) | async-done | bytes 1572880 | tf_op jit(solution)/shard_map/psum | solution.py:69
  428.5 1.8 multiply_reduce_fusion.1
  430.2 0.1 copy-done.1
  430.3 0.7 multiply_reduce_fusion
  431.0 0.8 multiply_convert_fusion
  431.8 0.9 copy-done.6
  432.7 0.3 convolution_bitcast_fusion.1
  433.0 0.2 copy-done.5
  433.2 1.7 convolution_convert_fusion
  434.8 0.9 copy.109
  435.7 2.4 pad_maximum_fusion.2
  438.2 32.0 %all_to_all.18 = bf16[2,512,512]{2,0,1:T(2,128)(2,1)S(1)} all-to-all(bf16[2,512,512]{2,0,1:T(2,128)(2,1)S(1)} %pad_maximum_fusion.2), channel_id=1, replica_groups=mesh['seq'=64,'head'=8] {'head'}, dimensions={1} | all-to-all | bytes 2097152 | tf_op jit(solution)/shard_map/all_to_all | solution.py:76
  470.2 0.2 copy.110
  470.3 1.1 copy.139
  (31 shorter events, 0.2 us)
Async XLA Ops:
  6.5 1.5 copy-start.9
  6.5 215.5 %all-reduce.3.cloned.1.call-start = ((), (), s32[]{:S(2)}) async-start(), calls=%async_computation.1 | async-start | bytes 3145728 | tf_op jit(solution)/shard_map/psum | solution.py:69
  8.3 2.6 copy-start.10
  11.0 1.6 copy-start.12
  11.2 1.4 copy-start.7
  12.6 1.9 copy-start.8
  16.9 411.6 %all-reduce.5.cloned.1.call-start = ((), (), s32[]{:S(2)}) async-start(), calls=%async_computation.2 | async-start | bytes 3145728 | tf_op jit(solution)/shard_map/psum | solution.py:69
  222.0 1.9 copy-start
  224.9 0.9 copy-start.2
  229.0 1.2 copy-start.11
  231.2 4.2 copy-start.3
  428.5 1.9 copy-start.1
  431.0 1.6 copy-start.4
  431.8 0.9 copy-start.6
  431.8 1.4 copy-start.5
Sparse Core Ops, SparseCore 0:
  17.0 204.9 all-reduce.2
  229.1 199.2 all-reduce.4
where the time goes:
time: 481 us; the launch traced here: 478 us
  waiting for transfers between devices  390 us (81%)
  blocking collectives  32 us (7%)
  matrix products  16.5 us (3%)
  local copies, waits for them, and re-layouts  15 us (3%)
  between operations  13.7 us (3%)
  other arithmetic  10.9 us (2%)
    psum x2, waiting for transfers between devices, body(): summed = lax.psum(gradients_now, 'seq')  390 us
    all_to_all x1, blocking collectives, body(): lax.all_to_all(jnp.stack(outputs), 'head', split_axis=1, concat_axis=2, t...  32 us
  transfers between devices with their start and end apart: 2, of which 2 were waited for; matrix products, arithmetic and copies ran while one was open for 3% of the time, Pallas kernels for 0%

commit v1 on v0

v1 whole, which is shorter than its diff:
```python
import jax
import jax.numpy as jnp
from jax import lax
from jax.experimental import pallas as pl
from jax.experimental.pallas import tpu as pltpu
from jax.sharding import Mesh, PartitionSpec as P

step_size = 0.05
eps_grad = 1e-05
eps_row = 1e-06
f32 = jnp.float32
bf16 = jnp.bfloat16
NT = (((1,), (1,)), ((), ()))
NN = (((1,), (0,)), ((), ()))


def dot(a, b, dims):
    return lax.dot_general(a, b, dims, preferred_element_type=f32)


def head_init(init_ref):
    return [
        jnp.transpose(init_ref[0, 0].astype(f32)),
        jnp.transpose(init_ref[1, 0].astype(f32)),
        init_ref[2, 0].astype(f32),
    ]


def row_mean(w, i):
    return jnp.mean(w * w, axis=1 if i == 2 else 0, keepdims=True)


def half_gradients(keys, values, rate_gate, rate_up, rate_down, w_gate, w_up, w_down):
    gate = dot(w_gate, keys, NT)
    up = dot(w_up, keys, NT)
    err = dot(w_down, values, NT)
    sig = jax.nn.sigmoid(gate)
    silu = gate * sig
    hidden = (silu * up).astype(bf16)
    scaled = (hidden.astype(f32) * rate_down).astype(bf16)
    gate_grad = err * up * sig * (1.0 + gate * (1.0 - sig))
    gate_scaled = (gate_grad * rate_gate).astype(bf16)
    up_scaled = (err * silu * rate_up).astype(bf16)
    return (
        dot(gate_scaled, keys, NN),
        dot(up_scaled, keys, NN),
        dot(scaled, values, NN),
    )


def all_gradients(c, block, weights, k_ref, v_ref, kv_ref, rates_ref, rates_other_ref, out_ref):
    own = half_gradients(
        k_ref[0], v_ref[0], *[rates_ref[i, block, pl.ds(c, 1), :] for i in (0, 1, 2)], *weights
    )
    other = half_gradients(
        kv_ref[0], kv_ref[1], *[rates_other_ref[i, block : block + 1, :] for i in (0, 1, 2)], *weights
    )
    for i in range(3):
        out_ref[256 * i : 256 * (i + 1), :] = (own[i] + other[i]).astype(bf16)


def updated(state, init, grad_ref):
    result = []
    for i in range(3):
        grad = grad_ref[256 * i : 256 * (i + 1), :].astype(f32)
        rms = jnp.sqrt(jnp.mean(grad * grad, keepdims=True) + eps_grad)
        stepped = state[i] + grad * (step_size / rms)
        target = jnp.sqrt(row_mean(init[i], i))
        result.append(stepped * (target * lax.rsqrt(row_mean(stepped, i) + eps_row)))
    return result


def first_kernel(c_ref, init_ref, k_ref, v_ref, kv_ref, rates_ref, rates_other_ref, out_ref):
    weights = [w.astype(bf16) for w in head_init(init_ref)]
    all_gradients(c_ref[0], 0, weights, k_ref, v_ref, kv_ref, rates_ref, rates_other_ref, out_ref)


def second_kernel(
    c_ref, init_ref, grad_ref, k_ref, v_ref, kv_ref, rates_ref, rates_other_ref, out_ref, state_ref, wb_ref
):
    init = head_init(init_ref)
    state = updated(init, init, grad_ref)
    weights = [w.astype(bf16) for w in state]
    for i in range(3):
        state_ref[i] = state[i]
        wb_ref[i] = weights[i]
    all_gradients(c_ref[0], 1, weights, k_ref, v_ref, kv_ref, rates_ref, rates_other_ref, out_ref)


def apply_half(q, weights):
    gate = dot(q, weights[0], NT)
    up = dot(q, weights[1], NT)
    hidden = (gate * jax.nn.sigmoid(gate) * up).astype(bf16)
    return dot(hidden, weights[2], NN).astype(bf16).reshape(8, 1, 64, 256)


def apply_both(c, weights, q_ref, q_other_ref, out_ref):
    out_ref[:, pl.ds(c, 1)] = apply_half(q_ref[0], weights)
    out_ref[:, pl.ds(1 - c, 1)] = apply_half(q_other_ref[...], weights)


def apply_kernel(c_ref, wb_ref, q_ref, q_other_ref, out_ref):
    apply_both(c_ref[0], [wb_ref[0], wb_ref[1], wb_ref[2]], q_ref, q_other_ref, out_ref)


def last_kernel(c_ref, init_ref, state_ref, grad_ref, q_ref, q_other_ref, out_ref):
    state = updated([state_ref[i] for i in range(3)], head_init(init_ref), grad_ref)
    apply_both(c_ref[0], [w.astype(bf16) for w in state], q_ref, q_other_ref, out_ref)


def sum_kernel(part_ref, out_ref):
    total = jnp.sum(part_ref[...].astype(f32), axis=0, keepdims=True)
    out_ref[...] = jnp.broadcast_to(total.astype(bf16), out_ref.shape)


def whole(shape):
    return pl.BlockSpec(shape, lambda i, c: (0,) * len(shape))


def token_spec(block):
    return pl.BlockSpec((1, 512, 256), lambda i, c: (block, 0, c[0]))


INIT = pl.BlockSpec((3, 1, 256, 256), lambda i, c: (0, c[0], 0, 0))
GRAD = ((768, 256), bf16)
STATE = ((3, 256, 256), f32)
WEIGHTS = ((3, 256, 256), bf16)
RESULT = ((8, 2, 64, 256), bf16)


def call(kernel, in_specs, outs, name):
    many = len(outs) > 1
    specs = [whole(shape) for shape, _ in outs]
    shapes = [jax.ShapeDtypeStruct(shape, dtype) for shape, dtype in outs]
    return pl.pallas_call(
        kernel,
        grid_spec=pltpu.PrefetchScalarGridSpec(
            num_scalar_prefetch=1,
            grid=(1,),
            in_specs=in_specs,
            out_specs=specs if many else specs[0],
        ),
        out_shape=shapes if many else shapes[0],
        name=name,
    )


def exchange(array, axes):
    return lax.all_to_all(array, axes, split_axis=0, concat_axis=0, tiled=True)


def reduced(partial):
    parts = exchange(partial.reshape(32, 24, 256), ("x", "z"))
    total = pl.pallas_call(
        sum_kernel, out_shape=jax.ShapeDtypeStruct((32, 24, 256), bf16), name="sum_parts"
    )(parts)
    return exchange(total, ("x", "z")).reshape(768, 256)


def body(query_tokens, key_tokens, value_tokens, token_rates, fast_init):
    core = lax.axis_index("c")
    c = core.astype(jnp.int32).reshape(1)
    swap = [(0, 1), (1, 0)]

    def others(array):
        return jnp.where(core == 0, array[..., 256:], array[..., :256])

    kv_first = lax.ppermute(
        jnp.stack([others(key_tokens[0]), others(value_tokens[0])]), "c", swap
    )
    rates_other = lax.ppermute(
        jnp.where(core == 0, token_rates[:, :, 1], token_rates[:, :, 0]), "c", swap
    )
    rest = lax.ppermute(
        jnp.stack(
            [
                others(key_tokens[1]),
                others(value_tokens[1]),
                others(query_tokens[0]),
                others(query_tokens[1]),
            ]
        ),
        "c",
        swap,
    )
    grad_specs = [
        token_spec(0),
        token_spec(0),
        whole((2, 512, 256)),
        whole((3, 2, 2, 512)),
        whole((3, 2, 512)),
    ]
    grad_specs_second = [token_spec(1), token_spec(1)] + grad_specs[2:]
    first = call(first_kernel, [INIT] + grad_specs, [GRAD], "first_gradients")(
        c, fast_init, key_tokens, value_tokens, kv_first, token_rates, rates_other
    )
    summed = reduced(first)
    second, state, weights = call(
        second_kernel, [INIT, whole((768, 256))] + grad_specs_second, [GRAD, STATE, WEIGHTS], "second_gradients"
    )(c, fast_init, summed, key_tokens, value_tokens, rest[:2], token_rates, rates_other)
    out_first = call(
        apply_kernel, [whole((3, 256, 256)), token_spec(0), whole((512, 256))], [RESULT], "apply_first"
    )(c, weights, query_tokens, rest[2])
    summed = reduced(second)
    out_first = exchange(out_first.reshape(16, 64, 256), ("y", "c"))
    out_second = call(
        last_kernel,
        [INIT, whole((3, 256, 256)), whole((768, 256)), token_spec(1), whole((512, 256))],
        [RESULT],
        "apply_second",
    )(c, fast_init, state, summed, query_tokens, rest[3])
    out_second = exchange(out_second.reshape(16, 64, 256), ("y", "c"))
    return jnp.stack(
        [jnp.transpose(o, (1, 0, 2)).reshape(64, 4096) for o in (out_first, out_second)]
    )


def solution(mesh):
    fine = Mesh(mesh.devices.reshape(4, 8, 2, 8), ("x", "z", "c", "y"))
    seq = ("x", "z", "c")
    return jax.shard_map(
        body,
        mesh=fine,
        in_specs=(
            P(None, seq, "y"),
            P(None, seq, "y"),
            P(None, seq, "y"),
            P(None, None, "y", seq),
            P(None, "y", None, None),
        ),
        out_specs=P(None, (*seq, "y"), None),
        check_vma=False,
    )
```

time: 481 us -> 155 us (0.32)
  waiting for transfers between devices: 390 us -> 58.2 us
  starting transfers between devices: 0.22 us -> 51.2 us
  Pallas kernels: 0 us -> 17.3 us
  matrix products: 16.5 us -> 0 us
  blocking collectives: 32 us -> 18.4 us
  between operations: 13.7 us -> 0.21 us
  other arithmetic: 10.9 us -> 1.43 us
  local copies, waits for them, and re-layouts: 15 us -> 7.48 us
    psum x2 -> x0, waiting for transfers between devices: 390 us -> none  [body(): summed = lax.psum(gradients_now, 'seq')]
    all_to_all x0 -> x5, waiting for transfers between devices: none -> 57.2 us  [exchange(): return lax.all_to_all(array, axes, split_axis=0, concat_axis=0, tiled=True)]
    all_to_all x0 -> x5, starting transfers between devices: none -> 38 us  [exchange(): return lax.all_to_all(array, axes, split_axis=0, concat_axis=0, tiled=True)]
    pallas_call x0 -> x6, Pallas kernels: none -> 17.3 us  [the longest x1 4.02 us: body(): call(second_kernel, [INIT, whole((768, 256))] + grad_specs_second, [GRAD,...]
    dot_general x16 -> x0, matrix products: 16.5 us -> none  [the longest x2 4.5 us: apply_weights(): jnp.einsum('the,hef->thf', hidden_query, applied[2], preferred_element_ty...]
    all_to_all x1, blocking collectives: 32 us -> 18.4 us  [exchange(): return lax.all_to_all(array, axes, split_axis=0, concat_axis=0, tiled=True)]
    ppermute x0 -> x3, starting transfers between devices: none -> 13.2 us  [the longest x1 8.88 us: body(): lax.ppermute(jnp.stack([others(key_tokens[0]), others(value_tokens[0])]),...]
    unnamed x33 -> x16, local copies, waits for them, and re-layouts: 9.29 us -> 3.23 us
  transfers between devices with their start and end apart: 2 -> 8, of which waited for: 2 -> 6; matrix products, arithmetic and copies ran while one was open for 3% -> 2% of each run, Pallas kernels for 0% -> 5%
where the time goes in v1:
time: 155 us; the launch traced here: 154 us
  waiting for transfers between devices  58.2 us (38%)
  starting transfers between devices  51.2 us (33%)
  blocking collectives  18.4 us (12%)
  Pallas kernels  17.3 us (11%)
  local copies, waits for them, and re-layouts  7.48 us (5%)
    all_to_all x5, waiting for transfers between devices, exchange(): return lax.all_to_all(array, axes, split_axis=0, concat_axis=0, tiled=True)  57.2 us
    all_to_all x5, starting transfers between devices, exchange(): return lax.all_to_all(array, axes, split_axis=0, concat_axis=0, tiled=True)  38 us
    all_to_all x1, blocking collectives, exchange(): return lax.all_to_all(array, axes, split_axis=0, concat_axis=0, tiled=True)  18.4 us
    ppermute x1, starting transfers between devices, body(): lax.ppermute(jnp.stack([others(key_tokens[0]), others(value_tokens[0])]),...  8.88 us
    pallas_call x1, Pallas kernels, body(): call(second_kernel, [INIT, whole((768, 256))] + grad_specs_second, [GRAD,...  4.02 us
    pallas_call x2, Pallas kernels, reduced(): pl.pallas_call(sum_kernel, out_shape=jax.ShapeDtypeStruct((32, 24, 256),...  3.66 us
    pallas_call x1, Pallas kernels, body(): call(first_kernel, [INIT] + grad_specs, [GRAD], 'first_gradients')  3.5 us
    pallas_call x1, Pallas kernels, body(): call(last_kernel, [INIT, whole((3, 256, 256)), whole((768, 256)), token_s...  3.44 us
  transfers between devices with their start and end apart: 8, of which 6 were waited for; matrix products, arithmetic and copies ran while one was open for 2% of the time, Pallas kernels for 5%

profile of v1, /device:TPU:1, one launch (start us, length us, event | category | flops | bytes accessed | tf_op | source)
XLA Modules:
  0.0 154.2 jit_solution(10728020927097514028)
XLA Ops:
  0.0 1.4 slice_bitcast_fusion.3
  1.4 0.2 copy-done
  1.5 0.1 slice_bitcast_fusion.2
  1.6 0.0 copy-start.1
  1.6 0.1 fusion.4
  1.7 0.0 copy-start.6
  1.7 0.1 pad_maximum_fusion.2
  1.8 8.9 %collective-permute-start = (bf16[2,512,256]{2,1,0:T(8,128)(2,1)S(1)}, bf16[2,512,256]{2,1,0:T(8,128)(2,1)S(1)}, u32[]{:S(2)}, u32[]{:S(2)}) collective-permute-start(bf16[2,512,256]{2,1,0:T(8,128)(2,1)S(1)} %pad_maximum_fusion.2), channel_id=1, source_target_pairs={{0,8},{8,0},{1,9},{9,1},{2,10},{10,2},{3,11},{11,3},{4,12},{12,4},... | collective-permute-start | bytes 1572872 | tf_op jit(solution)/shard_map/ppermute | solution.py:168
  10.6 0.0 copy-done.6
  10.7 1.9 %collective-permute-start.1 = (f32[3,2,512]{2,1,0:T(2,128)S(1)}, f32[3,2,512]{2,1,0:T(2,128)S(1)}, u32[]{:S(2)}, u32[]{:S(2)}) collective-permute-start(f32[3,2,512]{2,1,0:T(2,128)S(1)} %fusion.6), channel_id=1, source_target_pairs={{0,8},{8,0},{1,9},{9,1},{2,10},{10,2},{3,11},{11,3},{4,12},{12,4},... | collective-permute-start | bytes 36872 | tf_op jit(solution)/shard_map/ppermute | solution.py:171
  12.6 0.0 copy-done.1
  12.6 0.1 slice_bitcast_fusion.1
  12.7 1.1 collective-permute-done.1.rates_other_ref
  13.8 0.0 collective-permute-done.kv_ref
  13.8 0.6 copy-done.7
  14.4 0.2 copy-done.5
  14.6 3.5 %first_gradients.1 = bf16[768,256]{1,0:T(8,128)(2,1)} custom-call(s32[1]{0:T(128)} %bitcast.c_ref, bf16[3,2,256,256]{3,2,1,0:T(8,128)(2,1)} %init_ref.5, bf16[2,512,512]{2,1,0:T(8,128)(2,1)} %k_ref.3, bf16[2,512,512]{2,1,0:T(8,128)(2,1)} %v_ref.3, bf16[2,512,256]{2,1,0:T(8,128)(2,1)} %copy-done.5, f32[3,2,2,512]{3,2,1,0:T(2,128)} %rates_ref.3, ...), custom_call_target="tpu_custom_call" | custom-call | tf_op jit(solution)/shard_map/first_gradients/pallas_call | solution.py:194
  18.1 7.5 %all-to-all-start = ((bf16[32,24,256]{2,1,0:T(8,128)(2,1)}), bf16[32,24,256]{2,1,0:T(8,128)(2,1)S(1)}, u32[]{:S(2)}, u32[]{:S(2)}) async-start(bf16[32,24,256]{2,1,0:T(8,128)(2,1)} %bitcast.43), calls=%async_computation | async-start | bytes 786432 | tf_op jit(solution)/shard_map/all_to_all | solution.py:149
  25.6 0.1 fusion
  25.7 0.1 fusion.2
  25.8 0.1 pad_maximum_fusion
  25.9 2.4 %collective-permute-start.2 = (bf16[4,512,256]{2,1,0:T(8,128)(2,1)S(1)}, bf16[4,512,256]{2,1,0:T(8,128)(2,1)S(1)}, u32[]{:S(2)}, u32[]{:S(2)}) collective-permute-start(bf16[4,512,256]{2,1,0:T(8,128)(2,1)S(1)} %pad_maximum_fusion), channel_id=1, source_target_pairs={{0,8},{8,0},{1,9},{9,1},{2,10},{10,2},{3,11},{11,3},{4,12},{12,4},... | collective-permute-start | bytes 3145736 | tf_op jit(solution)/shard_map/ppermute | solution.py:174
  28.3 9.5 %all-to-all-done.part_ref = bf16[32,24,256]{2,1,0:T(8,128)(2,1)S(1)} async-done(((bf16[32,24,256]{2,1,0:T(8,128)(2,1)}), bf16[32,24,256]{2,1,0:T(8,128)(2,1)S(1)}, u32[]{:S(2)}, u32[]{:S(2)}) %all-to-all-start) | async-done | bytes 393248 | tf_op jit(solution)/shard_map/all_to_all | solution.py:149
  37.8 0.7 copy-done.2
  38.5 1.8 %sum_parts.2 = bf16[32,24,256]{2,1,0:T(8,128)(2,1)} custom-call(bf16[32,24,256]{2,1,0:T(8,128)(2,1)} %copy-done.2), custom_call_target="tpu_custom_call" | custom-call | tf_op jit(solution)/shard_map/sum_parts/pallas_call | solution.py:154
  40.4 7.4 %all-to-all-start.1 = ((bf16[32,24,256]{2,1,0:T(8,128)(2,1)}), bf16[32,24,256]{2,1,0:T(8,128)(2,1)S(1)}, u32[]{:S(2)}, u32[]{:S(2)}) async-start(bf16[32,24,256]{2,1,0:T(8,128)(2,1)} %sum_parts.2), calls=%async_computation.1 | async-start | bytes 786432 | tf_op jit(solution)/shard_map/all_to_all | solution.py:149
  47.7 0.0 collective-permute-done.2
  47.8 0.8 slice.104.kv_ref
  48.6 10.7 %all-to-all-done.1 = bf16[32,24,256]{2,1,0:T(8,128)(2,1)S(1)} async-done(((bf16[32,24,256]{2,1,0:T(8,128)(2,1)}), bf16[32,24,256]{2,1,0:T(8,128)(2,1)S(1)}, u32[]{:S(2)}, u32[]{:S(2)}) %all-to-all-start.1) | async-done | bytes 393248 | tf_op jit(solution)/shard_map/all_to_all | solution.py:149
  59.3 0.7 copy-done.4
  60.0 4.0 %second_gradients.1 = (bf16[768,256]{1,0:T(8,128)(2,1)}, f32[3,256,256]{2,1,0:T(8,128)}, bf16[3,256,256]{2,1,0:T(8,128)(2,1)}) custom-call(s32[1]{0:T(128)} %bitcast.c_ref, bf16[3,2,256,256]{3,2,1,0:T(8,128)(2,1)} %init_ref.5, bf16[768,256]{1,0:T(8,128)(2,1)} %bitcast.45, bf16[2,512,512]{2,1,0:T(8,128)(2,1)} %k_ref.3, bf16[2,512,512]{2,1,0:T(8,128)(2,1)} %v_ref.3, ...), custom_call_target="tpu_custom_call" | custom-call | tf_op jit(solution)/shard_map/second_gradients/pallas_call | solution.py:198
  64.1 18.4 %all_to_all.30.part_ref = bf16[32,24,256]{2,1,0:T(8,128)(2,1)} all-to-all(bf16[32,24,256]{2,1,0:T(8,128)(2,1)} %bitcast.46), channel_id=1, replica_groups=mesh['x'=4,'z'=8,'c'=2,'y'=8] {'x','z'}, dimensions={0} | all-to-all | bytes 786432 | tf_op jit(solution)/shard_map/all_to_all | solution.py:149
  82.5 1.8 %sum_parts.3 = bf16[32,24,256]{2,1,0:T(8,128)(2,1)} custom-call(bf16[32,24,256]{2,1,0:T(8,128)(2,1)} %all_to_all.30.part_ref), custom_call_target="tpu_custom_call" | custom-call | tf_op jit(solution)/shard_map/sum_parts/pallas_call | solution.py:154
  84.3 7.6 %all-to-all-start.4 = ((bf16[32,24,256]{2,1,0:T(8,128)(2,1)}), bf16[32,24,256]{2,1,0:T(8,128)(2,1)S(1)}, u32[]{:S(2)}, u32[]{:S(2)}) async-start(bf16[32,24,256]{2,1,0:T(8,128)(2,1)} %sum_parts.3), calls=%async_computation.4 | async-start | bytes 786432 | tf_op jit(solution)/shard_map/all_to_all | solution.py:149
  91.9 0.8 slice_bitcast_fusion.7
  92.7 2.7 %apply_first.1 = bf16[8,2,64,256]{3,2,1,0:T(8,128)(2,1)} custom-call(s32[1]{0:T(128)} %bitcast.c_ref, bf16[3,256,256]{2,1,0:T(8,128)(2,1)} %get-tuple-element.8.wb_ref, bf16[2,512,512]{2,1,0:T(8,128)(2,1)} %q_ref.3, bf16[512,256]{1,0:T(8,128)(2,1)} %get-tuple-element.11.q_other_ref), custom_call_target="tpu_custom_call" | custom-call | tf_op jit(solution)/shard_map/apply_first/pallas_call | solution.py:201
  95.4 7.0 %all-to-all-done.4 = bf16[32,24,256]{2,1,0:T(8,128)(2,1)S(1)} async-done(((bf16[32,24,256]{2,1,0:T(8,128)(2,1)}), bf16[32,24,256]{2,1,0:T(8,128)(2,1)S(1)}, u32[]{:S(2)}, u32[]{:S(2)}) %all-to-all-start.4) | async-done | bytes 393248 | tf_op jit(solution)/shard_map/all_to_all | solution.py:149
  102.4 0.8 copy-done.3
  103.2 12.1 %all-to-all-start.2 = ((bf16[16,64,256]{2,1,0:T(8,128)(2,1)}), bf16[16,64,256]{2,1,0:T(8,128)(2,1)S(1)}, u32[]{:S(2)}, u32[]{:S(2)}) async-start(bf16[16,64,256]{2,1,0:T(8,128)(2,1)} %bitcast.39), calls=%async_computation.2 | async-start | bytes 1048576 | tf_op jit(solution)/shard_map/all_to_all | solution.py:149
  115.2 3.4 %apply_second.1 = bf16[8,2,64,256]{3,2,1,0:T(8,128)(2,1)} custom-call(s32[1]{0:T(128)} %bitcast.c_ref, bf16[3,2,256,256]{3,2,1,0:T(8,128)(2,1)} %init_ref.5, f32[3,256,256]{2,1,0:T(8,128)} %get-tuple-element.9.state_ref, bf16[768,256]{1,0:T(8,128)(2,1)} %bitcast.44, bf16[2,512,512]{2,1,0:T(8,128)(2,1)} %q_ref.3, bf16[512,256]{1,0:T(8,128)(2,1)} %get-tuple-element.12.q_other_ref), custom_call_target="tpu_custom_call" | custom-call | tf_op jit(solution)/shard_map/apply_second/pallas_call | solution.py:206
  118.7 13.8 %all-to-all-done.2 = bf16[16,64,256]{2,1,0:T(8,128)(2,1)S(1)} async-done(((bf16[16,64,256]{2,1,0:T(8,128)(2,1)}), bf16[16,64,256]{2,1,0:T(8,128)(2,1)S(1)}, u32[]{:S(2)}, u32[]{:S(2)}) %all-to-all-start.2) | async-done | bytes 524320 | tf_op jit(solution)/shard_map/all_to_all | solution.py:149
  132.4 3.5 %all-to-all-start.5 = ((bf16[16,64,256]{2,1,0:T(8,128)(2,1)}), bf16[16,64,256]{2,1,0:T(8,128)(2,1)S(1)}, u32[]{:S(2)}, u32[]{:S(2)}) async-start(bf16[16,64,256]{2,1,0:T(8,128)(2,1)} %bitcast.42), calls=%async_computation.5 | async-start | bytes 1048576 | tf_op jit(solution)/shard_map/all_to_all | solution.py:149
  135.9 0.3 copy.8
  136.2 0.2 stack_reshape.6
  136.5 16.1 %all-to-all-done.5 = bf16[16,64,256]{2,1,0:T(8,128)(2,1)S(1)} async-done(((bf16[16,64,256]{2,1,0:T(8,128)(2,1)}), bf16[16,64,256]{2,1,0:T(8,128)(2,1)S(1)}, u32[]{:S(2)}, u32[]{:S(2)}) %all-to-all-start.5) | async-done | bytes 524320 | tf_op jit(solution)/shard_map/all_to_all | solution.py:149
  152.6 0.3 copy.9
  152.9 0.2 stack_reshape.7
  153.2 1.1 pad_maximum_fusion.1
  (8 shorter events, 0.0 us)
Async XLA Ops:
  0.0 1.5 copy-start
  1.6 11.0 %copy-start.1 = (bf16[2,512,512]{2,1,0:T(8,128)(2,1)S(1)}, bf16[2,512,512]{2,1,0:T(8,128)(2,1)}, u32[]{:S(2)}) copy-start(bf16[2,512,512]{2,1,0:T(8,128)(2,1)} %q_ref.3) | copy-start | bytes 3145732
  1.7 9.0 %copy-start.6 = (f32[3,2,2,512]{3,2,1,0:T(2,128)S(1)}, f32[3,2,2,512]{3,2,1,0:T(2,128)}, u32[]{:S(2)}) copy-start(f32[3,2,2,512]{3,2,1,0:T(2,128)} %rates_ref.3) | copy-start | bytes 73732
  1.8 12.0 %collective-permute-start = (bf16[2,512,256]{2,1,0:T(8,128)(2,1)S(1)}, bf16[2,512,256]{2,1,0:T(8,128)(2,1)S(1)}, u32[]{:S(2)}, u32[]{:S(2)}) collective-permute-start(bf16[2,512,256]{2,1,0:T(8,128)(2,1)S(1)} %pad_maximum_fusion.2), channel_id=1, source_target_pairs={{0,8},{8,0},{1,9},{9,1},{2,10},{10,2},{3,11},{11,3},{4,12},{12,4},... | collective-permute-start | bytes 1572872 | tf_op jit(solution)/shard_map/ppermute | solution.py:168
  10.7 3.1 %collective-permute-start.1 = (f32[3,2,512]{2,1,0:T(2,128)S(1)}, f32[3,2,512]{2,1,0:T(2,128)S(1)}, u32[]{:S(2)}, u32[]{:S(2)}) collective-permute-start(f32[3,2,512]{2,1,0:T(2,128)S(1)} %fusion.6), channel_id=1, source_target_pairs={{0,8},{8,0},{1,9},{9,1},{2,10},{10,2},{3,11},{11,3},{4,12},{12,4},... | collective-permute-start | bytes 36872 | tf_op jit(solution)/shard_map/ppermute | solution.py:171
  13.8 0.6 copy-start.7
  13.8 0.8 copy-start.5
  18.1 19.7 %all-to-all-start = ((bf16[32,24,256]{2,1,0:T(8,128)(2,1)}), bf16[32,24,256]{2,1,0:T(8,128)(2,1)S(1)}, u32[]{:S(2)}, u32[]{:S(2)}) async-start(bf16[32,24,256]{2,1,0:T(8,128)(2,1)} %bitcast.43), calls=%async_computation | async-start | bytes 786432 | tf_op jit(solution)/shard_map/all_to_all | solution.py:149
  25.9 21.8 %collective-permute-start.2 = (bf16[4,512,256]{2,1,0:T(8,128)(2,1)S(1)}, bf16[4,512,256]{2,1,0:T(8,128)(2,1)S(1)}, u32[]{:S(2)}, u32[]{:S(2)}) collective-permute-start(bf16[4,512,256]{2,1,0:T(8,128)(2,1)S(1)} %pad_maximum_fusion), channel_id=1, source_target_pairs={{0,8},{8,0},{1,9},{9,1},{2,10},{10,2},{3,11},{11,3},{4,12},{12,4},... | collective-permute-start | bytes 3145736 | tf_op jit(solution)/shard_map/ppermute | solution.py:174
  37.8 0.7 copy-start.2
  40.4 18.9 %all-to-all-start.1 = ((bf16[32,24,256]{2,1,0:T(8,128)(2,1)}), bf16[32,24,256]{2,1,0:T(8,128)(2,1)S(1)}, u32[]{:S(2)}, u32[]{:S(2)}) async-start(bf16[32,24,256]{2,1,0:T(8,128)(2,1)} %sum_parts.2), calls=%async_computation.1 | async-start | bytes 786432 | tf_op jit(solution)/shard_map/all_to_all | solution.py:149
  59.3 0.7 copy-start.4
  84.3 18.1 %all-to-all-start.4 = ((bf16[32,24,256]{2,1,0:T(8,128)(2,1)}), bf16[32,24,256]{2,1,0:T(8,128)(2,1)S(1)}, u32[]{:S(2)}, u32[]{:S(2)}) async-start(bf16[32,24,256]{2,1,0:T(8,128)(2,1)} %sum_parts.3), calls=%async_computation.4 | async-start | bytes 786432 | tf_op jit(solution)/shard_map/all_to_all | solution.py:149
  102.4 0.8 copy-start.3
  103.2 29.3 %all-to-all-start.2 = ((bf16[16,64,256]{2,1,0:T(8,128)(2,1)}), bf16[16,64,256]{2,1,0:T(8,128)(2,1)S(1)}, u32[]{:S(2)}, u32[]{:S(2)}) async-start(bf16[16,64,256]{2,1,0:T(8,128)(2,1)} %bitcast.39), calls=%async_computation.2 | async-start | bytes 1048576 | tf_op jit(solution)/shard_map/all_to_all | solution.py:149
  132.4 20.2 %all-to-all-start.5 = ((bf16[16,64,256]{2,1,0:T(8,128)(2,1)}), bf16[16,64,256]{2,1,0:T(8,128)(2,1)S(1)}, u32[]{:S(2)}, u32[]{:S(2)}) async-start(bf16[16,64,256]{2,1,0:T(8,128)(2,1)} %bitcast.42), calls=%async_computation.5 | async-start | bytes 1048576 | tf_op jit(solution)/shard_map/all_to_all | solution.py:149

commit v2 on v1

v2 whole, which is shorter than its diff:
```python
import jax
import jax.numpy as jnp
from jax import lax
from jax.experimental import pallas as pl
from jax.experimental.pallas import tpu as pltpu
from jax.sharding import Mesh, PartitionSpec as P


step_size = 0.05
eps_grad = 1e-05
eps_row = 1e-06
f32 = jnp.float32
bf16 = jnp.bfloat16
NT = (((1,), (1,)), ((), ()))
NN = (((1,), (0,)), ((), ()))
ROWS = 8


def dot(a, b, dims):
    return lax.dot_general(a, b, dims, preferred_element_type=f32)


def head_init(init_ref, kind):
    return [
        jnp.transpose(init_ref[0, 0].astype(f32)).astype(kind),
        jnp.transpose(init_ref[1, 0].astype(f32)).astype(kind),
        init_ref[2, 0].astype(kind),
    ]


def row_mean(w, i):
    return jnp.mean(w * w, axis=1 if i == 2 else 0, keepdims=True)


def gradients(keys, values, rate_gate, rate_up, rate_down, w_gate, w_up, w_down):
    gate = dot(w_gate, keys, NT)
    up = dot(w_up, keys, NT)
    err = dot(w_down, values, NT)
    sig = jax.nn.sigmoid(gate)
    silu = gate * sig
    hidden = (silu * up).astype(bf16)
    scaled = (hidden.astype(f32) * rate_down).astype(bf16)
    gate_grad = err * up * sig * (1.0 + gate * (1.0 - sig))
    gate_scaled = (gate_grad * rate_gate).astype(bf16)
    up_scaled = (err * silu * rate_up).astype(bf16)
    return (
        dot(gate_scaled, keys, NN),
        dot(up_scaled, keys, NN),
        dot(scaled, values, NN),
    )


def updated(state, init, grad_ref):
    result = []
    for i in range(3):
        grad = grad_ref[256 * i : 256 * (i + 1), :].astype(f32)
        rms = jnp.sqrt(jnp.mean(grad * grad, keepdims=True) + eps_grad)
        stepped = state[i] + grad * (step_size / rms)
        target = jnp.sqrt(row_mean(init[i], i))
        result.append(stepped * (target * lax.rsqrt(row_mean(stepped, i) + eps_row)))
    return result


def prepare_kernel(at, init_ref, out_ref):
    for i, w in enumerate(head_init(init_ref, f32)):
        out_ref[i] = w


def first_kernel(at, init_ref, k_ref, v_ref, rates_ref, out_ref):
    rates = [rates_ref[i, 0, pl.ds(at[0], 1), :] for i in (0, 1, 2)]
    grads = gradients(k_ref[0], v_ref[0], *rates, *head_init(init_ref, bf16))
    for i in range(3):
        out_ref[256 * i : 256 * (i + 1), :] = grads[i].astype(out_ref.dtype)


def second_kernel(at, init_ref, grad_ref, own_ref, other_ref, rates_ref, rates_other_ref, out_ref, state_ref, wb_ref):
    init = [init_ref[i] for i in range(3)]
    state = updated(init, init, grad_ref)
    weights = [w.astype(bf16) for w in state]
    for i in range(3):
        state_ref[i] = state[i]
        wb_ref[i] = weights[i]
    own = gradients(
        own_ref[0], own_ref[1], *[rates_ref[i, 1, pl.ds(at[0], 1), :] for i in (0, 1, 2)], *weights
    )
    other = gradients(
        other_ref[0], other_ref[1], *[rates_other_ref[i : i + 1, :] for i in (0, 1, 2)], *weights
    )
    for i in range(3):
        out_ref[256 * i : 256 * (i + 1), :] = (own[i] + other[i]).astype(bf16)


def applied(q, weights):
    gate = dot(q, weights[0], NT)
    up = dot(q, weights[1], NT)
    hidden = (gate * jax.nn.sigmoid(gate) * up).astype(bf16)
    return dot(hidden, weights[2], NN).astype(bf16)


def apply_first_kernel(at, own_ref, other_ref, q_ref, *refs):
    outs, scratch = refs[:-1], refs[-1]
    for weights_ref, head in ((own_ref, at[0]), (other_ref, 1 - at[0])):
        cols = pl.ds(pl.multiple_of(head * 256, 256), 256)
        weights = [weights_ref[i] for i in range(3)]
        scratch[:, :, cols] = applied(q_ref[0, :, cols], weights).reshape(ROWS, 64, 256)
    for d in range(ROWS):
        outs[d][...] = scratch[lax.rem(at[1] + d, ROWS)]


def gather_first_kernel(at, *refs):
    out_ref = refs[-1]
    for d in range(ROWS):
        source = lax.rem(at[1] + ROWS - d, ROWS)
        out_ref[0, :, pl.ds(pl.multiple_of(source * 512, 512), 512)] = refs[d][...]


def last_kernel(at, init_ref, state_ref, grad_ref, own_ref, other_ref, out_ref):
    state = updated([state_ref[i] for i in range(3)], [init_ref[i] for i in range(3)], grad_ref)
    weights = [w.astype(bf16) for w in state]
    for q, core in ((own_ref[2], at[0]), (other_ref[2], 1 - at[0])):
        out_ref[:, pl.ds(core, 1)] = applied(q, weights).reshape(ROWS, 1, 64, 256)


def gather_second_kernel(at, parts_ref, prev_ref, out_ref):
    for head in range(16):
        out_ref[0, :, 256 * head : 256 * (head + 1)] = parts_ref[head]


def whole(shape):
    return pl.BlockSpec(shape, lambda i, at: (0,) * len(shape))


VMEM = pl.BlockSpec(memory_space=pltpu.VMEM)
HEAD = pl.BlockSpec((3, 1, 256, 256), lambda i, at: (0, at[0], 0, 0))
TOKENS = pl.BlockSpec((1, 512, 256), lambda i, at: (0, 0, at[0]))
RATES = whole((3, 2, 2, 512))


def call(kernel, in_specs, outs, out_specs=None, scratch=(), aliases=None):
    specs = out_specs or [whole(shape) for shape, _ in outs]
    shapes = [jax.ShapeDtypeStruct(shape, dtype) for shape, dtype in outs]
    if len(outs) == 1:
        specs, shapes = specs[0], shapes[0]
    made = pl.pallas_call(
        kernel,
        grid_spec=pltpu.PrefetchScalarGridSpec(
            num_scalar_prefetch=1,
            grid=(1,),
            in_specs=in_specs,
            out_specs=specs,
            scratch_shapes=scratch,
        ),
        out_shape=shapes,
        input_output_aliases=aliases or {},
    )

    def run(at, *args):
        placed = [
            pltpu.with_memory_space_constraint(a, pltpu.VMEM) if s is VMEM else a
            for a, s in zip(args, in_specs)
        ]
        return made(at, *placed)

    return run


def exchange(array, axes):
    return lax.all_to_all(array, axes, split_axis=0, concat_axis=0, tiled=True)


def reduced(partial):
    parts = exchange(partial.reshape(32, 24, 256), ("x", "z"))
    total = jnp.sum(parts.astype(f32), axis=0, keepdims=True).astype(bf16)
    full = exchange(jnp.broadcast_to(total, (32, 24, 256)), ("x", "z"))
    return full.reshape(768, 256)


def swapped(array):
    return lax.ppermute(array, "c", [(0, 1), (1, 0)])


def program(query_tokens, key_tokens, value_tokens, token_rates, fast_init):
    core = lax.axis_index("c").astype(jnp.int32)
    row = lax.axis_index("y").astype(jnp.int32)
    at = jnp.stack([core, row])
    at_other = jnp.stack([1 - core, row])

    first_specs = [HEAD, TOKENS, TOKENS, RATES]
    first_args = (fast_init, key_tokens, value_tokens, token_rates)
    first_other = call(first_kernel, first_specs, [((768, 256), bf16)])(at_other, *first_args)
    first_got = swapped(first_other)
    first_own = call(first_kernel, first_specs, [((768, 256), f32)])(at, *first_args)
    first = (first_own + first_got.astype(f32)).astype(bf16)

    def half(which):
        return jnp.stack(
            [jnp.where(which == 0, a[1, :, :256], a[1, :, 256:]) for a in (key_tokens, value_tokens, query_tokens)]
        )

    other = swapped(half(1 - core))
    rates_other = swapped(jnp.where(core == 0, token_rates[:, 1, 1], token_rates[:, 1, 0]))
    own = half(core)
    init = call(prepare_kernel, [HEAD], [((3, 256, 256), f32)])(at, fast_init)

    summed = reduced(first)
    second, state, weights = call(
        second_kernel,
        [VMEM, VMEM, VMEM, VMEM, RATES, whole((3, 512))],
        [((768, 256), bf16), ((3, 256, 256), f32), ((3, 256, 256), bf16)],
    )(at, init, summed, own, other, token_rates, rates_other)

    weights_other = swapped(weights)
    pieces = call(
        apply_first_kernel,
        [whole((3, 256, 256)), whole((3, 256, 256)), pl.BlockSpec((1, 512, 512), lambda i, at: (0, 0, 0))],
        [((64, 512), bf16)] * ROWS,
        scratch=[pltpu.VMEM((ROWS, 64, 512), bf16)],
    )(at, weights, weights_other, query_tokens)
    got = [pieces[0]]
    for d in range(1, ROWS):
        got.append(lax.ppermute(pieces[d], "y", [(j, (j + d) % ROWS) for j in range(ROWS)]))

    summed = reduced(second)
    result = call(
        last_kernel, [VMEM, VMEM, VMEM, VMEM, VMEM], [((ROWS, 2, 64, 256), bf16)]
    )(at, init, state, summed, own, other)
    result = exchange(result.reshape(16, 64, 256), ("y", "c"))
    out = call(
        gather_first_kernel,
        [whole((64, 512))] * ROWS,
        [((2, 64, 4096), bf16)],
        [pl.BlockSpec((1, 64, 4096), lambda i, at: (0, 0, 0))],
    )(at, *got)
    return call(
        gather_second_kernel,
        [VMEM, pl.BlockSpec(memory_space=pl.ANY)],
        [((2, 64, 4096), bf16)],
        [pl.BlockSpec((1, 64, 4096), lambda i, at: (1, 0, 0))],
        aliases={2: 0},
    )(at, result, out)


def solution(mesh):
    fine = Mesh(mesh.devices.reshape(4, 8, 2, 8), ("x", "z", "c", "y"))
    seq = ("x", "z", "c")
    return jax.shard_map(
        program,
        mesh=fine,
        in_specs=(
            P(None, seq, "y"),
            P(None, seq, "y"),
            P(None, seq, "y"),
            P(None, None, "y", seq),
            P(None, "y", None, None),
        ),
        out_specs=P(None, (*seq, "y"), None),
        check_vma=False,
    )
```

time: 155 us -> 161 us (1.039); the launches traced: 154 us -> 159 us
  waiting for transfers between devices: 58.2 us -> 17.7 us
  starting transfers between devices: 51.2 us -> 71.4 us
  blocking collectives: 18.4 us -> 36.4 us
  Pallas kernels: 17.3 us -> 23.9 us
  local copies, waits for them, and re-layouts: 7.48 us -> 3.34 us
  other arithmetic: 1.43 us -> 5.42 us
    all_to_all x5 -> x3, waiting for transfers between devices: 57.2 us -> 13.9 us  [exchange(): return lax.all_to_all(array, axes, split_axis=0, concat_axis=0, tiled=True)]
    ppermute x3 -> x11, starting transfers between devices: 13.2 us -> 44 us  [the longest x7 28.1 us: program(): lax.ppermute(pieces[d], 'y', [(j, (j + d) % ROWS) for j in range(ROWS)])]
    all_to_all x1 -> x2, blocking collectives: 18.4 us -> 36.4 us  [exchange(): return lax.all_to_all(array, axes, split_axis=0, concat_axis=0, tiled=True)]
    all_to_all x5 -> x3, starting transfers between devices: 38 us -> 27.4 us  [exchange(): return lax.all_to_all(array, axes, split_axis=0, concat_axis=0, tiled=True)]
    pallas_call x6 -> x8, Pallas kernels: 17.3 us -> 23.9 us  [run(): return made(at, *placed)]
    ppermute x3 -> x11, waiting for transfers between devices: 1.06 us -> 3.8 us  [the longest x7 2.2 us: program(): lax.ppermute(pieces[d], 'y', [(j, (j + d) % ROWS) for j in range(ROWS)])]
    squeeze x4 -> x0, local copies, waits for them, and re-layouts: 2.33 us -> none  [the longest x1 1.36 us: body(): key_tokens[1]]
    convert_element_type x0 -> x1, other arithmetic: none -> 2.11 us  [program(): first = (first_own + first_got.astype(f32)).astype(bf16)]
  transfers between devices with their start and end apart: 8 -> 14, of which waited for: 6 -> 5; matrix products, arithmetic and copies ran while one was open for 2% -> 2% of each run, Pallas kernels for 5% -> 8%
where the time goes in v2:
time: 161 us; the launch traced here: 159 us
  starting transfers between devices  71.4 us (44%)
  blocking collectives  36.4 us (23%)
  Pallas kernels  23.9 us (15%)
  waiting for transfers between devices  17.7 us (11%)
  other arithmetic  5.42 us (3%)
  local copies, waits for them, and re-layouts  3.34 us (2%)
    all_to_all x2, blocking collectives, exchange(): return lax.all_to_all(array, axes, split_axis=0, concat_axis=0, tiled=True)  36.4 us
    ppermute x7, starting transfers between devices, program(): lax.ppermute(pieces[d], 'y', [(j, (j + d) % ROWS) for j in range(ROWS)])  28.1 us
    all_to_all x3, starting transfers between devices, exchange(): return lax.all_to_all(array, axes, split_axis=0, concat_axis=0, tiled=True)  27.4 us
    pallas_call x8, Pallas kernels, run(): return made(at, *placed)  23.9 us
    ppermute x4, starting transfers between devices, swapped(): return lax.ppermute(array, 'c', [(0, 1), (1, 0)])  15.9 us
    all_to_all x3, waiting for transfers between devices, exchange(): return lax.all_to_all(array, axes, split_axis=0, concat_axis=0, tiled=True)  13.9 us
  transfers between devices with their start and end apart: 14, of which 5 were waited for; matrix products, arithmetic and copies ran while one was open for 2% of the time, Pallas kernels for 8%

profile of v2, /device:TPU:1, one launch (start us, length us, event | category | flops | bytes accessed | tf_op | source)
XLA Modules:
  0.0 158.5 jit_solution(9318687209763483222)
XLA Ops:
  0.0 0.7 pad_add_fusion.1.at
  0.7 3.4 %shard_map.57 = bf16[768,256]{1,0:T(8,128)(2,1)} custom-call(s32[2]{0:T(128)} %pad_add_fusion.1.at, bf16[3,2,256,256]{3,2,1,0:T(8,128)(2,1)} %init_ref.5, bf16[2,512,512]{2,1,0:T(8,128)(2,1)} %k_ref.3, bf16[2,512,512]{2,1,0:T(8,128)(2,1)} %v_ref.3, f32[3,2,2,512]{3,2,1,0:T(2,128)} %rates_ref.5), custom_call_target="tpu_custom_call" | custom-call | tf_op jit(solution)/shard_map/pallas_call | solution.py:162
  4.1 8.7 %collective-permute-start = (bf16[768,256]{1,0:T(8,128)(2,1)}, bf16[768,256]{1,0:T(8,128)(2,1)S(1)}, u32[]{:S(2)}, u32[]{:S(2)}) collective-permute-start(bf16[768,256]{1,0:T(8,128)(2,1)} %shard_map.57), channel_id=1, source_target_pairs={{0,8},{8,0},{1,9},{9,1},{2,10},{10,2},{3,11},{11,3},{4,12},{12,4},... | collective-permute-start | bytes 1179656 | tf_op jit(solution)/shard_map/ppermute | solution.py:179
  12.8 0.6 pad_add_fusion.at
  13.4 3.6 %shard_map.56 = f32[768,256]{1,0:T(8,128)} custom-call(s32[2]{0:T(128)} %pad_add_fusion.at, bf16[3,2,256,256]{3,2,1,0:T(8,128)(2,1)} %init_ref.5, bf16[2,512,512]{2,1,0:T(8,128)(2,1)} %k_ref.3, bf16[2,512,512]{2,1,0:T(8,128)(2,1)} %v_ref.3, f32[3,2,2,512]{3,2,1,0:T(2,128)} %rates_ref.5), custom_call_target="tpu_custom_call" | custom-call | tf_op jit(solution)/shard_map/pallas_call | solution.py:162
  17.0 0.0 collective-permute-done
  17.0 2.1 %add_convert_fusion = bf16[768,256]{1,0:T(8,128)(2,1)} fusion(f32[768,256]{1,0:T(8,128)} %shard_map.56, bf16[768,256]{1,0:T(8,128)(2,1)S(1)} %collective-permute-done), kind=kLoop, calls=%fused_computation.2 | loop fusion | flops 589824 | bytes 1572864 | tf_op jit(solution)/shard_map/convert_element_type | solution.py:193
  19.1 7.7 %all-to-all-start = ((bf16[32,24,256]{2,1,0:T(8,128)(2,1)}), bf16[32,24,256]{2,1,0:T(8,128)(2,1)S(1)}, u32[]{:S(2)}, u32[]{:S(2)}) async-start(bf16[32,24,256]{2,1,0:T(8,128)(2,1)} %bitcast.13), calls=%async_computation | async-start | bytes 786432 | tf_op jit(solution)/shard_map/all_to_all | solution.py:168
  26.8 0.7 broadcast_select_fusion
  27.5 0.1 broadcast_select_fusion.1
  27.6 1.0 pad_maximum_fusion.1
  28.6 2.2 %collective-permute-start.1 = (bf16[3,512,256]{2,1,0:T(8,128)(2,1)}, bf16[3,512,256]{2,1,0:T(8,128)(2,1)S(1)}, u32[]{:S(2)}, u32[]{:S(2)}) collective-permute-start(bf16[3,512,256]{2,1,0:T(8,128)(2,1)} %pad_maximum_fusion.1), channel_id=1, source_target_pairs={{0,8},{8,0},{1,9},{9,1},{2,10},{10,2},{3,11},{11,3},{4,12},{12,4},... | collective-permute-start | bytes 2359304 | tf_op jit(solution)/shard_map/ppermute | solution.py:179
  30.8 8.1 %all-to-all-done = bf16[32,24,256]{2,1,0:T(8,128)(2,1)S(1)} async-done(((bf16[32,24,256]{2,1,0:T(8,128)(2,1)}), bf16[32,24,256]{2,1,0:T(8,128)(2,1)S(1)}, u32[]{:S(2)}, u32[]{:S(2)}) %all-to-all-start) | async-done | bytes 393248 | tf_op jit(solution)/shard_map/all_to_all | solution.py:168
  39.0 0.1 reduce_sum.24
  39.0 0.8 broadcast_in_dim.4
  39.8 7.5 %all-to-all-start.1 = ((bf16[32,24,256]{2,1,0:T(8,128)(2,1)}), bf16[32,24,256]{2,1,0:T(8,128)(2,1)S(1)}, u32[]{:S(2)}, u32[]{:S(2)}) async-start(bf16[32,24,256]{2,1,0:T(8,128)(2,1)} %broadcast_in_dim.4), calls=%async_computation.1 | async-start | bytes 786432 | tf_op jit(solution)/shard_map/all_to_all | solution.py:168
  47.4 3.0 %collective-permute-start.2 = (f32[3,512]{1,0:T(4,128)S(1)}, f32[3,512]{1,0:T(4,128)S(1)}, u32[]{:S(2)}, u32[]{:S(2)}) collective-permute-start(f32[3,512]{1,0:T(4,128)S(1)} %fusion), channel_id=1, source_target_pairs={{0,8},{8,0},{1,9},{9,1},{2,10},{10,2},{3,11},{11,3},{4,12},{12,4},... | collective-permute-start | bytes 18440 | tf_op jit(solution)/shard_map/ppermute | solution.py:179
  50.3 0.1 pad_maximum_fusion.own_ref
  50.5 2.7 %shard_map.55.init_ref = f32[3,256,256]{2,1,0:T(8,128)} custom-call(s32[2]{0:T(128)} %pad_add_fusion.at, bf16[3,2,256,256]{3,2,1,0:T(8,128)(2,1)} %init_ref.5), custom_call_target="tpu_custom_call" | custom-call | tf_op jit(solution)/shard_map/pallas_call | solution.py:162
  53.1 0.0 collective-permute-done.2.rates_other_ref
  53.1 0.0 collective-permute-done.1.other_ref
  53.2 5.8 %all-to-all-done.1 = bf16[32,24,256]{2,1,0:T(8,128)(2,1)S(1)} async-done(((bf16[32,24,256]{2,1,0:T(8,128)(2,1)}), bf16[32,24,256]{2,1,0:T(8,128)(2,1)S(1)}, u32[]{:S(2)}, u32[]{:S(2)}) %all-to-all-start.1) | async-done | bytes 393248 | tf_op jit(solution)/shard_map/all_to_all | solution.py:168
  58.9 1.1 copy-done.2
  60.1 4.1 %shard_map.58 = (bf16[768,256]{1,0:T(8,128)(2,1)}, f32[3,256,256]{2,1,0:T(8,128)}, bf16[3,256,256]{2,1,0:T(8,128)(2,1)}) custom-call(s32[2]{0:T(128)} %pad_add_fusion.at, f32[3,256,256]{2,1,0:T(8,128)S(1)} %copy-done.2, bf16[768,256]{1,0:T(8,128)(2,1)S(1)} %bitcast.10, bf16[3,512,256]{2,1,0:T(8,128)(2,1)S(1)} %pad_maximum_fusion.own_ref, ...), custom_call_target="tpu_custom_call" | custom-call | tf_op jit(solution)/shard_map/pallas_call | solution.py:162
  64.1 18.4 %all_to_all.25 = bf16[32,24,256]{2,1,0:T(8,128)(2,1)S(1)} all-to-all(bf16[32,24,256]{2,1,0:T(8,128)(2,1)} %bitcast.14), channel_id=1, replica_groups=mesh['x'=4,'z'=8,'c'=2,'y'=8] {'x','z'}, dimensions={0} | all-to-all | bytes 786432 | tf_op jit(solution)/shard_map/all_to_all | solution.py:168
  82.6 0.1 reduce_sum.25
  82.7 18.0 %all_to_all.26 = bf16[32,24,256]{2,1,0:T(8,128)(2,1)S(1)} all-to-all(bf16[32,24,256]{2,1,0:T(8,128)(2,1)S(1)} %broadcast_in_dim.5), channel_id=1, replica_groups=mesh['x'=4,'z'=8,'c'=2,'y'=8] {'x','z'}, dimensions={0} | all-to-all | bytes 786432 | tf_op jit(solution)/shard_map/all_to_all | solution.py:168
  100.7 2.6 %shard_map.59 = bf16[8,2,64,256]{3,2,1,0:T(8,128)(2,1)} custom-call(s32[2]{0:T(128)} %pad_add_fusion.at, f32[3,256,256]{2,1,0:T(8,128)S(1)} %copy-done.2, f32[3,256,256]{2,1,0:T(8,128)S(1)} %copy-done.5, bf16[768,256]{1,0:T(8,128)(2,1)S(1)} %bitcast.11, bf16[3,512,256]{2,1,0:T(8,128)(2,1)S(1)} %copy-done.1, bf16[3,512,256]{2,1,0:T(8,128)(2,1)S(1)} %copy-done.4), custom_call_target="tpu_custom_call" | custom-call | tf_op jit(solution)/shard_map/pallas_call | solution.py:162
  103.3 12.2 %all-to-all-start.4 = ((bf16[16,64,256]{2,1,0:T(8,128)(2,1)}), bf16[16,64,256]{2,1,0:T(8,128)(2,1)S(1)}, u32[]{:S(2)}, u32[]{:S(2)}) async-start(bf16[16,64,256]{2,1,0:T(8,128)(2,1)} %bitcast.12), calls=%async_computation.4 | async-start | bytes 1048576 | tf_op jit(solution)/shard_map/all_to_all | solution.py:168
  115.5 2.0 %collective-permute-start.3 = (bf16[3,256,256]{2,1,0:T(8,128)(2,1)S(1)}, bf16[3,256,256]{2,1,0:T(8,128)(2,1)S(1)}, u32[]{:S(2)}, u32[]{:S(2)}) collective-permute-start(bf16[3,256,256]{2,1,0:T(8,128)(2,1)S(1)} %copy-done.10), channel_id=1, source_target_pairs={{0,8},{8,0},{1,9},{9,1},{2,10},{10,2},{3,11},{11,3},{4,12},{12,4},... | collective-permute-start | bytes 1179656 | tf_op jit(solution)/shard_map/ppermute | solution.py:179
  117.5 1.6 %collective-permute-done.3.other_ref = bf16[3,256,256]{2,1,0:T(8,128)(2,1)S(1)} collective-permute-done((bf16[3,256,256]{2,1,0:T(8,128)(2,1)S(1)}, bf16[3,256,256]{2,1,0:T(8,128)(2,1)S(1)}, u32[]{:S(2)}, u32[]{:S(2)}) %collective-permute-start.3) | collective-permute-done | bytes 393248 | tf_op jit(solution)/shard_map/ppermute | solution.py:179
  119.1 0.7 copy-done.11
  119.9 3.5 %shard_map.60 = (bf16[64,512]{1,0:T(8,128)(2,1)}, bf16[64,512]{1,0:T(8,128)(2,1)}, bf16[64,512]{1,0:T(8,128)(2,1)}, bf16[64,512]{1,0:T(8,128)(2,1)}, bf16[64,512...) custom-call(s32[2]{0:T(128)} %pad_add_fusion.at, ...), custom_call_target="tpu_custom_call" | custom-call | tf_op jit(solution)/shard_map/pallas_call | solution.py:162
  123.4 3.3 %collective-permute-start.4 = (bf16[64,512]{1,0:T(8,128)(2,1)}, bf16[64,512]{1,0:T(8,128)(2,1)S(1)}, u32[]{:S(2)}, u32[]{:S(2)}) collective-permute-start(bf16[64,512]{1,0:T(8,128)(2,1)} %get-tuple-element.20), channel_id=1, source_target_pairs={{0,1},{1,2},{2,3},{3,4},{4,5},{5,6},{6,7},{7,0},{8,9},{9,10},{10,1... | collective-permute-start | bytes 196616 | tf_op jit(solution)/shard_map/ppermute | solution.py:221
  126.6 4.0 %collective-permute-start.5 = (bf16[64,512]{1,0:T(8,128)(2,1)}, bf16[64,512]{1,0:T(8,128)(2,1)S(1)}, u32[]{:S(2)}, u32[]{:S(2)}) collective-permute-start(bf16[64,512]{1,0:T(8,128)(2,1)} %get-tuple-element.21), channel_id=1, source_target_pairs={{0,2},{1,3},{2,4},{3,5},{4,6},{5,7},{6,0},{7,1},{8,10},{9,11},{10,... | collective-permute-start | bytes 196616 | tf_op jit(solution)/shard_map/ppermute | solution.py:221
  130.6 4.3 %collective-permute-start.6 = (bf16[64,512]{1,0:T(8,128)(2,1)}, bf16[64,512]{1,0:T(8,128)(2,1)S(1)}, u32[]{:S(2)}, u32[]{:S(2)}) collective-permute-start(bf16[64,512]{1,0:T(8,128)(2,1)} %get-tuple-element.22), channel_id=1, source_target_pairs={{0,3},{1,4},{2,5},{3,6},{4,7},{5,0},{6,1},{7,2},{8,11},{9,12},{10,... | collective-permute-start | bytes 196616 | tf_op jit(solution)/shard_map/ppermute | solution.py:221
  134.9 4.0 %collective-permute-start.7 = (bf16[64,512]{1,0:T(8,128)(2,1)}, bf16[64,512]{1,0:T(8,128)(2,1)S(1)}, u32[]{:S(2)}, u32[]{:S(2)}) collective-permute-start(bf16[64,512]{1,0:T(8,128)(2,1)} %get-tuple-element.23), channel_id=1, source_target_pairs={{0,4},{1,5},{2,6},{3,7},{4,0},{5,1},{6,2},{7,3},{8,12},{9,13},{10,... | collective-permute-start | bytes 196616 | tf_op jit(solution)/shard_map/ppermute | solution.py:221
  138.9 4.3 %collective-permute-start.8 = (bf16[64,512]{1,0:T(8,128)(2,1)}, bf16[64,512]{1,0:T(8,128)(2,1)S(1)}, u32[]{:S(2)}, u32[]{:S(2)}) collective-permute-start(bf16[64,512]{1,0:T(8,128)(2,1)} %get-tuple-element.24), channel_id=1, source_target_pairs={{0,5},{1,6},{2,7},{3,0},{4,1},{5,2},{6,3},{7,4},{8,13},{9,14},{10,... | collective-permute-start | bytes 196616 | tf_op jit(solution)/shard_map/ppermute | solution.py:221
  143.3 5.2 %collective-permute-start.9 = (bf16[64,512]{1,0:T(8,128)(2,1)}, bf16[64,512]{1,0:T(8,128)(2,1)S(1)}, u32[]{:S(2)}, u32[]{:S(2)}) collective-permute-start(bf16[64,512]{1,0:T(8,128)(2,1)} %get-tuple-element.25), channel_id=1, source_target_pairs={{0,6},{1,7},{2,0},{3,1},{4,2},{5,3},{6,4},{7,5},{8,14},{9,15},{10,... | collective-permute-start | bytes 196616 | tf_op jit(solution)/shard_map/ppermute | solution.py:221
  148.5 3.1 %collective-permute-start.10 = (bf16[64,512]{1,0:T(8,128)(2,1)}, bf16[64,512]{1,0:T(8,128)(2,1)S(1)}, u32[]{:S(2)}, u32[]{:S(2)}) collective-permute-start(bf16[64,512]{1,0:T(8,128)(2,1)} %get-tuple-element.26), channel_id=1, source_target_pairs={{0,7},{1,0},{2,1},{3,2},{4,3},{5,4},{6,5},{7,6},{8,15},{9,8},{10,9... | collective-permute-start | bytes 196616 | tf_op jit(solution)/shard_map/ppermute | solution.py:221
  151.6 0.0 collective-permute-done.8.refs_5_
  151.7 1.7 %collective-permute-done.9.refs_6_ = bf16[64,512]{1,0:T(8,128)(2,1)S(1)} collective-permute-done((bf16[64,512]{1,0:T(8,128)(2,1)}, bf16[64,512]{1,0:T(8,128)(2,1)S(1)}, u32[]{:S(2)}, u32[]{:S(2)}) %collective-permute-start.9) | collective-permute-done | bytes 65568 | tf_op jit(solution)/shard_map/ppermute | solution.py:221
  153.4 0.5 collective-permute-done.10.refs_7_
  153.9 0.1 copy-done.18
  154.0 0.5 copy-done.19
  154.5 2.6 %shard_map.61.prev_ref = bf16[2,64,4096]{2,1,0:T(8,128)(2,1)} custom-call(s32[2]{0:T(128)} %pad_add_fusion.at, bf16[64,512]{1,0:T(8,128)(2,1)} %get-tuple-element.19.refs_0_, bf16[64,512]{1,0:T(8,128)(2,1)} %copy-done.13, bf16[64,512]{1,0:T(8,128)(2,1)} %copy-done.14, bf16[64,512]{1,0:T(8,128)(2,1)} %copy-done.15, bf16[64,512]{1,0:T(8,128)(2,1)} %copy-done.16, ...), custom_call_target="tpu_custom_call" | custom-call | tf_op jit(solution)/shard_map/pallas_call | solution.py:162
  157.0 0.0 all-to-all-done.4.parts_ref
  157.0 1.5 shard_map.62
  (45 shorter events, 0.1 us)
Async XLA Ops:
  4.1 12.9 %collective-permute-start = (bf16[768,256]{1,0:T(8,128)(2,1)}, bf16[768,256]{1,0:T(8,128)(2,1)S(1)}, u32[]{:S(2)}, u32[]{:S(2)}) collective-permute-start(bf16[768,256]{1,0:T(8,128)(2,1)} %shard_map.57), channel_id=1, source_target_pairs={{0,8},{8,0},{1,9},{9,1},{2,10},{10,2},{3,11},{11,3},{4,12},{12,4},... | collective-permute-start | bytes 1179656 | tf_op jit(solution)/shard_map/ppermute | solution.py:179
  17.0 9.8 %copy-start.8 = (bf16[2,512,512]{2,1,0:T(8,128)(2,1)S(1)}, bf16[2,512,512]{2,1,0:T(8,128)(2,1)}, u32[]{:S(2)}) copy-start(bf16[2,512,512]{2,1,0:T(8,128)(2,1)} %q_ref.1) | copy-start | bytes 3145732
  17.0 10.6 %copy-start.7 = (bf16[2,512,512]{2,1,0:T(8,128)(2,1)S(1)}, bf16[2,512,512]{2,1,0:T(8,128)(2,1)}, u32[]{:S(2)}) copy-start(bf16[2,512,512]{2,1,0:T(8,128)(2,1)} %v_ref.3) | copy-start | bytes 3145732
  19.1 8.4 %copy-start.6 = (bf16[2,512,512]{2,1,0:T(8,128)(2,1)S(1)}, bf16[2,512,512]{2,1,0:T(8,128)(2,1)}, u32[]{:S(2)}) copy-start(bf16[2,512,512]{2,1,0:T(8,128)(2,1)} %k_ref.3) | copy-start | bytes 3145732
  19.1 19.9 %all-to-all-start = ((bf16[32,24,256]{2,1,0:T(8,128)(2,1)}), bf16[32,24,256]{2,1,0:T(8,128)(2,1)S(1)}, u32[]{:S(2)}, u32[]{:S(2)}) async-start(bf16[32,24,256]{2,1,0:T(8,128)(2,1)} %bitcast.13), calls=%async_computation | async-start | bytes 786432 | tf_op jit(solution)/shard_map/all_to_all | solution.py:168
  28.6 24.5 %collective-permute-start.1 = (bf16[3,512,256]{2,1,0:T(8,128)(2,1)}, bf16[3,512,256]{2,1,0:T(8,128)(2,1)S(1)}, u32[]{:S(2)}, u32[]{:S(2)}) collective-permute-start(bf16[3,512,256]{2,1,0:T(8,128)(2,1)} %pad_maximum_fusion.1), channel_id=1, source_target_pairs={{0,8},{8,0},{1,9},{9,1},{2,10},{10,2},{3,11},{11,3},{4,12},{12,4},... | collective-permute-start | bytes 2359304 | tf_op jit(solution)/shard_map/ppermute | solution.py:179
  39.8 7.5 %copy-start.12 = (f32[3,2,2,512]{3,2,1,0:T(2,128)S(1)}, f32[3,2,2,512]{3,2,1,0:T(2,128)}, u32[]{:S(2)}) copy-start(f32[3,2,2,512]{3,2,1,0:T(2,128)} %rates_ref.5) | copy-start | bytes 73732
  39.8 10.5 %copy-start.9 = (bf16[1,512,256]{2,1,0:T(8,128)(2,1)S(1)}, bf16[1,512,256]{2,1,0:T(8,128)(2,1)}, u32[]{:S(2)}) copy-start(bf16[1,512,256]{2,1,0:T(8,128)(2,1)} %get-tuple-element.32) | copy-start | bytes 786436
  39.8 19.1 %all-to-all-start.1 = ((bf16[32,24,256]{2,1,0:T(8,128)(2,1)}), bf16[32,24,256]{2,1,0:T(8,128)(2,1)S(1)}, u32[]{:S(2)}, u32[]{:S(2)}) async-start(bf16[32,24,256]{2,1,0:T(8,128)(2,1)} %broadcast_in_dim.4), calls=%async_computation.1 | async-start | bytes 786432 | tf_op jit(solution)/shard_map/all_to_all | solution.py:168
  47.4 5.8 %collective-permute-start.2 = (f32[3,512]{1,0:T(4,128)S(1)}, f32[3,512]{1,0:T(4,128)S(1)}, u32[]{:S(2)}, u32[]{:S(2)}) collective-permute-start(f32[3,512]{1,0:T(4,128)S(1)} %fusion), channel_id=1, source_target_pairs={{0,8},{8,0},{1,9},{9,1},{2,10},{10,2},{3,11},{11,3},{4,12},{12,4},... | collective-permute-start | bytes 18440 | tf_op jit(solution)/shard_map/ppermute | solution.py:179
  50.4 8.5 %copy-start = (bf16[3,512,256]{2,1,0:T(8,128)(2,1)}, bf16[3,512,256]{2,1,0:T(8,128)(2,1)S(1)}, u32[]{:S(2)}) copy-start(bf16[3,512,256]{2,1,0:T(8,128)(2,1)S(1)} %pad_maximum_fusion.own_ref) | copy-start | bytes 2359300
  53.1 5.8 %copy-start.20 = (f32[3,512]{1,0:T(4,128)}, f32[3,512]{1,0:T(4,128)S(1)}, u32[]{:S(2)}) copy-start(f32[3,512]{1,0:T(4,128)S(1)} %collective-permute-done.2.rates_other_ref) | copy-start | bytes 18436
  53.1 11.0 %copy-start.3 = (bf16[3,512,256]{2,1,0:T(8,128)(2,1)}, bf16[3,512,256]{2,1,0:T(8,128)(2,1)S(1)}, u32[]{:S(2)}) copy-start(bf16[3,512,256]{2,1,0:T(8,128)(2,1)S(1)} %collective-permute-done.1.other_ref) | copy-start | bytes 2359300
  58.9 1.1 copy-start.2
  64.1 36.6 %copy-start.5 = (f32[3,256,256]{2,1,0:T(8,128)S(1)}, f32[3,256,256]{2,1,0:T(8,128)}, u32[]{:S(2)}) copy-start(f32[3,256,256]{2,1,0:T(8,128)} %get-tuple-element.16.state_ref) | copy-start | bytes 2359300
  82.6 18.1 %copy-start.1 = (bf16[3,512,256]{2,1,0:T(8,128)(2,1)S(1)}, bf16[3,512,256]{2,1,0:T(8,128)(2,1)}, u32[]{:S(2)}) copy-start(bf16[3,512,256]{2,1,0:T(8,128)(2,1)} %copy-done) | copy-start | bytes 2359300
  82.6 18.1 %copy-start.4 = (bf16[3,512,256]{2,1,0:T(8,128)(2,1)S(1)}, bf16[3,512,256]{2,1,0:T(8,128)(2,1)}, u32[]{:S(2)}) copy-start(bf16[3,512,256]{2,1,0:T(8,128)(2,1)} %copy-done.3) | copy-start | bytes 2359300
  103.3 12.2 %copy-start.10 = (bf16[3,256,256]{2,1,0:T(8,128)(2,1)S(1)}, bf16[3,256,256]{2,1,0:T(8,128)(2,1)}, u32[]{:S(2)}) copy-start(bf16[3,256,256]{2,1,0:T(8,128)(2,1)} %get-tuple-element.18.own_ref) | copy-start | bytes 1179652
  103.3 53.7 %all-to-all-start.4 = ((bf16[16,64,256]{2,1,0:T(8,128)(2,1)}), bf16[16,64,256]{2,1,0:T(8,128)(2,1)S(1)}, u32[]{:S(2)}, u32[]{:S(2)}) async-start(bf16[16,64,256]{2,1,0:T(8,128)(2,1)} %bitcast.12), calls=%async_computation.4 | async-start | bytes 1048576 | tf_op jit(solution)/shard_map/all_to_all | solution.py:168
  115.5 3.6 %collective-permute-start.3 = (bf16[3,256,256]{2,1,0:T(8,128)(2,1)S(1)}, bf16[3,256,256]{2,1,0:T(8,128)(2,1)S(1)}, u32[]{:S(2)}, u32[]{:S(2)}) collective-permute-start(bf16[3,256,256]{2,1,0:T(8,128)(2,1)S(1)} %copy-done.10), channel_id=1, source_target_pairs={{0,8},{8,0},{1,9},{9,1},{2,10},{10,2},{3,11},{11,3},{4,12},{12,4},... | collective-permute-start | bytes 1179656 | tf_op jit(solution)/shard_map/ppermute | solution.py:179
  119.1 0.7 copy-start.11
  123.4 19.9 %collective-permute-start.4 = (bf16[64,512]{1,0:T(8,128)(2,1)}, bf16[64,512]{1,0:T(8,128)(2,1)S(1)}, u32[]{:S(2)}, u32[]{:S(2)}) collective-permute-start(bf16[64,512]{1,0:T(8,128)(2,1)} %get-tuple-element.20), channel_id=1, source_target_pairs={{0,1},{1,2},{2,3},{3,4},{4,5},{5,6},{6,7},{7,0},{8,9},{9,10},{10,1... | collective-permute-start | bytes 196616 | tf_op jit(solution)/shard_map/ppermute | solution.py:221
  126.6 21.8 %collective-permute-start.5 = (bf16[64,512]{1,0:T(8,128)(2,1)}, bf16[64,512]{1,0:T(8,128)(2,1)S(1)}, u32[]{:S(2)}, u32[]{:S(2)}) collective-permute-start(bf16[64,512]{1,0:T(8,128)(2,1)} %get-tuple-element.21), channel_id=1, source_target_pairs={{0,2},{1,3},{2,4},{3,5},{4,6},{5,7},{6,0},{7,1},{8,10},{9,11},{10,... | collective-permute-start | bytes 196616 | tf_op jit(solution)/shard_map/ppermute | solution.py:221
  130.6 21.0 %collective-permute-start.6 = (bf16[64,512]{1,0:T(8,128)(2,1)}, bf16[64,512]{1,0:T(8,128)(2,1)S(1)}, u32[]{:S(2)}, u32[]{:S(2)}) collective-permute-start(bf16[64,512]{1,0:T(8,128)(2,1)} %get-tuple-element.22), channel_id=1, source_target_pairs={{0,3},{1,4},{2,5},{3,6},{4,7},{5,0},{6,1},{7,2},{8,11},{9,12},{10,... | collective-permute-start | bytes 196616 | tf_op jit(solution)/shard_map/ppermute | solution.py:221
  134.9 16.7 %collective-permute-start.7 = (bf16[64,512]{1,0:T(8,128)(2,1)}, bf16[64,512]{1,0:T(8,128)(2,1)S(1)}, u32[]{:S(2)}, u32[]{:S(2)}) collective-permute-start(bf16[64,512]{1,0:T(8,128)(2,1)} %get-tuple-element.23), channel_id=1, source_target_pairs={{0,4},{1,5},{2,6},{3,7},{4,0},{5,1},{6,2},{7,3},{8,12},{9,13},{10,... | collective-permute-start | bytes 196616 | tf_op jit(solution)/shard_map/ppermute | solution.py:221
  138.9 12.7 %collective-permute-start.8 = (bf16[64,512]{1,0:T(8,128)(2,1)}, bf16[64,512]{1,0:T(8,128)(2,1)S(1)}, u32[]{:S(2)}, u32[]{:S(2)}) collective-permute-start(bf16[64,512]{1,0:T(8,128)(2,1)} %get-tuple-element.24), channel_id=1, source_target_pairs={{0,5},{1,6},{2,7},{3,0},{4,1},{5,2},{6,3},{7,4},{8,13},{9,14},{10,... | collective-permute-start | bytes 196616 | tf_op jit(solution)/shard_map/ppermute | solution.py:221
  143.3 10.6 %copy-start.13 = (bf16[64,512]{1,0:T(8,128)(2,1)}, bf16[64,512]{1,0:T(8,128)(2,1)S(1)}, u32[]{:S(2)}) copy-start(bf16[64,512]{1,0:T(8,128)(2,1)S(1)} %collective-permute-done.4.refs_1_) | copy-start | bytes 196612
  143.3 10.1 %collective-permute-start.9 = (bf16[64,512]{1,0:T(8,128)(2,1)}, bf16[64,512]{1,0:T(8,128)(2,1)S(1)}, u32[]{:S(2)}, u32[]{:S(2)}) collective-permute-start(bf16[64,512]{1,0:T(8,128)(2,1)} %get-tuple-element.25), channel_id=1, source_target_pairs={{0,6},{1,7},{2,0},{3,1},{4,2},{5,3},{6,4},{7,5},{8,14},{9,15},{10,... | collective-permute-start | bytes 196616 | tf_op jit(solution)/shard_map/ppermute | solution.py:221
  148.5 5.4 %copy-start.14 = (bf16[64,512]{1,0:T(8,128)(2,1)}, bf16[64,512]{1,0:T(8,128)(2,1)S(1)}, u32[]{:S(2)}) copy-start(bf16[64,512]{1,0:T(8,128)(2,1)S(1)} %collective-permute-done.5.refs_2_) | copy-start | bytes 196612
  148.5 5.3 %collective-permute-start.10 = (bf16[64,512]{1,0:T(8,128)(2,1)}, bf16[64,512]{1,0:T(8,128)(2,1)S(1)}, u32[]{:S(2)}, u32[]{:S(2)}) collective-permute-start(bf16[64,512]{1,0:T(8,128)(2,1)} %get-tuple-element.26), channel_id=1, source_target_pairs={{0,7},{1,0},{2,1},{3,2},{4,3},{5,4},{6,5},{7,6},{8,15},{9,8},{10,9... | collective-permute-start | bytes 196616 | tf_op jit(solution)/shard_map/ppermute | solution.py:221
  151.6 2.3 %copy-start.15 = (bf16[64,512]{1,0:T(8,128)(2,1)}, bf16[64,512]{1,0:T(8,128)(2,1)S(1)}, u32[]{:S(2)}) copy-start(bf16[64,512]{1,0:T(8,128)(2,1)S(1)} %collective-permute-done.6.refs_3_) | copy-start | bytes 196612
  151.6 2.2 %copy-start.16 = (bf16[64,512]{1,0:T(8,128)(2,1)}, bf16[64,512]{1,0:T(8,128)(2,1)S(1)}, u32[]{:S(2)}) copy-start(bf16[64,512]{1,0:T(8,128)(2,1)S(1)} %collective-permute-done.7.refs_4_) | copy-start | bytes 196612
  151.7 2.2 %copy-start.17 = (bf16[64,512]{1,0:T(8,128)(2,1)}, bf16[64,512]{1,0:T(8,128)(2,1)S(1)}, u32[]{:S(2)}) copy-start(bf16[64,512]{1,0:T(8,128)(2,1)S(1)} %collective-permute-done.8.refs_5_) | copy-start | bytes 196612
  153.4 0.6 copy-start.18
  153.9 0.6 copy-start.19

commit v3 on v2

v3 whole, which is shorter than its diff:
```python
import jax
import jax.numpy as jnp
from jax import lax
from jax.experimental import pallas as pl
from jax.experimental.pallas import tpu as pltpu
from jax.sharding import Mesh, PartitionSpec as P


step_size = 0.05
eps_grad = 1e-05
eps_row = 1e-06
f32 = jnp.float32
bf16 = jnp.bfloat16
NT = (((1,), (1,)), ((), ()))
NN = (((1,), (0,)), ((), ()))
ROWS = 8


def dot(a, b, dims):
    return lax.dot_general(a, b, dims, preferred_element_type=f32)


def row_mean(w, i):
    return jnp.mean(w * w, axis=1 if i == 2 else 0, keepdims=True)


def gradients(keys, values, rate_gate, rate_up, rate_down, w_gate, w_up, w_down):
    gate = dot(w_gate, keys, NT)
    up = dot(w_up, keys, NT)
    err = dot(w_down, values, NT)
    sig = jax.nn.sigmoid(gate)
    silu = gate * sig
    hidden = (silu * up).astype(bf16)
    scaled = (hidden.astype(f32) * rate_down).astype(bf16)
    gate_grad = err * up * sig * (1.0 + gate * (1.0 - sig))
    gate_scaled = (gate_grad * rate_gate).astype(bf16)
    up_scaled = (err * silu * rate_up).astype(bf16)
    return (
        dot(gate_scaled, keys, NN),
        dot(up_scaled, keys, NN),
        dot(scaled, values, NN),
    )


def updated(state, init, grad_ref):
    result = []
    for i in range(3):
        grad = grad_ref[256 * i : 256 * (i + 1), :].astype(f32)
        rms = jnp.sqrt(jnp.mean(grad * grad, keepdims=True) + eps_grad)
        stepped = state[i] + grad * (step_size / rms)
        target = jnp.sqrt(row_mean(init[i], i))
        result.append(stepped * (target * lax.rsqrt(row_mean(stepped, i) + eps_row)))
    return result


def first_kernel(at, init_ref, k_ref, v_ref, rates_ref, other_ref, own_ref):
    for head, out_ref in ((1 - at[0], other_ref), (at[0], own_ref)):
        cols = pl.ds(pl.multiple_of(head * 256, 256), 256)
        rates = [rates_ref[i, 0, pl.ds(head, 1), :] for i in range(3)]
        weights = [
            jnp.transpose(init_ref[0, head]),
            jnp.transpose(init_ref[1, head]),
            init_ref[2, head],
        ]
        grads = gradients(k_ref[0, :, cols], v_ref[0, :, cols], *rates, *weights)
        for i in range(3):
            out_ref[256 * i : 256 * (i + 1), :] = grads[i].astype(out_ref.dtype)


def second_kernel(init_ref, grad_ref, own_ref, other_ref, rates_own_ref, rates_other_ref, out_ref, state_ref):
    init = [init_ref[i].astype(f32) for i in range(3)]
    state = updated(init, init, grad_ref)
    weights = [w.astype(bf16) for w in state]
    for i in range(3):
        state_ref[i] = state[i]
    own = gradients(own_ref[0], own_ref[1], *[rates_own_ref[i : i + 1, :] for i in range(3)], *weights)
    other = gradients(other_ref[0], other_ref[1], *[rates_other_ref[i : i + 1, :] for i in range(3)], *weights)
    for i in range(3):
        out_ref[256 * i : 256 * (i + 1), :] = (own[i] + other[i]).astype(bf16)


def applied(q, weights):
    gate = dot(q, weights[0], NT)
    up = dot(q, weights[1], NT)
    hidden = (gate * jax.nn.sigmoid(gate) * up).astype(bf16)
    return dot(hidden, weights[2], NN).astype(bf16).reshape(ROWS, 1, 1, 64, 256)


def apply_first_kernel(at, state_ref, own_ref, other_ref, out_ref):
    weights = [state_ref[i].astype(bf16) for i in range(3)]
    for q, core in ((own_ref[2], at[0]), (other_ref[2], 1 - at[0])):
        out_ref[:, pl.ds(core, 1)] = applied(q, weights)


def last_kernel(at, init_ref, state_ref, grad_ref, own_ref, other_ref, prev_ref, out_ref):
    state = updated([state_ref[i] for i in range(3)], [init_ref[i].astype(f32) for i in range(3)], grad_ref)
    weights = [w.astype(bf16) for w in state]
    for q, core in ((own_ref[3], at[0]), (other_ref[3], 1 - at[0])):
        out_ref[:, pl.ds(core, 1)] = applied(q, weights)


def assemble_kernel(parts_ref, out_ref):
    block, part = pl.program_id(0), pl.program_id(1)
    for head in range(16):
        out_ref[0, :, 256 * head : 256 * (head + 1)] = parts_ref[head, block, pl.ds(part * 32, 32)]


def whole(shape):
    return pl.BlockSpec(shape, lambda i, at: (0,) * len(shape))


def on_chip(array):
    return pltpu.with_memory_space_constraint(array, pltpu.VMEM)


def off_chip(array):
    return pltpu.with_memory_space_constraint(array, pltpu.HBM)


VMEM = pl.BlockSpec(memory_space=pltpu.VMEM)
LIMIT = pltpu.CompilerParams(vmem_limit_bytes=12 << 20)
ANY = pl.BlockSpec(memory_space=pl.ANY)


def call(kernel, in_specs, outs, out_specs=None, aliases=None):
    specs = out_specs or [whole(shape) for shape, _ in outs]
    shapes = [jax.ShapeDtypeStruct(shape, dtype) for shape, dtype in outs]
    if len(outs) == 1:
        specs, shapes = specs[0], shapes[0]
    return pl.pallas_call(
        kernel,
        grid_spec=pltpu.PrefetchScalarGridSpec(
            num_scalar_prefetch=1, grid=(1,), in_specs=in_specs, out_specs=specs
        ),
        out_shape=shapes,
        input_output_aliases=aliases or {},
        compiler_params=LIMIT,
    )


def exchange(array, axes):
    return lax.all_to_all(array, axes, split_axis=0, concat_axis=0, tiled=True)


def scattered(partial):
    parts = exchange(partial.reshape(32, 24, 256), ("x", "z"))
    return jnp.sum(parts.astype(f32), axis=0, keepdims=True)


def gathered(total):
    full = exchange(jnp.broadcast_to(total.astype(bf16), (32, 24, 256)), ("x", "z"))
    return on_chip(full.reshape(768, 256))


def swapped(array):
    return lax.ppermute(array, "c", [(0, 1), (1, 0)])


def program(query_tokens, key_tokens, value_tokens, token_rates, fast_init):
    core = lax.axis_index("c").astype(jnp.int32)
    at = core.reshape(1)

    first_other, first_own = call(
        first_kernel,
        [
            whole((3, 2, 256, 256)),
            pl.BlockSpec((1, 512, 512), lambda i, at: (0, 0, 0)),
            pl.BlockSpec((1, 512, 512), lambda i, at: (0, 0, 0)),
            whole((3, 2, 2, 512)),
        ],
        [((768, 256), bf16), ((768, 256), f32)],
    )(at, *[off_chip(a) for a in (fast_init, key_tokens, value_tokens, token_rates)])
    first_got = swapped(first_other)
    first = (first_own + first_got.astype(f32)).astype(bf16)
    first, query_tokens, key_tokens, value_tokens, token_rates, fast_init = lax.optimization_barrier(
        (first, query_tokens, key_tokens, value_tokens, token_rates, fast_init)
    )

    def pick(which, low, high):
        return jnp.where(which == 0, low, high)

    def half(which):
        return jnp.stack(
            [
                pick(which, a[..., :256], a[..., 256:])
                for a in (key_tokens[1], value_tokens[1], query_tokens[0], query_tokens[1])
            ]
        )

    other = swapped(half(1 - core))
    rates_other = swapped(pick(1 - core, token_rates[:, 1, 0], token_rates[:, 1, 1]))
    own = half(core)
    rates_own = pick(core, token_rates[:, 1, 0], token_rates[:, 1, 1])
    init = pick(core, fast_init[:, 0], fast_init[:, 1])
    init = jnp.stack([init[0].T, init[1].T, init[2]])

    total = scattered(first)
    total, other, rates_other, own, rates_own, init = lax.optimization_barrier(
        (total, other, rates_other, own, rates_own, init)
    )
    summed = gathered(total)
    second, state = pl.pallas_call(
        second_kernel,
        in_specs=[VMEM] * 6,
        out_specs=[VMEM] * 2,
        out_shape=[
            jax.ShapeDtypeStruct((768, 256), bf16),
            jax.ShapeDtypeStruct((3, 256, 256), f32),
        ],
        name="second",
        compiler_params=LIMIT,
    )(on_chip(init), summed, on_chip(own), on_chip(other), on_chip(rates_own), on_chip(rates_other))

    tokens = (4, 512, 256)
    pieces = ((ROWS, 2, 2, 64, 256), bf16)
    out = call(
        apply_first_kernel,
        [whole((3, 256, 256)), whole(tokens), whole(tokens)],
        [pieces],
        [pl.BlockSpec((ROWS, 2, 1, 64, 256), lambda i, at: (0, 0, 0, 0, 0))],
    )(at, state, own, other)

    total = scattered(second)
    total, out = lax.optimization_barrier((total, out))
    summed = gathered(total)
    out = call(
        last_kernel,
        [VMEM, VMEM, VMEM, VMEM, VMEM, ANY],
        [pieces],
        [pl.BlockSpec((ROWS, 2, 1, 64, 256), lambda i, at: (0, 0, 1, 0, 0))],
        aliases={6: 0},
    )(at, on_chip(init), on_chip(state), summed, on_chip(own), on_chip(other), out)
    parts = exchange(out.reshape(16, 2, 64, 256), ("y", "c"))
    return pl.pallas_call(
        assemble_kernel,
        grid=(2, 2),
        in_specs=[VMEM],
        out_specs=pl.BlockSpec((1, 32, 4096), lambda i, j: (i, j, 0)),
        out_shape=jax.ShapeDtypeStruct((2, 64, 4096), bf16),
        name="assemble",
        compiler_params=LIMIT,
    )(on_chip(parts))


def solution(mesh):
    fine = Mesh(mesh.devices.reshape(4, 8, 2, 8), ("x", "z", "c", "y"))
    seq = ("x", "z", "c")
    return jax.shard_map(
        program,
        mesh=fine,
        in_specs=(
            P(None, seq, "y"),
            P(None, seq, "y"),
            P(None, seq, "y"),
            P(None, None, "y", seq),
            P(None, "y", None, None),
        ),
        out_specs=P(None, (*seq, "y"), None),
        check_vma=False,
    )
```

time: 161 us -> 137 us (0.85); the launches traced: 159 us -> 137 us
  starting transfers between devices: 71.4 us -> 28.6 us
  blocking collectives: 36.4 us -> 78.2 us
  Pallas kernels: 23.9 us -> 8.13 us
  waiting for transfers between devices: 17.7 us -> 11.6 us
    all_to_all x2 -> x3, blocking collectives: 36.4 us -> 78.2 us  [exchange(): return lax.all_to_all(array, axes, split_axis=0, concat_axis=0, tiled=True)]
    ppermute x7 -> x0, starting transfers between devices: 28.1 us -> none  [program(): lax.ppermute(pieces[d], 'y', [(j, (j + d) % ROWS) for j in range(ROWS)])]
    pallas_call x8 -> x5, Pallas kernels: 23.9 us -> 8.13 us  [the longest x1 2.91 us: program(): call(first_kernel, [whole((3, 2, 256, 256)), pl.BlockSpec((1, 512, 512),...]
    all_to_all x3 -> x2, starting transfers between devices: 27.4 us -> 15.4 us  [exchange(): return lax.all_to_all(array, axes, split_axis=0, concat_axis=0, tiled=True)]
    all_to_all x3 -> x2, waiting for transfers between devices: 13.9 us -> 10.3 us  [exchange(): return lax.all_to_all(array, axes, split_axis=0, concat_axis=0, tiled=True)]
    ppermute x4 -> x3, starting transfers between devices: 15.9 us -> 13.2 us  [swapped(): return lax.ppermute(array, 'c', [(0, 1), (1, 0)])]
    ppermute x7 -> x0, waiting for transfers between devices: 2.2 us -> none  [program(): lax.ppermute(pieces[d], 'y', [(j, (j + d) % ROWS) for j in range(ROWS)])]
  transfers between devices with their start and end apart: 14 -> 5, of which waited for: 5 -> 3; matrix products, arithmetic and copies ran while one was open for 2% -> 4% of each run, Pallas kernels for 8% -> 1%
where the time goes in v3:
time: 137 us
  blocking collectives  78.2 us (57%)
  starting transfers between devices  28.6 us (21%)
  waiting for transfers between devices  11.6 us (8%)
  Pallas kernels  8.13 us (6%)
  other arithmetic  5.53 us (4%)
  local copies, waits for them, and re-layouts  4.49 us (3%)
    all_to_all x3, blocking collectives, exchange(): return lax.all_to_all(array, axes, split_axis=0, concat_axis=0, tiled=True)  78.2 us
    all_to_all x2, starting transfers between devices, exchange(): return lax.all_to_all(array, axes, split_axis=0, concat_axis=0, tiled=True)  15.4 us
    ppermute x3, starting transfers between devices, swapped(): return lax.ppermute(array, 'c', [(0, 1), (1, 0)])  13.2 us
    all_to_all x2, waiting for transfers between devices, exchange(): return lax.all_to_all(array, axes, split_axis=0, concat_axis=0, tiled=True)  10.3 us
    pallas_call x1, Pallas kernels, program(): call(first_kernel, [whole((3, 2, 256, 256)), pl.BlockSpec((1, 512, 512),...  2.91 us
    unnamed x20, local copies, waits for them, and re-layouts  2.85 us
    another operation x6, other arithmetic, half(): jnp.stack([pick(which, a[..., :256], a[..., 256:]) for a in (key_tokens[1...  2.8 us
  transfers between devices with their start and end apart: 5, of which 3 were waited for; matrix products, arithmetic and copies ran while one was open for 4% of the time, Pallas kernels for 1%

profile of v3, /device:TPU:1, one launch (start us, length us, event | category | flops | bytes accessed | tf_op | source)
XLA Modules:
  0.0 136.8 jit_solution(4910704744715131890)
XLA Ops:
  0.0 2.9 %shard_map.55 = (bf16[768,256]{1,0:T(8,128)(2,1)S(1)}, f32[768,256]{1,0:T(8,128)S(1)}) custom-call(s32[1]{0:T(128)} %bitcast.at, bf16[3,2,256,256]{3,2,1,0:T(8,128)(2,1)} %init_ref.1, bf16[2,512,512]{2,1,0:T(8,128)(2,1)} %k_ref.1, bf16[2,512,512]{2,1,0:T(8,128)(2,1)} %v_ref.1, f32[3,2,2,512]{3,2,1,0:T(2,128)} %rates_ref.1), custom_call_target="tpu_custom_call" | custom-call | tf_op jit(solution)/shard_map/pallas_call | solution.py:163
  2.9 8.8 %collective-permute-start = (bf16[768,256]{1,0:T(8,128)(2,1)S(1)}, bf16[768,256]{1,0:T(8,128)(2,1)S(1)}, u32[]{:S(2)}, u32[]{:S(2)}) collective-permute-start(bf16[768,256]{1,0:T(8,128)(2,1)S(1)} %get-tuple-element.24), channel_id=1, source_target_pairs={{0,8},{8,0},{1,9},{9,1},{2,10},{10,2},{3,11},{11,3},{4,12},{12,4},... | collective-permute-start | bytes 1179656 | tf_op jit(solution)/shard_map/ppermute | solution.py:156
  11.7 1.3 collective-permute-done
  13.0 0.0 copy-start.9
  13.0 0.0 copy-start.5
  13.0 0.8 add_convert_fusion
  13.8 0.0 copy-start.6
  13.9 7.7 %all-to-all-start = ((bf16[32,24,256]{2,1,0:T(8,128)(2,1)}), bf16[32,24,256]{2,1,0:T(8,128)(2,1)S(1)}, u32[]{:S(2)}, u32[]{:S(2)}) async-start(bf16[32,24,256]{2,1,0:T(8,128)(2,1)} %bitcast.60), calls=%async_computation | async-start | bytes 786432 | tf_op jit(solution)/shard_map/all_to_all | solution.py:142
  21.5 0.0 copy-done.9
  21.6 0.0 copy-done.5
  21.6 0.0 copy-done.6
  21.6 1.3 slice_bitcast_fusion.1
  23.0 0.7 select_bitcast_fusion
  23.8 0.8 select_bitcast_fusion.2
  24.5 0.0 copy-start.4
  24.5 1.1 pad_maximum_fusion
  25.6 2.5 %collective-permute-start.1 = (bf16[4,512,256]{2,1,0:T(8,128)(2,1)}, bf16[4,512,256]{2,1,0:T(8,128)(2,1)S(1)}, u32[]{:S(2)}, u32[]{:S(2)}) collective-permute-start(bf16[4,512,256]{2,1,0:T(8,128)(2,1)} %pad_maximum_fusion), channel_id=1, source_target_pairs={{0,8},{8,0},{1,9},{9,1},{2,10},{10,2},{3,11},{11,3},{4,12},{12,4},... | collective-permute-start | bytes 3145736 | tf_op jit(solution)/shard_map/ppermute | solution.py:156
  28.2 0.6 select_bitcast_fusion.8
  28.8 1.9 %collective-permute-start.2 = (f32[3,512]{1,0:T(4,128)}, f32[3,512]{1,0:T(4,128)S(1)}, u32[]{:S(2)}, u32[]{:S(2)}) collective-permute-start(f32[3,512]{1,0:T(4,128)} %get-tuple-element.55), channel_id=1, source_target_pairs={{0,8},{8,0},{1,9},{9,1},{2,10},{10,2},{3,11},{11,3},{4,12},{12,4},... | collective-permute-start | bytes 18440 | tf_op jit(solution)/shard_map/ppermute | solution.py:156
  30.7 0.0 copy-done.4
  30.8 0.1 copy.9
  30.9 0.1 copy.10
  31.0 0.0 copy-start.7
  31.0 0.0 copy-start.8
  31.1 0.9 copy-done.7
  32.0 0.1 copy-done.8
  32.0 0.1 pad_maximum_fusion.1.own_ref
  32.2 1.2 all-to-all-done
  33.4 0.1 convert_reduce_fusion.1
  33.4 0.0 collective-permute-done.2.rates_other_ref
  33.4 0.0 collective-permute-done.1.other_ref
  33.5 19.9 %all_to_all.25 = bf16[32,24,256]{2,1,0:T(8,128)(2,1)S(1)} all-to-all(bf16[32,24,256]{2,1,0:T(8,128)(2,1)S(1)} %broadcast_in_dim.22), channel_id=1, replica_groups=mesh['x'=4,'z'=8,'c'=2,'y'=8] {'x','z'}, dimensions={0} | all-to-all | bytes 786432 | tf_op jit(solution)/shard_map/all_to_all | solution.py:142
  53.4 1.8 %second.1 = (bf16[768,256]{1,0:T(8,128)(2,1)S(1)}, f32[3,256,256]{2,1,0:T(8,128)S(1)}) custom-call(bf16[3,256,256]{2,1,0:T(8,128)(2,1)S(1)} %pad_maximum_fusion.2.init_ref, bf16[768,256]{1,0:T(8,128)(2,1)S(1)} %bitcast.58, bf16[4,512,256]{2,1,0:T(8,128)(2,1)S(1)} %pad_maximum_fusion.1.own_ref, bf16[4,512,256]{2,1,0:T(8,128)(2,1)S(1)} %collective-permute-done.1.other_ref, ...), custom_call_target="tpu_custom_call" | custom-call | tf_op jit(solution)/shard_map/second/pallas_call | solution.py:202
  55.2 0.0 copy-start.3
  55.2 0.7 copy-done.3
  55.9 0.0 copy-start
  55.9 7.7 %all-to-all-start.2 = ((bf16[32,24,256]{2,1,0:T(8,128)(2,1)}), bf16[32,24,256]{2,1,0:T(8,128)(2,1)}, u32[]{:S(2)}, u32[]{:S(2)}) async-start(bf16[32,24,256]{2,1,0:T(8,128)(2,1)} %bitcast.59), calls=%async_computation.2 | async-start | bytes 786432 | tf_op jit(solution)/shard_map/all_to_all | solution.py:142
  63.6 0.0 copy-done
  63.6 0.0 copy-start.1
  63.6 1.1 copy-done.1
  64.8 0.8 shard_map.56.prev_ref
  65.5 9.1 %all-to-all-done.2 = bf16[32,24,256]{2,1,0:T(8,128)(2,1)} async-done(((bf16[32,24,256]{2,1,0:T(8,128)(2,1)}), bf16[32,24,256]{2,1,0:T(8,128)(2,1)}, u32[]{:S(2)}, u32[]{:S(2)}) %all-to-all-start.2) | async-done | bytes 393248 | tf_op jit(solution)/shard_map/all_to_all | solution.py:142
  74.6 1.1 convert_reduce_fusion
  75.8 18.1 %all_to_all.26 = bf16[32,24,256]{2,1,0:T(8,128)(2,1)S(1)} all-to-all(bf16[32,24,256]{2,1,0:T(8,128)(2,1)S(1)} %broadcast_in_dim.25), channel_id=1, replica_groups=mesh['x'=4,'z'=8,'c'=2,'y'=8] {'x','z'}, dimensions={0} | all-to-all | bytes 786432 | tf_op jit(solution)/shard_map/all_to_all | solution.py:142
  93.8 0.0 copy-done.2
  93.8 1.2 shard_map.57
  95.0 40.3 %all_to_all.27.parts_ref = bf16[16,2,64,256]{3,2,1,0:T(8,128)(2,1)S(1)} all-to-all(bf16[16,2,64,256]{3,2,1,0:T(8,128)(2,1)S(1)} %bitcast.56), channel_id=1, replica_groups=mesh['x'=4,'z'=8,'c'=2,'y'=8] {'y','c'}, dimensions={0} | all-to-all | bytes 2097152 | tf_op jit(solution)/shard_map/all_to_all | solution.py:142
  135.3 1.5 %assemble.1 = bf16[2,64,4096]{2,1,0:T(8,128)(2,1)} custom-call(bf16[16,2,64,256]{3,2,1,0:T(8,128)(2,1)S(1)} %all_to_all.27.parts_ref), custom_call_target="tpu_custom_call" | custom-call | tf_op jit(solution)/shard_map/assemble/pallas_call | solution.py:234
  (10 shorter events, 0.3 us)
Async XLA Ops:
  2.9 10.1 %collective-permute-start = (bf16[768,256]{1,0:T(8,128)(2,1)S(1)}, bf16[768,256]{1,0:T(8,128)(2,1)S(1)}, u32[]{:S(2)}, u32[]{:S(2)}) collective-permute-start(bf16[768,256]{1,0:T(8,128)(2,1)S(1)} %get-tuple-element.24), channel_id=1, source_target_pairs={{0,8},{8,0},{1,9},{9,1},{2,10},{10,2},{3,11},{11,3},{4,12},{12,4},... | collective-permute-start | bytes 1179656 | tf_op jit(solution)/shard_map/ppermute | solution.py:156
  13.0 8.5 %copy-start.9 = (f32[3,2,2,512]{3,2,1,0:T(2,128)S(1)}, f32[3,2,2,512]{3,2,1,0:T(2,128)}, u32[]{:S(2)}) copy-start(f32[3,2,2,512]{3,2,1,0:T(2,128)} %rates_ref.1) | copy-start | bytes 73732
  13.0 8.6 %copy-start.5 = (bf16[2,512,512]{2,1,0:T(8,128)(2,1)S(1)}, bf16[2,512,512]{2,1,0:T(8,128)(2,1)}, u32[]{:S(2)}) copy-start(bf16[2,512,512]{2,1,0:T(8,128)(2,1)} %k_ref.1) | copy-start | bytes 3145732
  13.8 7.8 %copy-start.6 = (bf16[2,512,512]{2,1,0:T(8,128)(2,1)S(1)}, bf16[2,512,512]{2,1,0:T(8,128)(2,1)}, u32[]{:S(2)}) copy-start(bf16[2,512,512]{2,1,0:T(8,128)(2,1)} %v_ref.1) | copy-start | bytes 3145732
  13.9 19.5 %all-to-all-start = ((bf16[32,24,256]{2,1,0:T(8,128)(2,1)}), bf16[32,24,256]{2,1,0:T(8,128)(2,1)S(1)}, u32[]{:S(2)}, u32[]{:S(2)}) async-start(bf16[32,24,256]{2,1,0:T(8,128)(2,1)} %bitcast.60), calls=%async_computation | async-start | bytes 786432 | tf_op jit(solution)/shard_map/all_to_all | solution.py:142
  24.5 6.2 %copy-start.4 = (bf16[3,2,256,256]{3,2,1,0:T(8,128)(2,1)S(1)}, bf16[3,2,256,256]{3,2,1,0:T(8,128)(2,1)}, u32[]{:S(2)}) copy-start(bf16[3,2,256,256]{3,2,1,0:T(8,128)(2,1)} %init_ref.1) | copy-start | bytes 2359300
  25.6 7.8 %collective-permute-start.1 = (bf16[4,512,256]{2,1,0:T(8,128)(2,1)}, bf16[4,512,256]{2,1,0:T(8,128)(2,1)S(1)}, u32[]{:S(2)}, u32[]{:S(2)}) collective-permute-start(bf16[4,512,256]{2,1,0:T(8,128)(2,1)} %pad_maximum_fusion), channel_id=1, source_target_pairs={{0,8},{8,0},{1,9},{9,1},{2,10},{10,2},{3,11},{11,3},{4,12},{12,4},... | collective-permute-start | bytes 3145736 | tf_op jit(solution)/shard_map/ppermute | solution.py:156
  28.8 4.6 %collective-permute-start.2 = (f32[3,512]{1,0:T(4,128)}, f32[3,512]{1,0:T(4,128)S(1)}, u32[]{:S(2)}, u32[]{:S(2)}) collective-permute-start(f32[3,512]{1,0:T(4,128)} %get-tuple-element.55), channel_id=1, source_target_pairs={{0,8},{8,0},{1,9},{9,1},{2,10},{10,2},{3,11},{11,3},{4,12},{12,4},... | collective-permute-start | bytes 18440 | tf_op jit(solution)/shard_map/ppermute | solution.py:156
  31.0 1.0 copy-start.7
  31.0 1.0 copy-start.8
  55.2 0.7 copy-start.3
  55.9 7.7 %copy-start = (f32[3,256,256]{2,1,0:T(8,128)}, f32[3,256,256]{2,1,0:T(8,128)S(1)}, u32[]{:S(2)}) copy-start(f32[3,256,256]{2,1,0:T(8,128)S(1)} %get-tuple-element.37.state_ref) | copy-start | bytes 2359300
  55.9 18.7 %all-to-all-start.2 = ((bf16[32,24,256]{2,1,0:T(8,128)(2,1)}), bf16[32,24,256]{2,1,0:T(8,128)(2,1)}, u32[]{:S(2)}, u32[]{:S(2)}) async-start(bf16[32,24,256]{2,1,0:T(8,128)(2,1)} %bitcast.59), calls=%async_computation.2 | async-start | bytes 786432 | tf_op jit(solution)/shard_map/all_to_all | solution.py:142
  63.6 1.1 copy-start.1
  74.6 19.2 %copy-start.2 = (f32[3,256,256]{2,1,0:T(8,128)S(1)}, f32[3,256,256]{2,1,0:T(8,128)}, u32[]{:S(2)}) copy-start(f32[3,256,256]{2,1,0:T(8,128)} %copy-done) | copy-start | bytes 2359300

commit v4 on v3

--- a/solution.py
+++ b/solution.py
@@ -67,12 +67,13 @@
             out_ref[256 * i : 256 * (i + 1), :] = grads[i].astype(out_ref.dtype)
 
 
-def second_kernel(init_ref, grad_ref, own_ref, other_ref, rates_own_ref, rates_other_ref, out_ref, state_ref):
+def second_kernel(init_ref, grad_ref, own_ref, other_ref, rates_own_ref, rates_other_ref, out_ref, state_ref, weights_ref):
     init = [init_ref[i].astype(f32) for i in range(3)]
     state = updated(init, init, grad_ref)
     weights = [w.astype(bf16) for w in state]
     for i in range(3):
         state_ref[i] = state[i]
+        weights_ref[i] = weights[i]
     own = gradients(own_ref[0], own_ref[1], *[rates_own_ref[i : i + 1, :] for i in range(3)], *weights)
     other = gradients(other_ref[0], other_ref[1], *[rates_other_ref[i : i + 1, :] for i in range(3)], *weights)
     for i in range(3):
@@ -83,26 +84,40 @@
     gate = dot(q, weights[0], NT)
     up = dot(q, weights[1], NT)
     hidden = (gate * jax.nn.sigmoid(gate) * up).astype(bf16)
-    return dot(hidden, weights[2], NN).astype(bf16).reshape(ROWS, 1, 1, 64, 256)
-
-
-def apply_first_kernel(at, state_ref, own_ref, other_ref, out_ref):
-    weights = [state_ref[i].astype(bf16) for i in range(3)]
-    for q, core in ((own_ref[2], at[0]), (other_ref[2], 1 - at[0])):
-        out_ref[:, pl.ds(core, 1)] = applied(q, weights)
-
-
-def last_kernel(at, init_ref, state_ref, grad_ref, own_ref, other_ref, prev_ref, out_ref):
+    return dot(hidden, weights[2], NN).astype(bf16)
+
+
+def apply_first_kernel(at, own_ref, other_ref, q_ref, *refs):
+    outs, scratch = refs[:-1], refs[-1]
+    for weights_ref, head in ((own_ref, at[0]), (other_ref, 1 - at[0])):
+        cols = pl.ds(pl.multiple_of(head * 256, 256), 256)
+        weights = [weights_ref[i] for i in range(3)]
+        scratch[:, :, cols] = applied(q_ref[:, cols], weights).reshape(ROWS, 64, 256)
+    for d in range(ROWS):
+        outs[d][...] = scratch[lax.rem(at[1] + d, ROWS)]
+
+
+def last_kernel(at, init_ref, state_ref, grad_ref, own_ref, other_ref, out_ref):
     state = updated([state_ref[i] for i in range(3)], [init_ref[i].astype(f32) for i in range(3)], grad_ref)
     weights = [w.astype(bf16) for w in state]
-    for q, core in ((own_ref[3], at[0]), (other_ref[3], 1 - at[0])):
-        out_ref[:, pl.ds(core, 1)] = applied(q, weights)
-
-
-def assemble_kernel(parts_ref, out_ref):
-    block, part = pl.program_id(0), pl.program_id(1)
-    for head in range(16):
-        out_ref[0, :, 256 * head : 256 * (head + 1)] = parts_ref[head, block, pl.ds(part * 32, 32)]
+    for q, core in ((own_ref[2], at[0]), (other_ref[2], 1 - at[0])):
+        out_ref[:, pl.ds(core, 1)] = applied(q, weights).reshape(ROWS, 1, 64, 256)
+
+
+def assemble_kernel(at, *refs):
+    pieces, parts_ref, out_ref = refs[:ROWS], refs[ROWS], refs[ROWS + 1]
+    rows = pl.ds(pl.program_id(1) * 32, 32)
+
+    @pl.when(pl.program_id(0) == 0)
+    def _():
+        for d in range(ROWS):
+            source = lax.rem(at[1] + ROWS - d, ROWS)
+            out_ref[0, :, pl.ds(pl.multiple_of(source * 512, 512), 512)] = pieces[d][rows]
+
+    @pl.when(pl.program_id(0) == 1)
+    def _():
+        for head in range(16):
+            out_ref[0, :, 256 * head : 256 * (head + 1)] = parts_ref[head, rows]
 
 
 def whole(shape):
@@ -119,7 +134,7 @@
 
 VMEM = pl.BlockSpec(memory_space=pltpu.VMEM)
 LIMIT = pltpu.CompilerParams(vmem_limit_bytes=12 << 20)
-ANY = pl.BlockSpec(memory_space=pl.ANY)
+SCALARS = pl.BlockSpec(memory_space=pltpu.SMEM)
 
 
 def call(kernel, in_specs, outs, out_specs=None, aliases=None):
@@ -144,7 +159,7 @@
 
 def scattered(partial):
     parts = exchange(partial.reshape(32, 24, 256), ("x", "z"))
-    return jnp.sum(parts.astype(f32), axis=0, keepdims=True)
+    return lax.optimization_barrier(jnp.sum(parts.astype(f32), axis=0, keepdims=True))
 
 
 def gathered(total):
@@ -158,7 +173,7 @@
 
 def program(query_tokens, key_tokens, value_tokens, token_rates, fast_init):
     core = lax.axis_index("c").astype(jnp.int32)
-    at = core.reshape(1)
+    at = jnp.stack([core, lax.axis_index("y").astype(jnp.int32)])
 
     first_other, first_own = call(
         first_kernel,
@@ -183,7 +198,7 @@
         return jnp.stack(
             [
                 pick(which, a[..., :256], a[..., 256:])
-                for a in (key_tokens[1], value_tokens[1], query_tokens[0], query_tokens[1])
+                for a in (key_tokens[1], value_tokens[1], query_tokens[1])
             ]
         )
 
@@ -195,51 +210,53 @@
     init = jnp.stack([init[0].T, init[1].T, init[2]])
 
     total = scattered(first)
-    total, other, rates_other, own, rates_own, init = lax.optimization_barrier(
-        (total, other, rates_other, own, rates_own, init)
+    queries = query_tokens[0]
+    total, other, rates_other, own, rates_own, init, queries = lax.optimization_barrier(
+        (total, other, rates_other, own, rates_own, init, queries)
     )
     summed = gathered(total)
-    second, state = pl.pallas_call(
+    second, state, weights = pl.pallas_call(
         second_kernel,
         in_specs=[VMEM] * 6,
-        out_specs=[VMEM] * 2,
+        out_specs=[VMEM] * 3,
         out_shape=[
             jax.ShapeDtypeStruct((768, 256), bf16),
             jax.ShapeDtypeStruct((3, 256, 256), f32),
+            jax.ShapeDtypeStruct((3, 256, 256), bf16),
         ],
         name="second",
         compiler_params=LIMIT,
     )(on_chip(init), summed, on_chip(own), on_chip(other), on_chip(rates_own), on_chip(rates_other))
 
-    tokens = (4, 512, 256)
-    pieces = ((ROWS, 2, 2, 64, 256), bf16)
-    out = call(
+    weights_other = swapped(weights)
+    pieces = pl.pallas_call(
         apply_first_kernel,
-        [whole((3, 256, 256)), whole(tokens), whole(tokens)],
-        [pieces],
-        [pl.BlockSpec((ROWS, 2, 1, 64, 256), lambda i, at: (0, 0, 0, 0, 0))],
-    )(at, state, own, other)
+        in_specs=[SCALARS, VMEM, VMEM, VMEM],
+        out_specs=[VMEM] * ROWS,
+        out_shape=[jax.ShapeDtypeStruct((64, 512), bf16)] * ROWS,
+        scratch_shapes=[pltpu.VMEM((ROWS, 64, 512), bf16)],
+        name="apply_first",
+        compiler_params=LIMIT,
+    )(at, on_chip(weights), on_chip(weights_other), on_chip(queries))
+    got = [pieces[0]]
+    for d in range(1, ROWS):
+        got.append(lax.ppermute(pieces[d], "y", [(j, (j + d) % ROWS) for j in range(ROWS)]))
 
     total = scattered(second)
-    total, out = lax.optimization_barrier((total, out))
     summed = gathered(total)
-    out = call(
-        last_kernel,
-        [VMEM, VMEM, VMEM, VMEM, VMEM, ANY],
-        [pieces],
-        [pl.BlockSpec((ROWS, 2, 1, 64, 256), lambda i, at: (0, 0, 1, 0, 0))],
-        aliases={6: 0},
-    )(at, on_chip(init), on_chip(state), summed, on_chip(own), on_chip(other), out)
-    parts = exchange(out.reshape(16, 2, 64, 256), ("y", "c"))
+    result = call(
+        last_kernel, [VMEM, VMEM, VMEM, VMEM, VMEM], [((ROWS, 2, 64, 256), bf16)]
+    )(at, on_chip(init), on_chip(state), summed, on_chip(own), on_chip(other))
+    parts = exchange(result.reshape(16, 64, 256), ("y", "c"))
     return pl.pallas_call(
         assemble_kernel,
         grid=(2, 2),
-        in_specs=[VMEM],
+        in_specs=[SCALARS] + [VMEM] * (ROWS + 1),
         out_specs=pl.BlockSpec((1, 32, 4096), lambda i, j: (i, j, 0)),
         out_shape=jax.ShapeDtypeStruct((2, 64, 4096), bf16),
         name="assemble",
         compiler_params=LIMIT,
-    )(on_chip(parts))
+    )(at, *[on_chip(a) for a in got], on_chip(parts))
 
 
 def solution(mesh):

time: 137 us -> 146 us (1.066); the launches traced: 137 us -> 144 us
  starting transfers between devices: 28.6 us -> 63.1 us
  blocking collectives: 78.2 us -> 56 us
  waiting for transfers between devices: 11.6 us -> 7.35 us
  local copies, waits for them, and re-layouts: 4.49 us -> 1.49 us
  Pallas kernels: 8.13 us -> 11.1 us
    ppermute x0 -> x7, starting transfers between devices: none -> 28.2 us  [program(): lax.ppermute(pieces[d], 'y', [(j, (j + d) % ROWS) for j in range(ROWS)])]
    all_to_all x3, blocking collectives: 78.2 us -> 56 us  [exchange(): return lax.all_to_all(array, axes, split_axis=0, concat_axis=0, tiled=True)]
    all_to_all x2, waiting for transfers between devices: 10.3 us -> 2.4 us  [exchange(): return lax.all_to_all(array, axes, split_axis=0, concat_axis=0, tiled=True)]
    all_to_all x2, starting transfers between devices: 15.4 us -> 19.7 us  [exchange(): return lax.all_to_all(array, axes, split_axis=0, concat_axis=0, tiled=True)]
    pallas_call x4, Pallas kernels: 5.22 us -> 7.64 us  [the longest x1 2.45 us: program(): call(last_kernel, [VMEM, VMEM, VMEM, VMEM, VMEM], [((ROWS, 2, 64, 256), b...]
    ppermute x0 -> x7, waiting for transfers between devices: none -> 2.04 us  [program(): lax.ppermute(pieces[d], 'y', [(j, (j + d) % ROWS) for j in range(ROWS)])]
    ppermute x3 -> x4, starting transfers between devices: 13.2 us -> 15.2 us  [swapped(): return lax.ppermute(array, 'c', [(0, 1), (1, 0)])]
    unnamed x20 -> x16, local copies, waits for them, and re-layouts: 2.85 us -> 1.05 us
  transfers between devices with their start and end apart: 5 -> 13, of which waited for: 3 -> 5; matrix products, arithmetic and copies ran while one was open for 4% -> 3% of each run, Pallas kernels for 1% -> 1%
where the time goes in v4:
time: 146 us; the launch traced here: 144 us
  starting transfers between devices  63.1 us (43%)
  blocking collectives  56 us (38%)
  Pallas kernels  11.1 us (8%)
  waiting for transfers between devices  7.35 us (5%)
  other arithmetic  4.44 us (3%)
  local copies, waits for them, and re-layouts  1.49 us (1%)
    all_to_all x3, blocking collectives, exchange(): return lax.all_to_all(array, axes, split_axis=0, concat_axis=0, tiled=True)  56 us
    ppermute x7, starting transfers between devices, program(): lax.ppermute(pieces[d], 'y', [(j, (j + d) % ROWS) for j in range(ROWS)])  28.2 us
    all_to_all x2, starting transfers between devices, exchange(): return lax.all_to_all(array, axes, split_axis=0, concat_axis=0, tiled=True)  19.7 us
    ppermute x4, starting transfers between devices, swapped(): return lax.ppermute(array, 'c', [(0, 1), (1, 0)])  15.2 us
    pallas_call x1, Pallas kernels, program(): call(first_kernel, [whole((3, 2, 256, 256)), pl.BlockSpec((1, 512, 512),...  3.46 us
    another operation x5, other arithmetic, half(): jnp.stack([pick(which, a[..., :256], a[..., 256:]) for a in (key_tokens[1...  3.29 us
  transfers between devices with their start and end apart: 13, of which 5 were waited for; matrix products, arithmetic and copies ran while one was open for 3% of the time, Pallas kernels for 1%

profile of v4, /device:TPU:1, one launch (start us, length us, event | category | flops | bytes accessed | tf_op | source)
XLA Modules:
  0.0 143.8 jit_solution(7461557070413125180)
XLA Ops:
  0.0 0.1 pad_add_fusion.at
  0.1 3.5 %shard_map.55 = (bf16[768,256]{1,0:T(8,128)(2,1)S(1)}, f32[768,256]{1,0:T(8,128)S(1)}) custom-call(s32[2]{0:T(128)S(1)} %pad_add_fusion.at, bf16[3,2,256,256]{3,2,1,0:T(8,128)(2,1)} %init_ref.1, bf16[2,512,512]{2,1,0:T(8,128)(2,1)} %k_ref.1, bf16[2,512,512]{2,1,0:T(8,128)(2,1)} %v_ref.1, f32[3,2,2,512]{3,2,1,0:T(2,128)} %rates_ref.1), custom_call_target="tpu_custom_call" | custom-call | tf_op jit(solution)/shard_map/pallas_call | solution.py:178
  3.5 8.8 %collective-permute-start = (bf16[768,256]{1,0:T(8,128)(2,1)S(1)}, bf16[768,256]{1,0:T(8,128)(2,1)S(1)}, u32[]{:S(2)}, u32[]{:S(2)}) collective-permute-start(bf16[768,256]{1,0:T(8,128)(2,1)S(1)} %get-tuple-element.32), channel_id=1, source_target_pairs={{0,8},{8,0},{1,9},{9,1},{2,10},{10,2},{3,11},{11,3},{4,12},{12,4},... | collective-permute-start | bytes 1179656 | tf_op jit(solution)/shard_map/ppermute | solution.py:171
  12.3 1.3 collective-permute-done
  13.6 0.9 add_convert_fusion
  14.5 7.7 %all-to-all-start = ((bf16[32,24,256]{2,1,0:T(8,128)(2,1)}), bf16[32,24,256]{2,1,0:T(8,128)(2,1)S(1)}, u32[]{:S(2)}, u32[]{:S(2)}) async-start(bf16[32,24,256]{2,1,0:T(8,128)(2,1)} %bitcast.56), calls=%async_computation | async-start | bytes 786432 | tf_op jit(solution)/shard_map/all_to_all | solution.py:157
  22.2 2.6 %collective-permute-start.2 = (f32[3,512]{1,0:T(4,128)S(1)}, f32[3,512]{1,0:T(4,128)S(1)}, u32[]{:S(2)}, u32[]{:S(2)}) collective-permute-start(f32[3,512]{1,0:T(4,128)S(1)} %get-tuple-element.69), channel_id=1, source_target_pairs={{0,8},{8,0},{1,9},{9,1},{2,10},{10,2},{3,11},{11,3},{4,12},{12,4},... | collective-permute-start | bytes 18440 | tf_op jit(solution)/shard_map/ppermute | solution.py:171
  24.8 0.1 slice_bitcast_fusion.2
  24.9 0.0 copy-start.3
  24.9 0.7 select_bitcast_fusion.1
  25.6 0.8 select_bitcast_fusion.2
  26.4 0.1 slice_bitcast_fusion
  26.5 0.7 select_bitcast_fusion
  27.2 1.0 pad_maximum_fusion
  28.2 1.9 %collective-permute-start.1 = (bf16[3,512,256]{2,1,0:T(8,128)(2,1)}, bf16[3,512,256]{2,1,0:T(8,128)(2,1)S(1)}, u32[]{:S(2)}, u32[]{:S(2)}) collective-permute-start(bf16[3,512,256]{2,1,0:T(8,128)(2,1)} %pad_maximum_fusion), channel_id=1, source_target_pairs={{0,8},{8,0},{1,9},{9,1},{2,10},{10,2},{3,11},{11,3},{4,12},{12,4},... | collective-permute-start | bytes 2359304 | tf_op jit(solution)/shard_map/ppermute | solution.py:171
  30.2 0.1 copy.8
  30.3 0.1 copy.9
  30.5 0.9 copy-done.4
  31.4 0.1 copy-done.5
  31.4 0.1 copy-done.6
  31.5 0.1 pad_maximum_fusion.1.own_ref
  31.6 2.4 %all-to-all-done = bf16[32,24,256]{2,1,0:T(8,128)(2,1)S(1)} async-done(((bf16[32,24,256]{2,1,0:T(8,128)(2,1)}), bf16[32,24,256]{2,1,0:T(8,128)(2,1)S(1)}, u32[]{:S(2)}, u32[]{:S(2)}) %all-to-all-start) | async-done | bytes 393248 | tf_op jit(solution)/shard_map/all_to_all | solution.py:157
  34.0 0.1 convert_reduce_fusion.1
  34.1 0.0 collective-permute-done.2.rates_other_ref
  34.1 19.5 %all_to_all.25 = bf16[32,24,256]{2,1,0:T(8,128)(2,1)S(1)} all-to-all(bf16[32,24,256]{2,1,0:T(8,128)(2,1)S(1)} %broadcast_in_dim.22), channel_id=1, replica_groups=mesh['x'=4,'z'=8,'c'=2,'y'=8] {'x','z'}, dimensions={0} | all-to-all | bytes 786432 | tf_op jit(solution)/shard_map/all_to_all | solution.py:157
  53.6 1.8 %second.1 = (bf16[768,256]{1,0:T(8,128)(2,1)S(1)}, f32[3,256,256]{2,1,0:T(8,128)S(1)}, bf16[3,256,256]{2,1,0:T(8,128)(2,1)S(1)}) custom-call(bf16[3,256,256]{2,1,0:T(8,128)(2,1)S(1)} %pad_maximum_fusion.2.init_ref, bf16[768,256]{1,0:T(8,128)(2,1)S(1)} %bitcast.53, bf16[3,512,256]{2,1,0:T(8,128)(2,1)S(1)} %pad_maximum_fusion.1.own_ref, ...), custom_call_target="tpu_custom_call" | custom-call | tf_op jit(solution)/shard_map/second/pallas_call | solution.py:218
  55.4 18.4 %all_to_all.26 = bf16[32,24,256]{2,1,0:T(8,128)(2,1)S(1)} all-to-all(bf16[32,24,256]{2,1,0:T(8,128)(2,1)S(1)} %bitcast.55), channel_id=1, replica_groups=mesh['x'=4,'z'=8,'c'=2,'y'=8] {'x','z'}, dimensions={0} | all-to-all | bytes 786432 | tf_op jit(solution)/shard_map/all_to_all | solution.py:157
  73.8 0.1 convert_reduce_fusion
  73.9 18.1 %all_to_all.27 = bf16[32,24,256]{2,1,0:T(8,128)(2,1)S(1)} all-to-all(bf16[32,24,256]{2,1,0:T(8,128)(2,1)S(1)} %broadcast_in_dim.25), channel_id=1, replica_groups=mesh['x'=4,'z'=8,'c'=2,'y'=8] {'x','z'}, dimensions={0} | all-to-all | bytes 786432 | tf_op jit(solution)/shard_map/all_to_all | solution.py:157
  92.0 2.5 %shard_map.56 = bf16[8,2,64,256]{3,2,1,0:T(8,128)(2,1)} custom-call(s32[2]{0:T(128)S(1)} %pad_add_fusion.at, bf16[3,256,256]{2,1,0:T(8,128)(2,1)S(1)} %pad_maximum_fusion.2.init_ref, f32[3,256,256]{2,1,0:T(8,128)S(1)} %get-tuple-element.55.state_ref, bf16[768,256]{1,0:T(8,128)(2,1)S(1)} %bitcast.54, bf16[3,512,256]{2,1,0:T(8,128)(2,1)S(1)} %pad_maximum_fusion.1.own_ref, ...), custom_call_target="tpu_custom_call" | custom-call | tf_op jit(solution)/shard_map/pallas_call | solution.py:247
  94.5 12.0 %all-to-all-start.4 = ((bf16[16,64,256]{2,1,0:T(8,128)(2,1)}), bf16[16,64,256]{2,1,0:T(8,128)(2,1)S(1)}, u32[]{:S(2)}, u32[]{:S(2)}) async-start(bf16[16,64,256]{2,1,0:T(8,128)(2,1)} %bitcast.29), calls=%async_computation.4 | async-start | bytes 1048576 | tf_op jit(solution)/shard_map/all_to_all | solution.py:157
  106.5 2.0 %collective-permute-start.3 = (bf16[3,256,256]{2,1,0:T(8,128)(2,1)S(1)}, bf16[3,256,256]{2,1,0:T(8,128)(2,1)S(1)}, u32[]{:S(2)}, u32[]{:S(2)}) collective-permute-start(bf16[3,256,256]{2,1,0:T(8,128)(2,1)S(1)} %get-tuple-element.45.own_ref), channel_id=1, source_target_pairs={{0,8},{8,0},{1,9},{9,1},{2,10},{10,2},{3,11},{11,3},{4,12},{12,4},... | collective-permute-start | bytes 1179656 | tf_op jit(solution)/shard_map/ppermute | solution.py:171
  108.5 1.6 %collective-permute-done.3.other_ref = bf16[3,256,256]{2,1,0:T(8,128)(2,1)S(1)} collective-permute-done((bf16[3,256,256]{2,1,0:T(8,128)(2,1)S(1)}, bf16[3,256,256]{2,1,0:T(8,128)(2,1)S(1)}, u32[]{:S(2)}, u32[]{:S(2)}) %collective-permute-start.3) | collective-permute-done | bytes 393248 | tf_op jit(solution)/shard_map/ppermute | solution.py:171
  110.1 1.3 apply_first.1
  111.4 3.3 %collective-permute-start.4 = (bf16[64,512]{1,0:T(8,128)(2,1)S(1)}, bf16[64,512]{1,0:T(8,128)(2,1)S(1)}, u32[]{:S(2)}, u32[]{:S(2)}) collective-permute-start(bf16[64,512]{1,0:T(8,128)(2,1)S(1)} %get-tuple-element.48), channel_id=1, source_target_pairs={{0,1},{1,2},{2,3},{3,4},{4,5},{5,6},{6,7},{7,0},{8,9},{9,10},{10,1... | collective-permute-start | bytes 196616 | tf_op jit(solution)/shard_map/ppermute | solution.py:243
  114.7 4.0 %collective-permute-start.5 = (bf16[64,512]{1,0:T(8,128)(2,1)S(1)}, bf16[64,512]{1,0:T(8,128)(2,1)S(1)}, u32[]{:S(2)}, u32[]{:S(2)}) collective-permute-start(bf16[64,512]{1,0:T(8,128)(2,1)S(1)} %get-tuple-element.49), channel_id=1, source_target_pairs={{0,2},{1,3},{2,4},{3,5},{4,6},{5,7},{6,0},{7,1},{8,10},{9,11},{10,... | collective-permute-start | bytes 196616 | tf_op jit(solution)/shard_map/ppermute | solution.py:243
  118.7 4.3 %collective-permute-start.6 = (bf16[64,512]{1,0:T(8,128)(2,1)S(1)}, bf16[64,512]{1,0:T(8,128)(2,1)S(1)}, u32[]{:S(2)}, u32[]{:S(2)}) collective-permute-start(bf16[64,512]{1,0:T(8,128)(2,1)S(1)} %get-tuple-element.50), channel_id=1, source_target_pairs={{0,3},{1,4},{2,5},{3,6},{4,7},{5,0},{6,1},{7,2},{8,11},{9,12},{10,... | collective-permute-start | bytes 196616 | tf_op jit(solution)/shard_map/ppermute | solution.py:243
  123.0 4.0 %collective-permute-start.7 = (bf16[64,512]{1,0:T(8,128)(2,1)S(1)}, bf16[64,512]{1,0:T(8,128)(2,1)S(1)}, u32[]{:S(2)}, u32[]{:S(2)}) collective-permute-start(bf16[64,512]{1,0:T(8,128)(2,1)S(1)} %get-tuple-element.51), channel_id=1, source_target_pairs={{0,4},{1,5},{2,6},{3,7},{4,0},{5,1},{6,2},{7,3},{8,12},{9,13},{10,... | collective-permute-start | bytes 196616 | tf_op jit(solution)/shard_map/ppermute | solution.py:243
  127.0 4.3 %collective-permute-start.8 = (bf16[64,512]{1,0:T(8,128)(2,1)S(1)}, bf16[64,512]{1,0:T(8,128)(2,1)S(1)}, u32[]{:S(2)}, u32[]{:S(2)}) collective-permute-start(bf16[64,512]{1,0:T(8,128)(2,1)S(1)} %get-tuple-element.52), channel_id=1, source_target_pairs={{0,5},{1,6},{2,7},{3,0},{4,1},{5,2},{6,3},{7,4},{8,13},{9,14},{10,... | collective-permute-start | bytes 196616 | tf_op jit(solution)/shard_map/ppermute | solution.py:243
  131.3 0.0 collective-permute-done.4.refs_1_
  131.3 5.2 %collective-permute-start.9 = (bf16[64,512]{1,0:T(8,128)(2,1)S(1)}, bf16[64,512]{1,0:T(8,128)(2,1)S(1)}, u32[]{:S(2)}, u32[]{:S(2)}) collective-permute-start(bf16[64,512]{1,0:T(8,128)(2,1)S(1)} %get-tuple-element.53), channel_id=1, source_target_pairs={{0,6},{1,7},{2,0},{3,1},{4,2},{5,3},{6,4},{7,5},{8,14},{9,15},{10,... | collective-permute-start | bytes 196616 | tf_op jit(solution)/shard_map/ppermute | solution.py:243
  136.5 0.0 collective-permute-done.5.refs_2_
  136.5 3.1 %collective-permute-start.10 = (bf16[64,512]{1,0:T(8,128)(2,1)S(1)}, bf16[64,512]{1,0:T(8,128)(2,1)S(1)}, u32[]{:S(2)}, u32[]{:S(2)}) collective-permute-start(bf16[64,512]{1,0:T(8,128)(2,1)S(1)} %get-tuple-element.54), channel_id=1, source_target_pairs={{0,7},{1,0},{2,1},{3,2},{4,3},{5,4},{6,5},{7,6},{8,15},{9,8},{10,9... | collective-permute-start | bytes 196616 | tf_op jit(solution)/shard_map/ppermute | solution.py:243
  139.6 0.0 collective-permute-done.6.refs_3_
  139.7 0.0 collective-permute-done.8.refs_5_
  139.7 1.5 %collective-permute-done.9.refs_6_ = bf16[64,512]{1,0:T(8,128)(2,1)S(1)} collective-permute-done((bf16[64,512]{1,0:T(8,128)(2,1)S(1)}, bf16[64,512]{1,0:T(8,128)(2,1)S(1)}, u32[]{:S(2)}, u32[]{:S(2)}) %collective-permute-start.9) | collective-permute-done | bytes 65568 | tf_op jit(solution)/shard_map/ppermute | solution.py:243
  141.2 0.5 collective-permute-done.10.refs_7_
  141.7 2.1 %assemble.1 = bf16[2,64,4096]{2,1,0:T(8,128)(2,1)} custom-call(s32[2]{0:T(128)S(1)} %pad_add_fusion.at, bf16[64,512]{1,0:T(8,128)(2,1)S(1)} %get-tuple-element.47.refs_0_, bf16[64,512]{1,0:T(8,128)(2,1)S(1)} %collective-permute-done.4.refs_1_, bf16[64,512]{1,0:T(8,128)(2,1)S(1)} %collective-permute-done.5.refs_2_, ...), custom_call_target="tpu_custom_call" | custom-call | tf_op jit(solution)/shard_map/assemble/pallas_call | solution.py:251
  (22 shorter events, 0.2 us)
Async XLA Ops:
  3.5 10.1 %collective-permute-start = (bf16[768,256]{1,0:T(8,128)(2,1)S(1)}, bf16[768,256]{1,0:T(8,128)(2,1)S(1)}, u32[]{:S(2)}, u32[]{:S(2)}) collective-permute-start(bf16[768,256]{1,0:T(8,128)(2,1)S(1)} %get-tuple-element.32), channel_id=1, source_target_pairs={{0,8},{8,0},{1,9},{9,1},{2,10},{10,2},{3,11},{11,3},{4,12},{12,4},... | collective-permute-start | bytes 1179656 | tf_op jit(solution)/shard_map/ppermute | solution.py:171
  13.6 11.2 %copy-start.1 = (bf16[2,512,512]{2,1,0:T(8,128)(2,1)S(1)}, bf16[2,512,512]{2,1,0:T(8,128)(2,1)}, u32[]{:S(2)}) copy-start(bf16[2,512,512]{2,1,0:T(8,128)(2,1)} %k_ref.1) | copy-start | bytes 3145732
  13.6 11.2 %copy-start.2 = (bf16[2,512,512]{2,1,0:T(8,128)(2,1)S(1)}, bf16[2,512,512]{2,1,0:T(8,128)(2,1)}, u32[]{:S(2)}) copy-start(bf16[2,512,512]{2,1,0:T(8,128)(2,1)} %v_ref.1) | copy-start | bytes 3145732
  14.5 7.7 %copy-start.7 = (f32[3,2,2,512]{3,2,1,0:T(2,128)S(1)}, f32[3,2,2,512]{3,2,1,0:T(2,128)}, u32[]{:S(2)}) copy-start(f32[3,2,2,512]{3,2,1,0:T(2,128)} %rates_ref.1) | copy-start | bytes 73732
  14.5 19.5 %all-to-all-start = ((bf16[32,24,256]{2,1,0:T(8,128)(2,1)}), bf16[32,24,256]{2,1,0:T(8,128)(2,1)S(1)}, u32[]{:S(2)}, u32[]{:S(2)}) async-start(bf16[32,24,256]{2,1,0:T(8,128)(2,1)} %bitcast.56), calls=%async_computation | async-start | bytes 786432 | tf_op jit(solution)/shard_map/all_to_all | solution.py:157
  22.2 11.8 %collective-permute-start.2 = (f32[3,512]{1,0:T(4,128)S(1)}, f32[3,512]{1,0:T(4,128)S(1)}, u32[]{:S(2)}, u32[]{:S(2)}) collective-permute-start(f32[3,512]{1,0:T(4,128)S(1)} %get-tuple-element.69), channel_id=1, source_target_pairs={{0,8},{8,0},{1,9},{9,1},{2,10},{10,2},{3,11},{11,3},{4,12},{12,4},... | collective-permute-start | bytes 18440 | tf_op jit(solution)/shard_map/ppermute | solution.py:171
  24.9 1.5 %copy-start.3 = (bf16[2,512,512]{2,1,0:T(8,128)(2,1)S(1)}, bf16[2,512,512]{2,1,0:T(8,128)(2,1)}, u32[]{:S(2)}) copy-start(bf16[2,512,512]{2,1,0:T(8,128)(2,1)} %param.5) | copy-start | bytes 3145732
  27.2 2.9 %copy-start = (bf16[3,2,256,256]{3,2,1,0:T(8,128)(2,1)S(1)}, bf16[3,2,256,256]{3,2,1,0:T(8,128)(2,1)}, u32[]{:S(2)}) copy-start(bf16[3,2,256,256]{3,2,1,0:T(8,128)(2,1)} %init_ref.1) | copy-start | bytes 2359300
  28.2 5.9 %collective-permute-start.1 = (bf16[3,512,256]{2,1,0:T(8,128)(2,1)}, bf16[3,512,256]{2,1,0:T(8,128)(2,1)S(1)}, u32[]{:S(2)}, u32[]{:S(2)}) collective-permute-start(bf16[3,512,256]{2,1,0:T(8,128)(2,1)} %pad_maximum_fusion), channel_id=1, source_target_pairs={{0,8},{8,0},{1,9},{9,1},{2,10},{10,2},{3,11},{11,3},{4,12},{12,4},... | collective-permute-start | bytes 2359304 | tf_op jit(solution)/shard_map/ppermute | solution.py:171
  30.4 1.0 copy-start.4
  30.4 1.0 copy-start.5
  30.4 1.1 copy-start.6
  94.5 47.3 %all-to-all-start.4 = ((bf16[16,64,256]{2,1,0:T(8,128)(2,1)}), bf16[16,64,256]{2,1,0:T(8,128)(2,1)S(1)}, u32[]{:S(2)}, u32[]{:S(2)}) async-start(bf16[16,64,256]{2,1,0:T(8,128)(2,1)} %bitcast.29), calls=%async_computation.4 | async-start | bytes 1048576 | tf_op jit(solution)/shard_map/all_to_all | solution.py:157
  106.5 3.6 %collective-permute-start.3 = (bf16[3,256,256]{2,1,0:T(8,128)(2,1)S(1)}, bf16[3,256,256]{2,1,0:T(8,128)(2,1)S(1)}, u32[]{:S(2)}, u32[]{:S(2)}) collective-permute-start(bf16[3,256,256]{2,1,0:T(8,128)(2,1)S(1)} %get-tuple-element.45.own_ref), channel_id=1, source_target_pairs={{0,8},{8,0},{1,9},{9,1},{2,10},{10,2},{3,11},{11,3},{4,12},{12,4},... | collective-permute-start | bytes 1179656 | tf_op jit(solution)/shard_map/ppermute | solution.py:171
  111.4 19.9 %collective-permute-start.4 = (bf16[64,512]{1,0:T(8,128)(2,1)S(1)}, bf16[64,512]{1,0:T(8,128)(2,1)S(1)}, u32[]{:S(2)}, u32[]{:S(2)}) collective-permute-start(bf16[64,512]{1,0:T(8,128)(2,1)S(1)} %get-tuple-element.48), channel_id=1, source_target_pairs={{0,1},{1,2},{2,3},{3,4},{4,5},{5,6},{6,7},{7,0},{8,9},{9,10},{10,1... | collective-permute-start | bytes 196616 | tf_op jit(solution)/shard_map/ppermute | solution.py:243
  114.7 21.8 %collective-permute-start.5 = (bf16[64,512]{1,0:T(8,128)(2,1)S(1)}, bf16[64,512]{1,0:T(8,128)(2,1)S(1)}, u32[]{:S(2)}, u32[]{:S(2)}) collective-permute-start(bf16[64,512]{1,0:T(8,128)(2,1)S(1)} %get-tuple-element.49), channel_id=1, source_target_pairs={{0,2},{1,3},{2,4},{3,5},{4,6},{5,7},{6,0},{7,1},{8,10},{9,11},{10,... | collective-permute-start | bytes 196616 | tf_op jit(solution)/shard_map/ppermute | solution.py:243
  118.7 20.9 %collective-permute-start.6 = (bf16[64,512]{1,0:T(8,128)(2,1)S(1)}, bf16[64,512]{1,0:T(8,128)(2,1)S(1)}, u32[]{:S(2)}, u32[]{:S(2)}) collective-permute-start(bf16[64,512]{1,0:T(8,128)(2,1)S(1)} %get-tuple-element.50), channel_id=1, source_target_pairs={{0,3},{1,4},{2,5},{3,6},{4,7},{5,0},{6,1},{7,2},{8,11},{9,12},{10,... | collective-permute-start | bytes 196616 | tf_op jit(solution)/shard_map/ppermute | solution.py:243
  123.0 16.6 %collective-permute-start.7 = (bf16[64,512]{1,0:T(8,128)(2,1)S(1)}, bf16[64,512]{1,0:T(8,128)(2,1)S(1)}, u32[]{:S(2)}, u32[]{:S(2)}) collective-permute-start(bf16[64,512]{1,0:T(8,128)(2,1)S(1)} %get-tuple-element.51), channel_id=1, source_target_pairs={{0,4},{1,5},{2,6},{3,7},{4,0},{5,1},{6,2},{7,3},{8,12},{9,13},{10,... | collective-permute-start | bytes 196616 | tf_op jit(solution)/shard_map/ppermute | solution.py:243
  127.0 12.7 %collective-permute-start.8 = (bf16[64,512]{1,0:T(8,128)(2,1)S(1)}, bf16[64,512]{1,0:T(8,128)(2,1)S(1)}, u32[]{:S(2)}, u32[]{:S(2)}) collective-permute-start(bf16[64,512]{1,0:T(8,128)(2,1)S(1)} %get-tuple-element.52), channel_id=1, source_target_pairs={{0,5},{1,6},{2,7},{3,0},{4,1},{5,2},{6,3},{7,4},{8,13},{9,14},{10,... | collective-permute-start | bytes 196616 | tf_op jit(solution)/shard_map/ppermute | solution.py:243
  131.3 9.9 %collective-permute-start.9 = (bf16[64,512]{1,0:T(8,128)(2,1)S(1)}, bf16[64,512]{1,0:T(8,128)(2,1)S(1)}, u32[]{:S(2)}, u32[]{:S(2)}) collective-permute-start(bf16[64,512]{1,0:T(8,128)(2,1)S(1)} %get-tuple-element.53), channel_id=1, source_target_pairs={{0,6},{1,7},{2,0},{3,1},{4,2},{5,3},{6,4},{7,5},{8,14},{9,15},{10,... | collective-permute-start | bytes 196616 | tf_op jit(solution)/shard_map/ppermute | solution.py:243
  136.5 5.2 %collective-permute-start.10 = (bf16[64,512]{1,0:T(8,128)(2,1)S(1)}, bf16[64,512]{1,0:T(8,128)(2,1)S(1)}, u32[]{:S(2)}, u32[]{:S(2)}) collective-permute-start(bf16[64,512]{1,0:T(8,128)(2,1)S(1)} %get-tuple-element.54), channel_id=1, source_target_pairs={{0,7},{1,0},{2,1},{3,2},{4,3},{5,4},{6,5},{7,6},{8,15},{9,8},{10,9... | collective-permute-start | bytes 196616 | tf_op jit(solution)/shard_map/ppermute | solution.py:243

commit v5 on v4

--- a/solution.py
+++ b/solution.py
@@ -87,14 +87,18 @@
     return dot(hidden, weights[2], NN).astype(bf16)
 
 
-def apply_first_kernel(at, own_ref, other_ref, q_ref, *refs):
+FIRST_LEVEL = ((2, 3, 4), (-3, -2), (1,), (-1,), (0,))
+
+
+def apply_first_kernel(core_ref, row_ref, own_ref, other_ref, q_ref, *refs):
     outs, scratch = refs[:-1], refs[-1]
-    for weights_ref, head in ((own_ref, at[0]), (other_ref, 1 - at[0])):
+    for weights_ref, head in ((own_ref, core_ref[0]), (other_ref, 1 - core_ref[0])):
         cols = pl.ds(pl.multiple_of(head * 256, 256), 256)
         weights = [weights_ref[i] for i in range(3)]
         scratch[:, :, cols] = applied(q_ref[:, cols], weights).reshape(ROWS, 64, 256)
-    for d in range(ROWS):
-        outs[d][...] = scratch[lax.rem(at[1] + d, ROWS)]
+    for ahead, out_ref in zip(FIRST_LEVEL, outs):
+        for i, d in enumerate(ahead):
+            out_ref[i] = scratch[lax.rem(row_ref[0] + ROWS + d, ROWS)]
 
 
 def last_kernel(at, init_ref, state_ref, grad_ref, own_ref, other_ref, out_ref):
@@ -104,20 +108,25 @@
         out_ref[:, pl.ds(core, 1)] = applied(q, weights).reshape(ROWS, 1, 64, 256)
 
 
-def assemble_kernel(at, *refs):
-    pieces, parts_ref, out_ref = refs[:ROWS], refs[ROWS], refs[ROWS + 1]
-    rows = pl.ds(pl.program_id(1) * 32, 32)
-
-    @pl.when(pl.program_id(0) == 0)
-    def _():
-        for d in range(ROWS):
-            source = lax.rem(at[1] + ROWS - d, ROWS)
-            out_ref[0, :, pl.ds(pl.multiple_of(source * 512, 512), 512)] = pieces[d][rows]
-
-    @pl.when(pl.program_id(0) == 1)
-    def _():
-        for head in range(16):
-            out_ref[0, :, 256 * head : 256 * (head + 1)] = parts_ref[head, rows]
+def assemble_first_kernel(row_ref, here_ref, far_ahead_ref, far_behind_ref, ahead_ref, behind_ref, out_ref):
+    for source, piece in (
+        (0, here_ref[0]),
+        (-3, far_ahead_ref[1]),
+        (2, far_behind_ref[1]),
+        (-1, ahead_ref[0]),
+        (-4, ahead_ref[1]),
+        (1, behind_ref[0]),
+        (-2, behind_ref[1]),
+        (3, behind_ref[2]),
+    ):
+        cols = lax.rem(row_ref[0] + ROWS + source, ROWS) * 512
+        out_ref[0, :, pl.ds(pl.multiple_of(cols, 512), 512)] = piece
+
+
+def assemble_second_kernel(parts_ref, prev_ref, out_ref):
+    rows = pl.ds(pl.program_id(0) * 32, 32)
+    for head in range(16):
+        out_ref[0, :, 256 * head : 256 * (head + 1)] = parts_ref[head, rows]
 
 
 def whole(shape):
@@ -134,6 +143,7 @@
 
 VMEM = pl.BlockSpec(memory_space=pltpu.VMEM)
 LIMIT = pltpu.CompilerParams(vmem_limit_bytes=12 << 20)
+ANY = pl.BlockSpec(memory_space=pl.ANY)
 SCALARS = pl.BlockSpec(memory_space=pltpu.SMEM)
 
 
@@ -173,7 +183,8 @@
 
 def program(query_tokens, key_tokens, value_tokens, token_rates, fast_init):
     core = lax.axis_index("c").astype(jnp.int32)
-    at = jnp.stack([core, lax.axis_index("y").astype(jnp.int32)])
+    at = core.reshape(1)
+    row = lax.axis_index("y").astype(jnp.int32).reshape(1)
 
     first_other, first_own = call(
         first_kernel,
@@ -220,27 +231,32 @@
         in_specs=[VMEM] * 6,
         out_specs=[VMEM] * 3,
         out_shape=[
-            jax.ShapeDtypeStruct((768, 256), bf16),
+            pltpu.HBM((768, 256), bf16),
             jax.ShapeDtypeStruct((3, 256, 256), f32),
-            jax.ShapeDtypeStruct((3, 256, 256), bf16),
+            pltpu.HBM((3, 256, 256), bf16),
         ],
         name="second",
         compiler_params=LIMIT,
     )(on_chip(init), summed, on_chip(own), on_chip(other), on_chip(rates_own), on_chip(rates_other))
 
     weights_other = swapped(weights)
-    pieces = pl.pallas_call(
+    far_ahead, far_behind, ahead, behind, here = pl.pallas_call(
         apply_first_kernel,
-        in_specs=[SCALARS, VMEM, VMEM, VMEM],
-        out_specs=[VMEM] * ROWS,
-        out_shape=[jax.ShapeDtypeStruct((64, 512), bf16)] * ROWS,
+        in_specs=[SCALARS, SCALARS, VMEM, VMEM, VMEM],
+        out_specs=[VMEM] * len(FIRST_LEVEL),
+        out_shape=[(pltpu.HBM if len(d) < 3 else jax.ShapeDtypeStruct)((len(d), 64, 512), bf16) for d in FIRST_LEVEL],
         scratch_shapes=[pltpu.VMEM((ROWS, 64, 512), bf16)],
         name="apply_first",
         compiler_params=LIMIT,
-    )(at, on_chip(weights), on_chip(weights_other), on_chip(queries))
-    got = [pieces[0]]
-    for d in range(1, ROWS):
-        got.append(lax.ppermute(pieces[d], "y", [(j, (j + d) % ROWS) for j in range(ROWS)]))
+    )(at, row, off_chip(weights), on_chip(weights_other), on_chip(queries))
+
+    def sent(array, step):
+        return lax.ppermute(array, "y", [(j, (j + step) % ROWS) for j in range(ROWS)])
+
+    far_ahead = sent(far_ahead, 3)
+    far_behind = sent(far_behind, -2)
+    ahead = sent(jnp.concatenate([ahead, far_ahead[2:]]), 1)
+    behind = sent(jnp.concatenate([behind, far_ahead[:1], far_behind[:1]]), -1)
 
     total = scattered(second)
     summed = gathered(total)
@@ -248,15 +264,25 @@
         last_kernel, [VMEM, VMEM, VMEM, VMEM, VMEM], [((ROWS, 2, 64, 256), bf16)]
     )(at, on_chip(init), on_chip(state), summed, on_chip(own), on_chip(other))
     parts = exchange(result.reshape(16, 64, 256), ("y", "c"))
+    out = pl.pallas_call(
+        assemble_first_kernel,
+        grid=(1,),
+        in_specs=[SCALARS] + [VMEM] * 5,
+        out_specs=pl.BlockSpec((1, 64, 4096), lambda i: (0, 0, 0)),
+        out_shape=jax.ShapeDtypeStruct((2, 64, 4096), bf16),
+        name="assemble_first",
+        compiler_params=LIMIT,
+    )(row, off_chip(here), *[on_chip(a) for a in (far_ahead, far_behind, ahead, behind)])
     return pl.pallas_call(
-        assemble_kernel,
-        grid=(2, 2),
-        in_specs=[SCALARS] + [VMEM] * (ROWS + 1),
-        out_specs=pl.BlockSpec((1, 32, 4096), lambda i, j: (i, j, 0)),
+        assemble_second_kernel,
+        grid=(2,),
+        in_specs=[VMEM, ANY],
+        out_specs=pl.BlockSpec((1, 32, 4096), lambda i: (1, i, 0)),
         out_shape=jax.ShapeDtypeStruct((2, 64, 4096), bf16),
-        name="assemble",
-        compiler_params=LIMIT,
-    )(at, *[on_chip(a) for a in got], on_chip(parts))
+        input_output_aliases={1: 0},
+        name="assemble_second",
+        compiler_params=LIMIT,
+    )(on_chip(parts), out)
 
 
 def solution(mesh):

time: 146 us -> 152 us (1.041)
  waiting for transfers between devices: 7.35 us -> 31.7 us
  blocking collectives: 56 us -> 36.6 us
  local copies, waits for them, and re-layouts: 1.49 us -> 5.84 us
  starting transfers between devices: 63.1 us -> 59.2 us
    all_to_all x3 -> x2, blocking collectives: 56 us -> 36.6 us  [exchange(): return lax.all_to_all(array, axes, split_axis=0, concat_axis=0, tiled=True)]
    ppermute x7 -> x4, waiting for transfers between devices: 2.04 us -> 20.9 us  [sent(): lax.ppermute(array, 'y', [(j, (j + step) % ROWS) for j in range(ROWS)])]
    ppermute x7 -> x4, starting transfers between devices: 28.2 us -> 13.9 us  [sent(): lax.ppermute(array, 'y', [(j, (j + step) % ROWS) for j in range(ROWS)])]
    all_to_all x2 -> x3, starting transfers between devices: 19.7 us -> 27.6 us  [exchange(): return lax.all_to_all(array, axes, split_axis=0, concat_axis=0, tiled=True)]
    all_to_all x2 -> x3, waiting for transfers between devices: 2.4 us -> 9.48 us  [exchange(): return lax.all_to_all(array, axes, split_axis=0, concat_axis=0, tiled=True)]
    unnamed x16 -> x22, local copies, waits for them, and re-layouts: 1.05 us -> 3.82 us
    ppermute x4, starting transfers between devices: 15.2 us -> 17.8 us  [swapped(): return lax.ppermute(array, 'c', [(0, 1), (1, 0)])]
    another operation x5, other arithmetic: 3.29 us -> 1.18 us  [half(): jnp.stack([pick(which, a[..., :256], a[..., 256:]) for a in (key_tokens[1...]
  transfers between devices with their start and end apart: 13 -> 11, of which waited for: 5 -> 6; matrix products, arithmetic and copies ran while one was open for 3% -> 2% of each run, Pallas kernels for 1% -> 4%
where the time goes in v5:
time: 152 us; the launch traced here: 150 us
  starting transfers between devices  59.2 us (39%)
  blocking collectives  36.6 us (24%)
  waiting for transfers between devices  31.7 us (21%)
  Pallas kernels  12.3 us (8%)
  local copies, waits for them, and re-layouts  5.84 us (4%)
  other arithmetic  3.89 us (3%)
    all_to_all x2, blocking collectives, exchange(): return lax.all_to_all(array, axes, split_axis=0, concat_axis=0, tiled=True)  36.6 us
    all_to_all x3, starting transfers between devices, exchange(): return lax.all_to_all(array, axes, split_axis=0, concat_axis=0, tiled=True)  27.6 us
    ppermute x4, waiting for transfers between devices, sent(): lax.ppermute(array, 'y', [(j, (j + step) % ROWS) for j in range(ROWS)])  20.9 us
    ppermute x4, starting transfers between devices, swapped(): return lax.ppermute(array, 'c', [(0, 1), (1, 0)])  17.8 us
    ppermute x4, starting transfers between devices, sent(): lax.ppermute(array, 'y', [(j, (j + step) % ROWS) for j in range(ROWS)])  13.9 us
    all_to_all x3, waiting for transfers between devices, exchange(): return lax.all_to_all(array, axes, split_axis=0, concat_axis=0, tiled=True)  9.48 us
    unnamed x22, local copies, waits for them, and re-layouts  3.82 us
  transfers between devices with their start and end apart: 11, of which 6 were waited for; matrix products, arithmetic and copies ran while one was open for 2% of the time, Pallas kernels for 4%

profile of v5, /device:TPU:1, one launch (start us, length us, event | category | flops | bytes accessed | tf_op | source)
XLA Modules:
  0.0 149.8 jit_solution(12235877312299058386)
XLA Ops:
  0.0 2.9 %shard_map.55 = (bf16[768,256]{1,0:T(8,128)(2,1)S(1)}, f32[768,256]{1,0:T(8,128)S(1)}) custom-call(s32[1]{0:T(128)} %bitcast.at.core_ref, bf16[3,2,256,256]{3,2,1,0:T(8,128)(2,1)} %init_ref.1, bf16[2,512,512]{2,1,0:T(8,128)(2,1)} %k_ref.1, bf16[2,512,512]{2,1,0:T(8,128)(2,1)} %v_ref.1, f32[3,2,2,512]{3,2,1,0:T(2,128)} %rates_ref.1), custom_call_target="tpu_custom_call" | custom-call | tf_op jit(solution)/shard_map/pallas_call | solution.py:189
  2.9 8.8 %collective-permute-start = (bf16[768,256]{1,0:T(8,128)(2,1)S(1)}, bf16[768,256]{1,0:T(8,128)(2,1)S(1)}, u32[]{:S(2)}, u32[]{:S(2)}) collective-permute-start(bf16[768,256]{1,0:T(8,128)(2,1)S(1)} %get-tuple-element.29), channel_id=1, source_target_pairs={{0,8},{8,0},{1,9},{9,1},{2,10},{10,2},{3,11},{11,3},{4,12},{12,4},... | collective-permute-start | bytes 1179656 | tf_op jit(solution)/shard_map/ppermute | solution.py:181
  11.7 1.3 collective-permute-done
  13.0 0.9 add_convert_fusion
  13.9 7.8 %all-to-all-start = ((bf16[32,24,256]{2,1,0:T(8,128)(2,1)}), bf16[32,24,256]{2,1,0:T(8,128)(2,1)}, u32[]{:S(2)}, u32[]{:S(2)}) async-start(bf16[32,24,256]{2,1,0:T(8,128)(2,1)} %bitcast.1), calls=%async_computation | async-start | bytes 786432 | tf_op jit(solution)/shard_map/all_to_all | solution.py:167
  21.7 0.6 select_bitcast_fusion.6
  22.3 2.5 %collective-permute-start.2 = (f32[3,512]{1,0:T(4,128)}, f32[3,512]{1,0:T(4,128)S(1)}, u32[]{:S(2)}, u32[]{:S(2)}) collective-permute-start(f32[3,512]{1,0:T(4,128)} %get-tuple-element.65), channel_id=1, source_target_pairs={{0,8},{8,0},{1,9},{9,1},{2,10},{10,2},{3,11},{11,3},{4,12},{12,4},... | collective-permute-start | bytes 18440 | tf_op jit(solution)/shard_map/ppermute | solution.py:181
  24.9 0.1 slice_bitcast_fusion.2
  24.9 0.0 copy-start.7
  25.1 1.1 copy-done.7
  26.2 0.1 slice_bitcast_fusion
  26.3 0.0 copy-start.4
  26.3 1.0 pad_maximum_fusion
  27.3 1.9 %collective-permute-start.1 = (bf16[3,512,256]{2,1,0:T(8,128)(2,1)}, bf16[3,512,256]{2,1,0:T(8,128)(2,1)S(1)}, u32[]{:S(2)}, u32[]{:S(2)}) collective-permute-start(bf16[3,512,256]{2,1,0:T(8,128)(2,1)} %pad_maximum_fusion), channel_id=1, source_target_pairs={{0,8},{8,0},{1,9},{9,1},{2,10},{10,2},{3,11},{11,3},{4,12},{12,4},... | collective-permute-start | bytes 2359304 | tf_op jit(solution)/shard_map/ppermute | solution.py:181
  29.3 0.1 copy.9
  29.4 0.1 copy.10
  29.6 0.1 pad_maximum_fusion.1.own_ref
  29.7 3.8 %all-to-all-done = bf16[32,24,256]{2,1,0:T(8,128)(2,1)} async-done(((bf16[32,24,256]{2,1,0:T(8,128)(2,1)}), bf16[32,24,256]{2,1,0:T(8,128)(2,1)}, u32[]{:S(2)}, u32[]{:S(2)}) %all-to-all-start) | async-done | bytes 393248 | tf_op jit(solution)/shard_map/all_to_all | solution.py:167
  33.5 1.1 convert_reduce_fusion.1
  34.6 0.0 collective-permute-done.1.other_ref
  34.6 18.3 %all_to_all.25 = bf16[32,24,256]{2,1,0:T(8,128)(2,1)S(1)} all-to-all(bf16[32,24,256]{2,1,0:T(8,128)(2,1)S(1)} %broadcast_in_dim.22), channel_id=1, replica_groups=mesh['x'=4,'z'=8,'c'=2,'y'=8] {'x','z'}, dimensions={0} | all-to-all | bytes 786432 | tf_op jit(solution)/shard_map/all_to_all | solution.py:167
  52.9 2.5 %second.1 = (bf16[768,256]{1,0:T(8,128)(2,1)}, f32[3,256,256]{2,1,0:T(8,128)S(1)}, bf16[3,256,256]{2,1,0:T(8,128)(2,1)}) custom-call(bf16[3,256,256]{2,1,0:T(8,128)(2,1)S(1)} %pad_maximum_fusion.2.init_ref, bf16[768,256]{1,0:T(8,128)(2,1)S(1)} %bitcast.53, bf16[3,512,256]{2,1,0:T(8,128)(2,1)S(1)} %pad_maximum_fusion.1.own_ref, ...), custom_call_target="tpu_custom_call" | custom-call | tf_op jit(solution)/shard_map/second/pallas_call | solution.py:229
  55.4 0.9 copy-done
  56.3 18.3 %all_to_all.26 = bf16[32,24,256]{2,1,0:T(8,128)(2,1)S(1)} all-to-all(bf16[32,24,256]{2,1,0:T(8,128)(2,1)} %bitcast.55), channel_id=1, replica_groups=mesh['x'=4,'z'=8,'c'=2,'y'=8] {'x','z'}, dimensions={0} | all-to-all | bytes 786432 | tf_op jit(solution)/shard_map/all_to_all | solution.py:167
  74.6 0.1 convert_reduce_fusion
  74.7 0.8 broadcast_in_dim.25
  75.5 7.4 %all-to-all-start.3 = ((bf16[32,24,256]{2,1,0:T(8,128)(2,1)}), bf16[32,24,256]{2,1,0:T(8,128)(2,1)S(1)}, u32[]{:S(2)}, u32[]{:S(2)}) async-start(bf16[32,24,256]{2,1,0:T(8,128)(2,1)} %broadcast_in_dim.25), calls=%async_computation.3 | async-start | bytes 786432 | tf_op jit(solution)/shard_map/all_to_all | solution.py:167
  82.9 4.6 %collective-permute-start.3 = (bf16[3,256,256]{2,1,0:T(8,128)(2,1)}, bf16[3,256,256]{2,1,0:T(8,128)(2,1)S(1)}, u32[]{:S(2)}, u32[]{:S(2)}) collective-permute-start(bf16[3,256,256]{2,1,0:T(8,128)(2,1)} %get-tuple-element.44.own_ref), channel_id=1, source_target_pairs={{0,8},{8,0},{1,9},{9,1},{2,10},{10,2},{3,11},{11,3},{4,12},{12,4},... | collective-permute-start | bytes 1179656 | tf_op jit(solution)/shard_map/ppermute | solution.py:181
  87.5 5.7 %all-to-all-done.3 = bf16[32,24,256]{2,1,0:T(8,128)(2,1)S(1)} async-done(((bf16[32,24,256]{2,1,0:T(8,128)(2,1)}), bf16[32,24,256]{2,1,0:T(8,128)(2,1)S(1)}, u32[]{:S(2)}, u32[]{:S(2)}) %all-to-all-start.3) | async-done | bytes 393248 | tf_op jit(solution)/shard_map/all_to_all | solution.py:167
  93.1 1.1 copy-done.1
  94.3 1.9 %shard_map.56 = bf16[8,2,64,256]{3,2,1,0:T(8,128)(2,1)} custom-call(s32[1]{0:T(128)} %bitcast.at.core_ref, bf16[3,256,256]{2,1,0:T(8,128)(2,1)S(1)} %pad_maximum_fusion.2.init_ref, f32[3,256,256]{2,1,0:T(8,128)S(1)} %copy-done.1, bf16[768,256]{1,0:T(8,128)(2,1)S(1)} %bitcast.54, bf16[3,512,256]{2,1,0:T(8,128)(2,1)S(1)} %pad_maximum_fusion.1.own_ref, ...), custom_call_target="tpu_custom_call" | custom-call | tf_op jit(solution)/shard_map/pallas_call | solution.py:263
  96.2 12.4 %all-to-all-start.4 = ((bf16[16,64,256]{2,1,0:T(8,128)(2,1)}), bf16[16,64,256]{2,1,0:T(8,128)(2,1)S(1)}, u32[]{:S(2)}, u32[]{:S(2)}) async-start(bf16[16,64,256]{2,1,0:T(8,128)(2,1)} %bitcast.28), calls=%async_computation.4 | async-start | bytes 1048576 | tf_op jit(solution)/shard_map/all_to_all | solution.py:167
  108.6 0.0 collective-permute-done.3.other_ref
  108.6 2.4 %apply_first.1 = (bf16[3,64,512]{2,1,0:T(8,128)(2,1)S(1)}, bf16[2,64,512]{2,1,0:T(8,128)(2,1)}, bf16[1,64,512]{2,1,0:T(8,128)(2,1)}, bf16[1,64,512]{2,1,0:T(8,128)(2,1)}, bf16[1,64,512]{2,1,0:T(8,128)(2,1)}) custom-call(s32[1]{0:T(128)} %bitcast.at.core_ref, s32[1]{0:T(128)} %bitcast.29.row_ref, bf16[3,256,256]{2,1,0:T(8,128)(2,1)} %get-tuple-element.44.own_ref, ...), custom_call_target="tpu_custom_call" | custom-call | tf_op jit(solution)/shard_map/apply_first/pallas_call | solution.py:243
  111.0 5.0 %collective-permute-start.4 = (bf16[3,64,512]{2,1,0:T(8,128)(2,1)S(1)}, bf16[3,64,512]{2,1,0:T(8,128)(2,1)S(1)}, u32[]{:S(2)}, u32[]{:S(2)}) collective-permute-start(bf16[3,64,512]{2,1,0:T(8,128)(2,1)S(1)} %get-tuple-element.47), channel_id=1, source_target_pairs={{0,3},{1,4},{2,5},{3,6},{4,7},{5,0},{6,1},{7,2},{8,11},{9,12},{10,... | collective-permute-start | bytes 589832 | tf_op jit(solution)/shard_map/ppermute | solution.py:254
  116.1 3.4 %collective-permute-start.5 = (bf16[2,64,512]{2,1,0:T(8,128)(2,1)}, bf16[2,64,512]{2,1,0:T(8,128)(2,1)S(1)}, u32[]{:S(2)}, u32[]{:S(2)}) collective-permute-start(bf16[2,64,512]{2,1,0:T(8,128)(2,1)} %get-tuple-element.48), channel_id=1, source_target_pairs={{0,6},{1,7},{2,0},{3,1},{4,2},{5,3},{6,4},{7,5},{8,14},{9,15},{10,... | collective-permute-start | bytes 393224 | tf_op jit(solution)/shard_map/ppermute | solution.py:254
  119.5 7.9 %collective-permute-done.5.far_behind_ref = bf16[2,64,512]{2,1,0:T(8,128)(2,1)S(1)} collective-permute-done((bf16[2,64,512]{2,1,0:T(8,128)(2,1)}, bf16[2,64,512]{2,1,0:T(8,128)(2,1)S(1)}, u32[]{:S(2)}, u32[]{:S(2)}) %collective-permute-start.5) | collective-permute-done | bytes 131104 | tf_op jit(solution)/shard_map/ppermute | solution.py:254
  127.4 0.7 copy-done.2
  128.1 9.4 %collective-permute-done.4.far_ahead_ref = bf16[3,64,512]{2,1,0:T(8,128)(2,1)S(1)} collective-permute-done((bf16[3,64,512]{2,1,0:T(8,128)(2,1)S(1)}, bf16[3,64,512]{2,1,0:T(8,128)(2,1)S(1)}, u32[]{:S(2)}, u32[]{:S(2)}) %collective-permute-start.4) | collective-permute-done | bytes 196640 | tf_op jit(solution)/shard_map/ppermute | solution.py:254
  137.5 0.8 slice-done
  138.3 1.9 %collective-permute-start.7 = (bf16[3,64,512]{2,1,0:T(8,128)(2,1)S(1)}, bf16[3,64,512]{2,1,0:T(8,128)(2,1)S(1)}, u32[]{:S(2)}, u32[]{:S(2)}) collective-permute-start(bf16[3,64,512]{2,1,0:T(8,128)(2,1)S(1)} %pad_maximum_fusion.3), channel_id=1, source_target_pairs={{0,7},{1,0},{2,1},{3,2},{4,3},{5,4},{6,5},{7,6},{8,15},{9,8},{10,9... | collective-permute-start | bytes 589832 | tf_op jit(solution)/shard_map/ppermute | solution.py:254
  140.3 0.0 copy-start.3
  140.3 3.5 %collective-permute-start.6 = (bf16[2,64,512]{2,1,0:T(8,128)(2,1)S(1)}, bf16[2,64,512]{2,1,0:T(8,128)(2,1)S(1)}, u32[]{:S(2)}, u32[]{:S(2)}) collective-permute-start(bf16[2,64,512]{2,1,0:T(8,128)(2,1)S(1)} %pad_maximum_fusion.4), channel_id=1, source_target_pairs={{0,1},{1,2},{2,3},{3,4},{4,5},{5,6},{6,7},{7,0},{8,9},{9,10},{10,1... | collective-permute-start | bytes 393224 | tf_op jit(solution)/shard_map/ppermute | solution.py:254
  143.8 3.6 %collective-permute-done.6.ahead_ref = bf16[2,64,512]{2,1,0:T(8,128)(2,1)S(1)} collective-permute-done((bf16[2,64,512]{2,1,0:T(8,128)(2,1)S(1)}, bf16[2,64,512]{2,1,0:T(8,128)(2,1)S(1)}, u32[]{:S(2)}, u32[]{:S(2)}) %collective-permute-start.6) | collective-permute-done | bytes 131104 | tf_op jit(solution)/shard_map/ppermute | solution.py:254
  147.3 0.0 collective-permute-done.7.behind_ref
  147.4 1.7 %assemble_first.1.prev_ref = bf16[2,64,4096]{2,1,0:T(8,128)(2,1)} custom-call(s32[1]{0:T(128)} %bitcast.29.row_ref, bf16[1,64,512]{2,1,0:T(8,128)(2,1)} %get-tuple-element.46.here_ref, bf16[3,64,512]{2,1,0:T(8,128)(2,1)S(1)} %collective-permute-done.4.far_ahead_ref, bf16[2,64,512]{2,1,0:T(8,128)(2,1)S(1)} %copy-done.3, ...), custom_call_target="tpu_custom_call" | custom-call | tf_op jit(solution)/shard_map/assemble_first/pallas_call | solution.py:267
  149.0 0.0 all-to-all-done.4.parts_ref
  149.0 0.8 assemble_second.1
  (28 shorter events, 0.4 us)
Async XLA Ops:
  2.9 10.1 %collective-permute-start = (bf16[768,256]{1,0:T(8,128)(2,1)S(1)}, bf16[768,256]{1,0:T(8,128)(2,1)S(1)}, u32[]{:S(2)}, u32[]{:S(2)}) collective-permute-start(bf16[768,256]{1,0:T(8,128)(2,1)S(1)} %get-tuple-element.29), channel_id=1, source_target_pairs={{0,8},{8,0},{1,9},{9,1},{2,10},{10,2},{3,11},{11,3},{4,12},{12,4},... | collective-permute-start | bytes 1179656 | tf_op jit(solution)/shard_map/ppermute | solution.py:181
  13.0 11.8 %copy-start.5 = (bf16[2,512,512]{2,1,0:T(8,128)(2,1)S(1)}, bf16[2,512,512]{2,1,0:T(8,128)(2,1)}, u32[]{:S(2)}) copy-start(bf16[2,512,512]{2,1,0:T(8,128)(2,1)} %k_ref.1) | copy-start | bytes 3145732
  13.0 11.9 %copy-start.6 = (bf16[2,512,512]{2,1,0:T(8,128)(2,1)S(1)}, bf16[2,512,512]{2,1,0:T(8,128)(2,1)}, u32[]{:S(2)}) copy-start(bf16[2,512,512]{2,1,0:T(8,128)(2,1)} %v_ref.1) | copy-start | bytes 3145732
  13.9 7.8 %copy-start.8 = (f32[3,2,2,512]{3,2,1,0:T(2,128)S(1)}, f32[3,2,2,512]{3,2,1,0:T(2,128)}, u32[]{:S(2)}) copy-start(f32[3,2,2,512]{3,2,1,0:T(2,128)} %rates_ref.1) | copy-start | bytes 73732
  13.9 19.6 %all-to-all-start = ((bf16[32,24,256]{2,1,0:T(8,128)(2,1)}), bf16[32,24,256]{2,1,0:T(8,128)(2,1)}, u32[]{:S(2)}, u32[]{:S(2)}) async-start(bf16[32,24,256]{2,1,0:T(8,128)(2,1)} %bitcast.1), calls=%async_computation | async-start | bytes 786432 | tf_op jit(solution)/shard_map/all_to_all | solution.py:167
  22.3 12.3 %collective-permute-start.2 = (f32[3,512]{1,0:T(4,128)}, f32[3,512]{1,0:T(4,128)S(1)}, u32[]{:S(2)}, u32[]{:S(2)}) collective-permute-start(f32[3,512]{1,0:T(4,128)} %get-tuple-element.65), channel_id=1, source_target_pairs={{0,8},{8,0},{1,9},{9,1},{2,10},{10,2},{3,11},{11,3},{4,12},{12,4},... | collective-permute-start | bytes 18440 | tf_op jit(solution)/shard_map/ppermute | solution.py:181
  24.9 1.2 copy-start.7
  26.3 2.9 %copy-start.4 = (bf16[3,2,256,256]{3,2,1,0:T(8,128)(2,1)S(1)}, bf16[3,2,256,256]{3,2,1,0:T(8,128)(2,1)}, u32[]{:S(2)}) copy-start(bf16[3,2,256,256]{3,2,1,0:T(8,128)(2,1)} %init_ref.1) | copy-start | bytes 2359300
  27.3 7.3 %collective-permute-start.1 = (bf16[3,512,256]{2,1,0:T(8,128)(2,1)}, bf16[3,512,256]{2,1,0:T(8,128)(2,1)S(1)}, u32[]{:S(2)}, u32[]{:S(2)}) collective-permute-start(bf16[3,512,256]{2,1,0:T(8,128)(2,1)} %pad_maximum_fusion), channel_id=1, source_target_pairs={{0,8},{8,0},{1,9},{9,1},{2,10},{10,2},{3,11},{11,3},{4,12},{12,4},... | collective-permute-start | bytes 2359304 | tf_op jit(solution)/shard_map/ppermute | solution.py:181
  55.4 0.9 copy-start
  75.5 17.7 %all-to-all-start.3 = ((bf16[32,24,256]{2,1,0:T(8,128)(2,1)}), bf16[32,24,256]{2,1,0:T(8,128)(2,1)S(1)}, u32[]{:S(2)}, u32[]{:S(2)}) async-start(bf16[32,24,256]{2,1,0:T(8,128)(2,1)} %broadcast_in_dim.25), calls=%async_computation.3 | async-start | bytes 786432 | tf_op jit(solution)/shard_map/all_to_all | solution.py:167
  82.9 25.7 %collective-permute-start.3 = (bf16[3,256,256]{2,1,0:T(8,128)(2,1)}, bf16[3,256,256]{2,1,0:T(8,128)(2,1)S(1)}, u32[]{:S(2)}, u32[]{:S(2)}) collective-permute-start(bf16[3,256,256]{2,1,0:T(8,128)(2,1)} %get-tuple-element.44.own_ref), channel_id=1, source_target_pairs={{0,8},{8,0},{1,9},{9,1},{2,10},{10,2},{3,11},{11,3},{4,12},{12,4},... | collective-permute-start | bytes 1179656 | tf_op jit(solution)/shard_map/ppermute | solution.py:181
  93.1 1.1 copy-start.1
  96.2 52.8 %all-to-all-start.4 = ((bf16[16,64,256]{2,1,0:T(8,128)(2,1)}), bf16[16,64,256]{2,1,0:T(8,128)(2,1)S(1)}, u32[]{:S(2)}, u32[]{:S(2)}) async-start(bf16[16,64,256]{2,1,0:T(8,128)(2,1)} %bitcast.28), calls=%async_computation.4 | async-start | bytes 1048576 | tf_op jit(solution)/shard_map/all_to_all | solution.py:167
  111.0 26.4 %collective-permute-start.4 = (bf16[3,64,512]{2,1,0:T(8,128)(2,1)S(1)}, bf16[3,64,512]{2,1,0:T(8,128)(2,1)S(1)}, u32[]{:S(2)}, u32[]{:S(2)}) collective-permute-start(bf16[3,64,512]{2,1,0:T(8,128)(2,1)S(1)} %get-tuple-element.47), channel_id=1, source_target_pairs={{0,3},{1,4},{2,5},{3,6},{4,7},{5,0},{6,1},{7,2},{8,11},{9,12},{10,... | collective-permute-start | bytes 589832 | tf_op jit(solution)/shard_map/ppermute | solution.py:254
  116.1 11.4 %collective-permute-start.5 = (bf16[2,64,512]{2,1,0:T(8,128)(2,1)}, bf16[2,64,512]{2,1,0:T(8,128)(2,1)S(1)}, u32[]{:S(2)}, u32[]{:S(2)}) collective-permute-start(bf16[2,64,512]{2,1,0:T(8,128)(2,1)} %get-tuple-element.48), channel_id=1, source_target_pairs={{0,6},{1,7},{2,0},{3,1},{4,2},{5,3},{6,4},{7,5},{8,14},{9,15},{10,... | collective-permute-start | bytes 393224 | tf_op jit(solution)/shard_map/ppermute | solution.py:254
  127.4 0.7 copy-start.2
  128.1 9.4 %copy-start.10 = (bf16[1,64,512]{2,1,0:T(8,128)(2,1)S(1)}, bf16[1,64,512]{2,1,0:T(8,128)(2,1)}, u32[]{:S(2)}) copy-start(bf16[1,64,512]{2,1,0:T(8,128)(2,1)} %get-tuple-element.50) | copy-start | bytes 196612
  137.4 0.8 slice-start
  138.3 2.0 %copy-start.9 = (bf16[1,64,512]{2,1,0:T(8,128)(2,1)S(1)}, bf16[1,64,512]{2,1,0:T(8,128)(2,1)}, u32[]{:S(2)}) copy-start(bf16[1,64,512]{2,1,0:T(8,128)(2,1)} %get-tuple-element.49) | copy-start | bytes 196612
  138.3 9.0 %collective-permute-start.7 = (bf16[3,64,512]{2,1,0:T(8,128)(2,1)S(1)}, bf16[3,64,512]{2,1,0:T(8,128)(2,1)S(1)}, u32[]{:S(2)}, u32[]{:S(2)}) collective-permute-start(bf16[3,64,512]{2,1,0:T(8,128)(2,1)S(1)} %pad_maximum_fusion.3), channel_id=1, source_target_pairs={{0,7},{1,0},{2,1},{3,2},{4,3},{5,4},{6,5},{7,6},{8,15},{9,8},{10,9... | collective-permute-start | bytes 589832 | tf_op jit(solution)/shard_map/ppermute | solution.py:254
  140.3 7.1 %copy-start.3 = (bf16[2,64,512]{2,1,0:T(8,128)(2,1)S(1)}, bf16[2,64,512]{2,1,0:T(8,128)(2,1)}, u32[]{:S(2)}) copy-start(bf16[2,64,512]{2,1,0:T(8,128)(2,1)} %copy-done.2) | copy-start | bytes 393220
  140.3 7.1 %collective-permute-start.6 = (bf16[2,64,512]{2,1,0:T(8,128)(2,1)S(1)}, bf16[2,64,512]{2,1,0:T(8,128)(2,1)S(1)}, u32[]{:S(2)}, u32[]{:S(2)}) collective-permute-start(bf16[2,64,512]{2,1,0:T(8,128)(2,1)S(1)} %pad_maximum_fusion.4), channel_id=1, source_target_pairs={{0,1},{1,2},{2,3},{3,4},{4,5},{5,6},{6,7},{7,0},{8,9},{9,10},{10,1... | collective-permute-start | bytes 393224 | tf_op jit(solution)/shard_map/ppermute | solution.py:254

commit v6 on v5

--- a/solution.py
+++ b/solution.py
@@ -42,14 +42,13 @@
     )
 
 
-def updated(state, init, grad_ref):
+def updated(state, targets, grad_ref):
     result = []
     for i in range(3):
         grad = grad_ref[256 * i : 256 * (i + 1), :].astype(f32)
         rms = jnp.sqrt(jnp.mean(grad * grad, keepdims=True) + eps_grad)
         stepped = state[i] + grad * (step_size / rms)
-        target = jnp.sqrt(row_mean(init[i], i))
-        result.append(stepped * (target * lax.rsqrt(row_mean(stepped, i) + eps_row)))
+        result.append(stepped * (targets[i] * lax.rsqrt(row_mean(stepped, i) + eps_row)))
     return result
 
 
@@ -67,17 +66,28 @@
             out_ref[256 * i : 256 * (i + 1), :] = grads[i].astype(out_ref.dtype)
 
 
-def second_kernel(init_ref, grad_ref, own_ref, other_ref, rates_own_ref, rates_other_ref, out_ref, state_ref, weights_ref):
+KEPT = (1032, 256)
+
+
+def second_kernel(init_ref, grad_ref, own_ref, other_ref, rates_own_ref, rates_other_ref, out_ref, kept_ref):
     init = [init_ref[i].astype(f32) for i in range(3)]
-    state = updated(init, init, grad_ref)
+    targets = [jnp.sqrt(row_mean(w, i)) for i, w in enumerate(init)]
+    state = updated(init, targets, grad_ref)
     weights = [w.astype(bf16) for w in state]
     for i in range(3):
-        state_ref[i] = state[i]
-        weights_ref[i] = weights[i]
+        kept_ref[256 * i : 256 * (i + 1), :] = state[i]
+    kept_ref[768:1024, :] = jnp.broadcast_to(targets[2], (256, 256))
+    kept_ref[1024:1025, :] = targets[0]
+    kept_ref[1025:1026, :] = targets[1]
+    kept_ref[1026:1032, :] = jnp.zeros((6, 256), f32)
     own = gradients(own_ref[0], own_ref[1], *[rates_own_ref[i : i + 1, :] for i in range(3)], *weights)
     other = gradients(other_ref[0], other_ref[1], *[rates_other_ref[i : i + 1, :] for i in range(3)], *weights)
     for i in range(3):
         out_ref[256 * i : 256 * (i + 1), :] = (own[i] + other[i]).astype(bf16)
+
+
+def state_of(kept_ref):
+    return [kept_ref[256 * i : 256 * (i + 1), :] for i in range(3)]
 
 
 def applied(q, weights):
@@ -87,40 +97,76 @@
     return dot(hidden, weights[2], NN).astype(bf16)
 
 
+def prepare_kernel(core_ref, k_ref, v_ref, q_ref, init_ref, rates_ref, own_ref, other_ref, w_ref, rates_own_ref, rates_other_ref):
+    for head, out_ref, rates_out_ref in (
+        (core_ref[0], own_ref, rates_own_ref),
+        (1 - core_ref[0], other_ref, rates_other_ref),
+    ):
+        cols = pl.ds(pl.multiple_of(head * 256, 256), 256)
+        out_ref[0] = k_ref[0, :, cols]
+        out_ref[1] = v_ref[0, :, cols]
+        out_ref[2] = q_ref[1, :, cols]
+        out_ref[3] = q_ref[0, :, cols]
+        for i in range(3):
+            rates_out_ref[i : i + 1, :] = rates_ref[i, 1, pl.ds(head, 1), :]
+    for i in range(3):
+        w = init_ref[i, core_ref[0]]
+        w_ref[i] = w if i == 2 else jnp.transpose(w)
+
+
 FIRST_LEVEL = ((2, 3, 4), (-3, -2), (1,), (-1,), (0,))
-
-
-def apply_first_kernel(core_ref, row_ref, own_ref, other_ref, q_ref, *refs):
+SOURCES = (0, -3, 2, -1, -4, 1, -2, 3)
+
+
+def apply_first_kernel(row_ref, kept_ref, own_ref, other_ref, *refs):
     outs, scratch = refs[:-1], refs[-1]
-    for weights_ref, head in ((own_ref, core_ref[0]), (other_ref, 1 - core_ref[0])):
-        cols = pl.ds(pl.multiple_of(head * 256, 256), 256)
-        weights = [weights_ref[i] for i in range(3)]
-        scratch[:, :, cols] = applied(q_ref[:, cols], weights).reshape(ROWS, 64, 256)
+    weights = [w.astype(bf16) for w in state_of(kept_ref)]
+    for q, side in ((own_ref[3], 0), (other_ref[3], 1)):
+        scratch[:, side] = applied(q, weights).reshape(ROWS, 64, 256)
     for ahead, out_ref in zip(FIRST_LEVEL, outs):
         for i, d in enumerate(ahead):
             out_ref[i] = scratch[lax.rem(row_ref[0] + ROWS + d, ROWS)]
 
 
-def last_kernel(at, init_ref, state_ref, grad_ref, own_ref, other_ref, out_ref):
-    state = updated([state_ref[i] for i in range(3)], [init_ref[i].astype(f32) for i in range(3)], grad_ref)
+def last_kernel(at, kept_ref, grad_ref, own_ref, other_ref, out_ref):
+    targets = [kept_ref[1024:1025, :], kept_ref[1025:1026, :], kept_ref[768:1024, :]]
+    state = updated(state_of(kept_ref), targets, grad_ref)
     weights = [w.astype(bf16) for w in state]
     for q, core in ((own_ref[2], at[0]), (other_ref[2], 1 - at[0])):
         out_ref[:, pl.ds(core, 1)] = applied(q, weights).reshape(ROWS, 1, 64, 256)
 
 
-def assemble_first_kernel(row_ref, here_ref, far_ahead_ref, far_behind_ref, ahead_ref, behind_ref, out_ref):
-    for source, piece in (
-        (0, here_ref[0]),
-        (-3, far_ahead_ref[1]),
-        (2, far_behind_ref[1]),
-        (-1, ahead_ref[0]),
-        (-4, ahead_ref[1]),
-        (1, behind_ref[0]),
-        (-2, behind_ref[1]),
-        (3, behind_ref[2]),
-    ):
-        cols = lax.rem(row_ref[0] + ROWS + source, ROWS) * 512
-        out_ref[0, :, pl.ds(pl.multiple_of(cols, 512), 512)] = piece
+def total_kernel(parts_ref, out_ref):
+    total = jnp.sum(parts_ref[...].astype(f32), axis=0, keepdims=True)
+    out_ref[...] = jnp.broadcast_to(total.astype(bf16), out_ref.shape)
+
+
+def pieces_of(here_ref, far_ahead_ref, far_behind_ref, ahead_ref, behind_ref, side):
+    return (
+        here_ref[0, side],
+        far_ahead_ref[1, side],
+        far_behind_ref[1, side],
+        ahead_ref[0, side],
+        ahead_ref[1, side],
+        behind_ref[0, side],
+        behind_ref[1, side],
+        behind_ref[2, side],
+    )
+
+
+def collect_kernel(*refs):
+    for i, piece in enumerate(pieces_of(*refs[:5], 1)):
+        refs[5][i] = piece
+
+
+def assemble_first_kernel(core_ref, row_ref, *refs):
+    swapped_ref, out_ref = refs[5], refs[6]
+    for i, (source, piece) in enumerate(zip(SOURCES, pieces_of(*refs[:5], 0))):
+        first = lax.rem(row_ref[0] + ROWS + source, ROWS) * 512
+        own = pl.multiple_of(first + core_ref[0] * 256, 256)
+        other = pl.multiple_of(first + (1 - core_ref[0]) * 256, 256)
+        out_ref[0, :, pl.ds(own, 256)] = piece
+        out_ref[0, :, pl.ds(other, 256)] = swapped_ref[i]
 
 
 def assemble_second_kernel(parts_ref, prev_ref, out_ref):
@@ -169,11 +215,18 @@
 
 def scattered(partial):
     parts = exchange(partial.reshape(32, 24, 256), ("x", "z"))
-    return lax.optimization_barrier(jnp.sum(parts.astype(f32), axis=0, keepdims=True))
+    return pl.pallas_call(
+        total_kernel,
+        in_specs=[VMEM],
+        out_specs=VMEM,
+        out_shape=jax.ShapeDtypeStruct((32, 24, 256), bf16),
+        name="total",
+        compiler_params=LIMIT,
+    )(on_chip(parts))
 
 
 def gathered(total):
-    full = exchange(jnp.broadcast_to(total.astype(bf16), (32, 24, 256)), ("x", "z"))
+    full = exchange(total, ("x", "z"))
     return on_chip(full.reshape(768, 256))
 
 
@@ -202,53 +255,50 @@
         (first, query_tokens, key_tokens, value_tokens, token_rates, fast_init)
     )
 
-    def pick(which, low, high):
-        return jnp.where(which == 0, low, high)
-
-    def half(which):
-        return jnp.stack(
-            [
-                pick(which, a[..., :256], a[..., 256:])
-                for a in (key_tokens[1], value_tokens[1], query_tokens[1])
-            ]
-        )
-
-    other = swapped(half(1 - core))
-    rates_other = swapped(pick(1 - core, token_rates[:, 1, 0], token_rates[:, 1, 1]))
-    own = half(core)
-    rates_own = pick(core, token_rates[:, 1, 0], token_rates[:, 1, 1])
-    init = pick(core, fast_init[:, 0], fast_init[:, 1])
-    init = jnp.stack([init[0].T, init[1].T, init[2]])
+    tokens = (4, 512, 256)
+    own, other, init, rates_own, rates_other = call(
+        prepare_kernel,
+        [
+            pl.BlockSpec((1, 512, 512), lambda i, at: (1, 0, 0)),
+            pl.BlockSpec((1, 512, 512), lambda i, at: (1, 0, 0)),
+            whole((2, 512, 512)),
+            whole((3, 2, 256, 256)),
+            whole((3, 2, 2, 512)),
+        ],
+        [(tokens, bf16), (tokens, bf16), ((3, 256, 256), bf16), ((3, 512), f32), ((3, 512), f32)],
+    )(at, *[off_chip(a) for a in (key_tokens, value_tokens, query_tokens, fast_init, token_rates)])
+    other = swapped(other)
+    rates_other = swapped(rates_other)
 
     total = scattered(first)
-    queries = query_tokens[0]
-    total, other, rates_other, own, rates_own, init, queries = lax.optimization_barrier(
-        (total, other, rates_other, own, rates_own, init, queries)
+    total, other, rates_other, own, rates_own, init = lax.optimization_barrier(
+        (total, other, rates_other, own, rates_own, init)
     )
     summed = gathered(total)
-    second, state, weights = pl.pallas_call(
+    second, kept = pl.pallas_call(
         second_kernel,
         in_specs=[VMEM] * 6,
-        out_specs=[VMEM] * 3,
+        out_specs=[VMEM] * 2,
         out_shape=[
             pltpu.HBM((768, 256), bf16),
-            jax.ShapeDtypeStruct((3, 256, 256), f32),
-            pltpu.HBM((3, 256, 256), bf16),
+            jax.ShapeDtypeStruct(KEPT, f32),
         ],
         name="second",
         compiler_params=LIMIT,
-    )(on_chip(init), summed, on_chip(own), on_chip(other), on_chip(rates_own), on_chip(rates_other))
-
-    weights_other = swapped(weights)
+    )(on_chip(init), summed, on_chip(own), on_chip(other), rates_own, rates_other)
+
     far_ahead, far_behind, ahead, behind, here = pl.pallas_call(
         apply_first_kernel,
-        in_specs=[SCALARS, SCALARS, VMEM, VMEM, VMEM],
+        in_specs=[SCALARS, VMEM, VMEM, VMEM],
         out_specs=[VMEM] * len(FIRST_LEVEL),
-        out_shape=[(pltpu.HBM if len(d) < 3 else jax.ShapeDtypeStruct)((len(d), 64, 512), bf16) for d in FIRST_LEVEL],
-        scratch_shapes=[pltpu.VMEM((ROWS, 64, 512), bf16)],
+        out_shape=[
+            (pltpu.HBM if d in ((1,), (-1,)) else jax.ShapeDtypeStruct)((len(d), 2, 64, 256), bf16)
+            for d in FIRST_LEVEL
+        ],
+        scratch_shapes=[pltpu.VMEM((ROWS, 2, 64, 256), bf16)],
         name="apply_first",
         compiler_params=LIMIT,
-    )(at, row, off_chip(weights), on_chip(weights_other), on_chip(queries))
+    )(row, on_chip(kept), on_chip(own), on_chip(other))
 
     def sent(array, step):
         return lax.ppermute(array, "y", [(j, (j + step) % ROWS) for j in range(ROWS)])
@@ -261,18 +311,28 @@
     total = scattered(second)
     summed = gathered(total)
     result = call(
-        last_kernel, [VMEM, VMEM, VMEM, VMEM, VMEM], [((ROWS, 2, 64, 256), bf16)]
-    )(at, on_chip(init), on_chip(state), summed, on_chip(own), on_chip(other))
+        last_kernel, [VMEM, VMEM, VMEM, VMEM], [((ROWS, 2, 64, 256), bf16)]
+    )(at, on_chip(kept), summed, on_chip(own), on_chip(other))
     parts = exchange(result.reshape(16, 64, 256), ("y", "c"))
+    got = [on_chip(a) for a in (here, far_ahead, far_behind, ahead, behind)]
+    halves = pl.pallas_call(
+        collect_kernel,
+        in_specs=[VMEM] * 5,
+        out_specs=VMEM,
+        out_shape=jax.ShapeDtypeStruct((ROWS, 64, 256), bf16),
+        name="collect",
+        compiler_params=LIMIT,
+    )(*got)
+    halves = swapped(halves)
     out = pl.pallas_call(
         assemble_first_kernel,
         grid=(1,),
-        in_specs=[SCALARS] + [VMEM] * 5,
+        in_specs=[SCALARS] * 2 + [VMEM] * 6,
         out_specs=pl.BlockSpec((1, 64, 4096), lambda i: (0, 0, 0)),
         out_shape=jax.ShapeDtypeStruct((2, 64, 4096), bf16),
         name="assemble_first",
         compiler_params=LIMIT,
-    )(row, off_chip(here), *[on_chip(a) for a in (far_ahead, far_behind, ahead, behind)])
+    )(at, row, *got, on_chip(halves))
     return pl.pallas_call(
         assemble_second_kernel,
         grid=(2,),

time: 152 us -> 139 us (0.914)
  waiting for transfers between devices: 31.7 us -> 21.8 us
  other arithmetic: 3.89 us -> 0.88 us
  Pallas kernels: 12.3 us -> 14.8 us
    ppermute x4, waiting for transfers between devices: 20.9 us -> 9.49 us  [sent(): lax.ppermute(array, 'y', [(j, (j + step) % ROWS) for j in range(ROWS)])]
    pallas_call x4 -> x8, Pallas kernels: 8.61 us -> 11.1 us  [the longest x1 2.93 us: program(): call(prepare_kernel, [pl.BlockSpec((1, 512, 512), lambda i, at: (1, 0, 0)...]
    ppermute x4, starting transfers between devices: 17.8 us -> 16.2 us  [swapped(): return lax.ppermute(array, 'c', [(0, 1), (1, 0)])]
    unnamed x22 -> x16, local copies, waits for them, and re-layouts: 3.82 us -> 2.87 us
  transfers between devices with their start and end apart: 11 -> 11, of which waited for: 6 -> 5; matrix products, arithmetic and copies ran while one was open for 2% -> 1% of each run, Pallas kernels for 4% -> 4%
where the time goes in v6:
time: 139 us; the launch traced here: 138 us
  starting transfers between devices  58.3 us (42%)
  blocking collectives  37.1 us (27%)
  waiting for transfers between devices  21.8 us (16%)
  Pallas kernels  14.8 us (11%)
  local copies, waits for them, and re-layouts  4.59 us (3%)
    all_to_all x2, blocking collectives, exchange(): return lax.all_to_all(array, axes, split_axis=0, concat_axis=0, tiled=True)  37.1 us
    all_to_all x3, starting transfers between devices, exchange(): return lax.all_to_all(array, axes, split_axis=0, concat_axis=0, tiled=True)  27.3 us
    ppermute x4, starting transfers between devices, swapped(): return lax.ppermute(array, 'c', [(0, 1), (1, 0)])  16.2 us
    ppermute x4, starting transfers between devices, sent(): lax.ppermute(array, 'y', [(j, (j + step) % ROWS) for j in range(ROWS)])  14.8 us
    all_to_all x3, waiting for transfers between devices, exchange(): return lax.all_to_all(array, axes, split_axis=0, concat_axis=0, tiled=True)  9.83 us
    ppermute x4, waiting for transfers between devices, sent(): lax.ppermute(array, 'y', [(j, (j + step) % ROWS) for j in range(ROWS)])  9.49 us
    pallas_call x1, Pallas kernels, program(): call(prepare_kernel, [pl.BlockSpec((1, 512, 512), lambda i, at: (1, 0, 0)...  2.93 us
    pallas_call x1, Pallas kernels, program(): call(first_kernel, [whole((3, 2, 256, 256)), pl.BlockSpec((1, 512, 512),...  2.91 us
  transfers between devices with their start and end apart: 11, of which 5 were waited for; matrix products, arithmetic and copies ran while one was open for 1% of the time, Pallas kernels for 4%

profile of v6, /device:TPU:1, one launch (start us, length us, event | category | flops | bytes accessed | tf_op | source)
XLA Modules:
  0.0 137.6 jit_solution(13599163319646577718)
XLA Ops:
  0.0 2.9 %shard_map.55 = (bf16[768,256]{1,0:T(8,128)(2,1)S(1)}, f32[768,256]{1,0:T(8,128)S(1)}) custom-call(s32[1]{0:T(128)} %bitcast.at.core_ref, bf16[3,2,256,256]{3,2,1,0:T(8,128)(2,1)} %init_ref.2, bf16[2,512,512]{2,1,0:T(8,128)(2,1)} %k_ref.2, bf16[2,512,512]{2,1,0:T(8,128)(2,1)} %v_ref.2, f32[3,2,2,512]{3,2,1,0:T(2,128)} %rates_ref.2), custom_call_target="tpu_custom_call" | custom-call | tf_op jit(solution)/shard_map/pallas_call | solution.py:242
  2.9 8.8 %collective-permute-start = (bf16[768,256]{1,0:T(8,128)(2,1)S(1)}, bf16[768,256]{1,0:T(8,128)(2,1)S(1)}, u32[]{:S(2)}, u32[]{:S(2)}) collective-permute-start(bf16[768,256]{1,0:T(8,128)(2,1)S(1)} %get-tuple-element.32), channel_id=1, source_target_pairs={{0,8},{8,0},{1,9},{9,1},{2,10},{10,2},{3,11},{11,3},{4,12},{12,4},... | collective-permute-start | bytes 1179656 | tf_op jit(solution)/shard_map/ppermute | solution.py:234
  11.7 1.3 collective-permute-done
  13.0 0.8 add_convert_fusion
  13.8 2.9 %shard_map.56 = (bf16[4,512,256]{2,1,0:T(8,128)(2,1)S(1)}, bf16[4,512,256]{2,1,0:T(8,128)(2,1)}, bf16[3,256,256]{2,1,0:T(8,128)(2,1)S(1)}, f32[3,512]{1,0:T(4,128)S(1)}, f32[3,512]{1,0:T(4,128)S(1)}) custom-call(s32[1]{0:T(128)} %bitcast.at.core_ref, bf16[2,512,512]{2,1,0:T(8,128)(2,1)} %k_ref.2, bf16[2,512,512]{2,1,0:T(8,128)(2,1)} %v_ref.2, ...), custom_call_target="tpu_custom_call" | custom-call | tf_op jit(solution)/shard_map/pallas_call | solution.py:259
  16.8 2.3 %collective-permute-start.1 = (bf16[4,512,256]{2,1,0:T(8,128)(2,1)}, bf16[4,512,256]{2,1,0:T(8,128)(2,1)S(1)}, u32[]{:S(2)}, u32[]{:S(2)}) collective-permute-start(bf16[4,512,256]{2,1,0:T(8,128)(2,1)} %get-tuple-element.39), channel_id=1, source_target_pairs={{0,8},{8,0},{1,9},{9,1},{2,10},{10,2},{3,11},{11,3},{4,12},{12,4},... | collective-permute-start | bytes 3145736 | tf_op jit(solution)/shard_map/ppermute | solution.py:234
  19.1 7.6 %all-to-all-start = ((bf16[32,24,256]{2,1,0:T(8,128)(2,1)}), bf16[32,24,256]{2,1,0:T(8,128)(2,1)S(1)}, u32[]{:S(2)}, u32[]{:S(2)}) async-start(bf16[32,24,256]{2,1,0:T(8,128)(2,1)} %bitcast.1), calls=%async_computation | async-start | bytes 786432 | tf_op jit(solution)/shard_map/all_to_all | solution.py:213
  26.6 2.3 %collective-permute-start.2 = (f32[3,512]{1,0:T(4,128)S(1)}, f32[3,512]{1,0:T(4,128)S(1)}, u32[]{:S(2)}, u32[]{:S(2)}) collective-permute-start(f32[3,512]{1,0:T(4,128)S(1)} %get-tuple-element.40), channel_id=1, source_target_pairs={{0,8},{8,0},{1,9},{9,1},{2,10},{10,2},{3,11},{11,3},{4,12},{12,4},... | collective-permute-start | bytes 18440 | tf_op jit(solution)/shard_map/ppermute | solution.py:234
  28.9 9.8 %all-to-all-done.parts_ref = bf16[32,24,256]{2,1,0:T(8,128)(2,1)S(1)} async-done(((bf16[32,24,256]{2,1,0:T(8,128)(2,1)}), bf16[32,24,256]{2,1,0:T(8,128)(2,1)S(1)}, u32[]{:S(2)}, u32[]{:S(2)}) %all-to-all-start) | async-done | bytes 393248 | tf_op jit(solution)/shard_map/all_to_all | solution.py:213
  38.8 0.1 total.2
  38.9 0.0 collective-permute-done.2.rates_other_ref
  38.9 0.0 copy-start.4
  38.9 0.0 collective-permute-done.1.other_ref
  38.9 18.8 %all_to_all.25 = bf16[32,24,256]{2,1,0:T(8,128)(2,1)S(1)} all-to-all(bf16[32,24,256]{2,1,0:T(8,128)(2,1)S(1)} %total.2), channel_id=1, replica_groups=mesh['x'=4,'z'=8,'c'=2,'y'=8] {'x','z'}, dimensions={0} | all-to-all | bytes 786432 | tf_op jit(solution)/shard_map/all_to_all | solution.py:213
  57.7 0.0 copy-done.4
  57.7 0.7 copy-done.5
  58.4 2.5 %second.1 = (bf16[768,256]{1,0:T(8,128)(2,1)}, f32[1032,256]{1,0:T(8,128)S(1)}) custom-call(bf16[3,256,256]{2,1,0:T(8,128)(2,1)S(1)} %get-tuple-element.44.init_ref, bf16[768,256]{1,0:T(8,128)(2,1)S(1)} %bitcast.9, bf16[4,512,256]{2,1,0:T(8,128)(2,1)S(1)} %get-tuple-element.46.own_ref, bf16[4,512,256]{2,1,0:T(8,128)(2,1)S(1)} %collective-permute-done.1.other_ref, ...), custom_call_target="tpu_custom_call" | custom-call | tf_op jit(solution)/shard_map/second/pallas_call | solution.py:278
  60.9 18.3 %all_to_all.26.parts_ref = bf16[32,24,256]{2,1,0:T(8,128)(2,1)S(1)} all-to-all(bf16[32,24,256]{2,1,0:T(8,128)(2,1)} %bitcast.10), channel_id=1, replica_groups=mesh['x'=4,'z'=8,'c'=2,'y'=8] {'x','z'}, dimensions={0} | all-to-all | bytes 786432 | tf_op jit(solution)/shard_map/all_to_all | solution.py:213
  79.2 0.1 total.3
  79.2 0.0 copy-start.1
  79.3 0.7 copy-done.1
  80.0 7.6 %all-to-all-start.3 = ((bf16[32,24,256]{2,1,0:T(8,128)(2,1)}), bf16[32,24,256]{2,1,0:T(8,128)(2,1)S(1)}, u32[]{:S(2)}, u32[]{:S(2)}) async-start(bf16[32,24,256]{2,1,0:T(8,128)(2,1)} %copy-done.1), calls=%async_computation.3 | async-start | bytes 786432 | tf_op jit(solution)/shard_map/all_to_all | solution.py:213
  87.6 1.5 %apply_first.1 = (bf16[3,2,64,256]{3,2,1,0:T(8,128)(2,1)}, bf16[2,2,64,256]{3,2,1,0:T(8,128)(2,1)}, bf16[1,2,64,256]{3,2,1,0:T(8,128)(2,1)}, bf16[1,2,64,256]{3,2,1,0:T(8,128)(2,1)}, bf16[1,2,64,256]{3,2,1,0:T(8,128)(2,1)S(1)}) custom-call(s32[1]{0:T(128)} %bitcast.6.row_ref, f32[1032,256]{1,0:T(8,128)S(1)} %get-tuple-element.50.kept_ref, ...), custom_call_target="tpu_custom_call" | custom-call | tf_op jit(solution)/shard_map/apply_first/pallas_call | solution.py:290
  89.1 0.6 copy-done.2
  89.7 5.2 %collective-permute-start.3 = (bf16[3,2,64,256]{3,2,1,0:T(8,128)(2,1)}, bf16[3,2,64,256]{3,2,1,0:T(8,128)(2,1)}, u32[]{:S(2)}, u32[]{:S(2)}) collective-permute-start(bf16[3,2,64,256]{3,2,1,0:T(8,128)(2,1)} %get-tuple-element.53), channel_id=1, source_target_pairs={{0,3},{1,4},{2,5},{3,6},{4,7},{5,0},{6,1},{7,2},{8,11},{9,12},{10,... | collective-permute-start | bytes 589832 | tf_op jit(solution)/shard_map/ppermute | solution.py:304
  94.9 3.2 %collective-permute-start.4 = (bf16[2,2,64,256]{3,2,1,0:T(8,128)(2,1)}, bf16[2,2,64,256]{3,2,1,0:T(8,128)(2,1)}, u32[]{:S(2)}, u32[]{:S(2)}) collective-permute-start(bf16[2,2,64,256]{3,2,1,0:T(8,128)(2,1)} %get-tuple-element.54), channel_id=1, source_target_pairs={{0,6},{1,7},{2,0},{3,1},{4,2},{5,3},{6,4},{7,5},{8,14},{9,15},{10,... | collective-permute-start | bytes 393224 | tf_op jit(solution)/shard_map/ppermute | solution.py:304
  98.1 0.0 all-to-all-done.3
  98.1 1.1 shard_map.57
  99.2 0.0 copy-start
  99.2 0.8 copy-done
  100.0 12.1 %all-to-all-start.4 = ((bf16[16,64,256]{2,1,0:T(8,128)(2,1)}), bf16[16,64,256]{2,1,0:T(8,128)(2,1)S(1)}, u32[]{:S(2)}, u32[]{:S(2)}) async-start(bf16[16,64,256]{2,1,0:T(8,128)(2,1)} %bitcast.7), calls=%async_computation.4 | async-start | bytes 1048576 | tf_op jit(solution)/shard_map/all_to_all | solution.py:213
  112.2 0.0 collective-permute-done.4.refs_2_
  112.2 0.8 slice.14
  113.0 0.0 collective-permute-done.3.refs_1_
  113.0 0.9 fusion
  113.9 0.0 copy-done.7
  114.0 4.5 %collective-permute-start.6 = (bf16[3,2,64,256]{3,2,1,0:T(8,128)(2,1)S(1)}, bf16[3,2,64,256]{3,2,1,0:T(8,128)(2,1)S(1)}, u32[]{:S(2)}, u32[]{:S(2)}) collective-permute-start(bf16[3,2,64,256]{3,2,1,0:T(8,128)(2,1)S(1)} %pad_maximum_fusion), channel_id=1, source_target_pairs={{0,7},{1,0},{2,1},{3,2},{4,3},{5,4},{6,5},{7,6},{8,15},{9,8},{10,9... | collective-permute-start | bytes 589832 | tf_op jit(solution)/shard_map/ppermute | solution.py:304
  118.4 0.0 copy-done.6
  118.5 1.9 %collective-permute-start.5 = (bf16[2,2,64,256]{3,2,1,0:T(8,128)(2,1)S(1)}, bf16[2,2,64,256]{3,2,1,0:T(8,128)(2,1)S(1)}, u32[]{:S(2)}, u32[]{:S(2)}) collective-permute-start(bf16[2,2,64,256]{3,2,1,0:T(8,128)(2,1)S(1)} %pad_maximum_fusion.1), channel_id=1, source_target_pairs={{0,1},{1,2},{2,3},{3,4},{4,5},{5,6},{6,7},{7,0},{8,9},{9,10},{10,1... | collective-permute-start | bytes 393224 | tf_op jit(solution)/shard_map/ppermute | solution.py:304
  120.4 9.2 %collective-permute-done.5.refs_3_ = bf16[2,2,64,256]{3,2,1,0:T(8,128)(2,1)S(1)} collective-permute-done((bf16[2,2,64,256]{3,2,1,0:T(8,128)(2,1)S(1)}, bf16[2,2,64,256]{3,2,1,0:T(8,128)(2,1)S(1)}, u32[]{:S(2)}, u32[]{:S(2)}) %collective-permute-start.5) | collective-permute-done | bytes 131104 | tf_op jit(solution)/shard_map/ppermute | solution.py:304
  129.6 0.3 collective-permute-done.6.refs_4_
  129.9 0.0 copy-done.3
  129.9 1.0 collect.1
  130.9 2.9 %collective-permute-start.7 = (bf16[8,64,256]{2,1,0:T(8,128)(2,1)S(1)}, bf16[8,64,256]{2,1,0:T(8,128)(2,1)S(1)}, u32[]{:S(2)}, u32[]{:S(2)}) collective-permute-start(bf16[8,64,256]{2,1,0:T(8,128)(2,1)S(1)} %collect.1), channel_id=1, source_target_pairs={{0,8},{8,0},{1,9},{9,1},{2,10},{10,2},{3,11},{11,3},{4,12},{12,4},... | collective-permute-start | bytes 786440 | tf_op jit(solution)/shard_map/ppermute | solution.py:234
  133.8 1.1 collective-permute-done.7.refs_5_
  134.9 1.8 %assemble_first.1.prev_ref = bf16[2,64,4096]{2,1,0:T(8,128)(2,1)} custom-call(s32[1]{0:T(128)} %bitcast.at.core_ref, s32[1]{0:T(128)} %bitcast.6.row_ref, bf16[1,2,64,256]{3,2,1,0:T(8,128)(2,1)S(1)} %copy-done.3, bf16[3,2,64,256]{3,2,1,0:T(8,128)(2,1)} %collective-permute-done.3.refs_1_, bf16[2,2,64,256]{3,2,1,0:T(8,128)(2,1)} %collective-permute-done.4.refs_2_, ...), custom_call_target="tpu_custom_call" | custom-call | tf_op jit(solution)/shard_map/assemble_first/pallas_call | solution.py:327
  136.8 0.0 all-to-all-done.4.parts_ref
  136.8 0.8 assemble_second.1
  (7 shorter events, 0.0 us)
Async XLA Ops:
  2.9 10.1 %collective-permute-start = (bf16[768,256]{1,0:T(8,128)(2,1)S(1)}, bf16[768,256]{1,0:T(8,128)(2,1)S(1)}, u32[]{:S(2)}, u32[]{:S(2)}) collective-permute-start(bf16[768,256]{1,0:T(8,128)(2,1)S(1)} %get-tuple-element.32), channel_id=1, source_target_pairs={{0,8},{8,0},{1,9},{9,1},{2,10},{10,2},{3,11},{11,3},{4,12},{12,4},... | collective-permute-start | bytes 1179656 | tf_op jit(solution)/shard_map/ppermute | solution.py:234
  16.8 22.1 %collective-permute-start.1 = (bf16[4,512,256]{2,1,0:T(8,128)(2,1)}, bf16[4,512,256]{2,1,0:T(8,128)(2,1)S(1)}, u32[]{:S(2)}, u32[]{:S(2)}) collective-permute-start(bf16[4,512,256]{2,1,0:T(8,128)(2,1)} %get-tuple-element.39), channel_id=1, source_target_pairs={{0,8},{8,0},{1,9},{9,1},{2,10},{10,2},{3,11},{11,3},{4,12},{12,4},... | collective-permute-start | bytes 3145736 | tf_op jit(solution)/shard_map/ppermute | solution.py:234
  19.1 19.7 %all-to-all-start = ((bf16[32,24,256]{2,1,0:T(8,128)(2,1)}), bf16[32,24,256]{2,1,0:T(8,128)(2,1)S(1)}, u32[]{:S(2)}, u32[]{:S(2)}) async-start(bf16[32,24,256]{2,1,0:T(8,128)(2,1)} %bitcast.1), calls=%async_computation | async-start | bytes 786432 | tf_op jit(solution)/shard_map/all_to_all | solution.py:213
  26.6 12.2 %collective-permute-start.2 = (f32[3,512]{1,0:T(4,128)S(1)}, f32[3,512]{1,0:T(4,128)S(1)}, u32[]{:S(2)}, u32[]{:S(2)}) collective-permute-start(f32[3,512]{1,0:T(4,128)S(1)} %get-tuple-element.40), channel_id=1, source_target_pairs={{0,8},{8,0},{1,9},{9,1},{2,10},{10,2},{3,11},{11,3},{4,12},{12,4},... | collective-permute-start | bytes 18440 | tf_op jit(solution)/shard_map/ppermute | solution.py:234
  38.9 18.8 %copy-start.4 = (f32[3,512]{1,0:T(4,128)}, f32[3,512]{1,0:T(4,128)S(1)}, u32[]{:S(2)}) copy-start(f32[3,512]{1,0:T(4,128)S(1)} %collective-permute-done.2.rates_other_ref) | copy-start | bytes 18436
  57.7 0.7 copy-start.5
  79.2 0.7 copy-start.1
  80.0 18.1 %all-to-all-start.3 = ((bf16[32,24,256]{2,1,0:T(8,128)(2,1)}), bf16[32,24,256]{2,1,0:T(8,128)(2,1)S(1)}, u32[]{:S(2)}, u32[]{:S(2)}) async-start(bf16[32,24,256]{2,1,0:T(8,128)(2,1)} %copy-done.1), calls=%async_computation.3 | async-start | bytes 786432 | tf_op jit(solution)/shard_map/all_to_all | solution.py:213
  89.1 0.6 copy-start.2
  89.7 23.3 %collective-permute-start.3 = (bf16[3,2,64,256]{3,2,1,0:T(8,128)(2,1)}, bf16[3,2,64,256]{3,2,1,0:T(8,128)(2,1)}, u32[]{:S(2)}, u32[]{:S(2)}) collective-permute-start(bf16[3,2,64,256]{3,2,1,0:T(8,128)(2,1)} %get-tuple-element.53), channel_id=1, source_target_pairs={{0,3},{1,4},{2,5},{3,6},{4,7},{5,0},{6,1},{7,2},{8,11},{9,12},{10,... | collective-permute-start | bytes 589832 | tf_op jit(solution)/shard_map/ppermute | solution.py:304
  94.9 17.2 %collective-permute-start.4 = (bf16[2,2,64,256]{3,2,1,0:T(8,128)(2,1)}, bf16[2,2,64,256]{3,2,1,0:T(8,128)(2,1)}, u32[]{:S(2)}, u32[]{:S(2)}) collective-permute-start(bf16[2,2,64,256]{3,2,1,0:T(8,128)(2,1)} %get-tuple-element.54), channel_id=1, source_target_pairs={{0,6},{1,7},{2,0},{3,1},{4,2},{5,3},{6,4},{7,5},{8,14},{9,15},{10,... | collective-permute-start | bytes 393224 | tf_op jit(solution)/shard_map/ppermute | solution.py:304
  99.2 0.8 copy-start
  100.0 13.9 %copy-start.7 = (bf16[1,2,64,256]{3,2,1,0:T(8,128)(2,1)S(1)}, bf16[1,2,64,256]{3,2,1,0:T(8,128)(2,1)}, u32[]{:S(2)}) copy-start(bf16[1,2,64,256]{3,2,1,0:T(8,128)(2,1)} %get-tuple-element.56) | copy-start | bytes 196612
  100.0 18.4 %copy-start.6 = (bf16[1,2,64,256]{3,2,1,0:T(8,128)(2,1)S(1)}, bf16[1,2,64,256]{3,2,1,0:T(8,128)(2,1)}, u32[]{:S(2)}) copy-start(bf16[1,2,64,256]{3,2,1,0:T(8,128)(2,1)} %get-tuple-element.55) | copy-start | bytes 196612
  100.0 29.9 %copy-start.3 = (bf16[1,2,64,256]{3,2,1,0:T(8,128)(2,1)S(1)}, bf16[1,2,64,256]{3,2,1,0:T(8,128)(2,1)}, u32[]{:S(2)}) copy-start(bf16[1,2,64,256]{3,2,1,0:T(8,128)(2,1)} %copy-done.2) | copy-start | bytes 196612
  100.0 36.7 %all-to-all-start.4 = ((bf16[16,64,256]{2,1,0:T(8,128)(2,1)}), bf16[16,64,256]{2,1,0:T(8,128)(2,1)S(1)}, u32[]{:S(2)}, u32[]{:S(2)}) async-start(bf16[16,64,256]{2,1,0:T(8,128)(2,1)} %bitcast.7), calls=%async_computation.4 | async-start | bytes 1048576 | tf_op jit(solution)/shard_map/all_to_all | solution.py:213
  114.0 15.9 %collective-permute-start.6 = (bf16[3,2,64,256]{3,2,1,0:T(8,128)(2,1)S(1)}, bf16[3,2,64,256]{3,2,1,0:T(8,128)(2,1)S(1)}, u32[]{:S(2)}, u32[]{:S(2)}) collective-permute-start(bf16[3,2,64,256]{3,2,1,0:T(8,128)(2,1)S(1)} %pad_maximum_fusion), channel_id=1, source_target_pairs={{0,7},{1,0},{2,1},{3,2},{4,3},{5,4},{6,5},{7,6},{8,15},{9,8},{10,9... | collective-permute-start | bytes 589832 | tf_op jit(solution)/shard_map/ppermute | solution.py:304
  118.5 11.1 %collective-permute-start.5 = (bf16[2,2,64,256]{3,2,1,0:T(8,128)(2,1)S(1)}, bf16[2,2,64,256]{3,2,1,0:T(8,128)(2,1)S(1)}, u32[]{:S(2)}, u32[]{:S(2)}) collective-permute-start(bf16[2,2,64,256]{3,2,1,0:T(8,128)(2,1)S(1)} %pad_maximum_fusion.1), channel_id=1, source_target_pairs={{0,1},{1,2},{2,3},{3,4},{4,5},{5,6},{6,7},{7,0},{8,9},{9,10},{10,1... | collective-permute-start | bytes 393224 | tf_op jit(solution)/shard_map/ppermute | solution.py:304
  130.9 4.0 %collective-permute-start.7 = (bf16[8,64,256]{2,1,0:T(8,128)(2,1)S(1)}, bf16[8,64,256]{2,1,0:T(8,128)(2,1)S(1)}, u32[]{:S(2)}, u32[]{:S(2)}) collective-permute-start(bf16[8,64,256]{2,1,0:T(8,128)(2,1)S(1)} %collect.1), channel_id=1, source_target_pairs={{0,8},{8,0},{1,9},{9,1},{2,10},{10,2},{3,11},{11,3},{4,12},{12,4},... | collective-permute-start | bytes 786440 | tf_op jit(solution)/shard_map/ppermute | solution.py:234

commit v7 on v6

--- a/solution.py
+++ b/solution.py
@@ -141,6 +141,14 @@
     out_ref[...] = jnp.broadcast_to(total.astype(bf16), out_ref.shape)
 
 
+def pack_kernel(ahead_own_ref, behind_own_ref, far_ahead_ref, far_behind_ref, ahead_ref, behind_ref):
+    ahead_ref[0] = ahead_own_ref[0]
+    ahead_ref[1] = far_ahead_ref[2]
+    behind_ref[0] = behind_own_ref[0]
+    behind_ref[1] = far_ahead_ref[0]
+    behind_ref[2] = far_behind_ref[0]
+
+
 def pieces_of(here_ref, far_ahead_ref, far_behind_ref, ahead_ref, behind_ref, side):
     return (
         here_ref[0, side],
@@ -213,13 +221,13 @@
     return lax.all_to_all(array, axes, split_axis=0, concat_axis=0, tiled=True)
 
 
-def scattered(partial):
+def scattered(partial, block):
     parts = exchange(partial.reshape(32, 24, 256), ("x", "z"))
     return pl.pallas_call(
         total_kernel,
         in_specs=[VMEM],
         out_specs=VMEM,
-        out_shape=jax.ShapeDtypeStruct((32, 24, 256), bf16),
+        out_shape=(pltpu.HBM if block else jax.ShapeDtypeStruct)((32, 24, 256), bf16),
         name="total",
         compiler_params=LIMIT,
     )(on_chip(parts))
@@ -270,7 +278,7 @@
     other = swapped(other)
     rates_other = swapped(rates_other)
 
-    total = scattered(first)
+    total = scattered(first, 0)
     total, other, rates_other, own, rates_own, init = lax.optimization_barrier(
         (total, other, rates_other, own, rates_own, init)
     )
@@ -292,7 +300,7 @@
         in_specs=[SCALARS, VMEM, VMEM, VMEM],
         out_specs=[VMEM] * len(FIRST_LEVEL),
         out_shape=[
-            (pltpu.HBM if d in ((1,), (-1,)) else jax.ShapeDtypeStruct)((len(d), 2, 64, 256), bf16)
+            (pltpu.HBM if len(d) == 1 else jax.ShapeDtypeStruct)((len(d), 2, 64, 256), bf16)
             for d in FIRST_LEVEL
         ],
         scratch_shapes=[pltpu.VMEM((ROWS, 2, 64, 256), bf16)],
@@ -305,16 +313,24 @@
 
     far_ahead = sent(far_ahead, 3)
     far_behind = sent(far_behind, -2)
-    ahead = sent(jnp.concatenate([ahead, far_ahead[2:]]), 1)
-    behind = sent(jnp.concatenate([behind, far_ahead[:1], far_behind[:1]]), -1)
-
-    total = scattered(second)
+    ahead, behind = pl.pallas_call(
+        pack_kernel,
+        in_specs=[VMEM] * 4,
+        out_specs=[VMEM] * 2,
+        out_shape=[pltpu.HBM((n, 2, 64, 256), bf16) for n in (2, 3)],
+        name="pack",
+        compiler_params=LIMIT,
+    )(*[off_chip(a) for a in (ahead, behind)], *[on_chip(a) for a in (far_ahead, far_behind)])
+    ahead = sent(ahead, 1)
+    behind = sent(behind, -1)
+
+    total = scattered(second, 1)
     summed = gathered(total)
     result = call(
         last_kernel, [VMEM, VMEM, VMEM, VMEM], [((ROWS, 2, 64, 256), bf16)]
     )(at, on_chip(kept), summed, on_chip(own), on_chip(other))
     parts = exchange(result.reshape(16, 64, 256), ("y", "c"))
-    got = [on_chip(a) for a in (here, far_ahead, far_behind, ahead, behind)]
+    got = [off_chip(here)] + [on_chip(a) for a in (far_ahead, far_behind, ahead, behind)]
     halves = pl.pallas_call(
         collect_kernel,
         in_specs=[VMEM] * 5,

time: 139 us -> 163 us (1.17)
  blocking collectives: 37.1 us -> 55.2 us
  waiting for transfers between devices: 21.8 us -> 35.1 us
  starting transfers between devices: 58.3 us -> 51.2 us
  local copies, waits for them, and re-layouts: 4.59 us -> 1.49 us
  Pallas kernels: 14.8 us -> 17.7 us
    all_to_all x2 -> x3, blocking collectives: 37.1 us -> 55.2 us  [exchange(): return lax.all_to_all(array, axes, split_axis=0, concat_axis=0, tiled=True)]
    ppermute x4, waiting for transfers between devices: 9.49 us -> 22.8 us  [sent(): lax.ppermute(array, 'y', [(j, (j + step) % ROWS) for j in range(ROWS)])]
    all_to_all x3 -> x2, starting transfers between devices: 27.3 us -> 19.6 us  [exchange(): return lax.all_to_all(array, axes, split_axis=0, concat_axis=0, tiled=True)]
    pallas_call x2 -> x3, Pallas kernels: 0.15 us -> 2.5 us  [the longest x1 1.6 us: program(): pl.pallas_call(pack_kernel, in_specs=[VMEM] * 4, out_specs=[VMEM] * 2, ou...]
    slice x2 -> x0, local copies, waits for them, and re-layouts: 1.73 us -> none  [program(): behind = sent(jnp.concatenate([behind, far_ahead[:1], far_behind[:1]]), -1)]
    ppermute x4, starting transfers between devices: 16.2 us -> 17.9 us  [swapped(): return lax.ppermute(array, 'c', [(0, 1), (1, 0)])]
    all_to_all x3 -> x2, waiting for transfers between devices: 9.83 us -> 9.83 us  [exchange(): return lax.all_to_all(array, axes, split_axis=0, concat_axis=0, tiled=True)]
  transfers between devices with their start and end apart: 11 -> 10, of which waited for: 5 -> 6; matrix products, arithmetic and copies ran while one was open for 1% -> 0% of each run, Pallas kernels for 4% -> 3%
where the time goes in v7:
time: 163 us; the launch traced here: 162 us
  blocking collectives  55.2 us (34%)
  starting transfers between devices  51.2 us (31%)
  waiting for transfers between devices  35.1 us (22%)
  Pallas kernels  17.7 us (11%)
    all_to_all x3, blocking collectives, exchange(): return lax.all_to_all(array, axes, split_axis=0, concat_axis=0, tiled=True)  55.2 us
    ppermute x4, waiting for transfers between devices, sent(): lax.ppermute(array, 'y', [(j, (j + step) % ROWS) for j in range(ROWS)])  22.8 us
    all_to_all x2, starting transfers between devices, exchange(): return lax.all_to_all(array, axes, split_axis=0, concat_axis=0, tiled=True)  19.6 us
    ppermute x4, starting transfers between devices, swapped(): return lax.ppermute(array, 'c', [(0, 1), (1, 0)])  17.9 us
    ppermute x4, starting transfers between devices, sent(): lax.ppermute(array, 'y', [(j, (j + step) % ROWS) for j in range(ROWS)])  13.7 us
    all_to_all x2, waiting for transfers between devices, exchange(): return lax.all_to_all(array, axes, split_axis=0, concat_axis=0, tiled=True)  9.83 us
  transfers between devices with their start and end apart: 10, of which 6 were waited for; matrix products, arithmetic and copies ran while one was open for 0% of the time, Pallas kernels for 3%

profile of v7, /device:TPU:1, one launch (start us, length us, event | category | flops | bytes accessed | tf_op | source)
XLA Modules:
  0.0 161.6 jit_solution(16232631760326698852)
XLA Ops:
  0.0 2.9 %shard_map.55 = (bf16[768,256]{1,0:T(8,128)(2,1)S(1)}, f32[768,256]{1,0:T(8,128)S(1)}) custom-call(s32[1]{0:T(128)} %bitcast.at.core_ref, bf16[3,2,256,256]{3,2,1,0:T(8,128)(2,1)} %init_ref.2, bf16[2,512,512]{2,1,0:T(8,128)(2,1)} %k_ref.2, bf16[2,512,512]{2,1,0:T(8,128)(2,1)} %v_ref.2, f32[3,2,2,512]{3,2,1,0:T(2,128)} %rates_ref.2), custom_call_target="tpu_custom_call" | custom-call | tf_op jit(solution)/shard_map/pallas_call | solution.py:250
  2.9 8.8 %collective-permute-start = (bf16[768,256]{1,0:T(8,128)(2,1)S(1)}, bf16[768,256]{1,0:T(8,128)(2,1)S(1)}, u32[]{:S(2)}, u32[]{:S(2)}) collective-permute-start(bf16[768,256]{1,0:T(8,128)(2,1)S(1)} %get-tuple-element.34), channel_id=1, source_target_pairs={{0,8},{8,0},{1,9},{9,1},{2,10},{10,2},{3,11},{11,3},{4,12},{12,4},... | collective-permute-start | bytes 1179656 | tf_op jit(solution)/shard_map/ppermute | solution.py:242
  11.7 1.3 collective-permute-done
  13.0 0.8 add_convert_fusion
  13.8 2.9 %shard_map.56 = (bf16[4,512,256]{2,1,0:T(8,128)(2,1)S(1)}, bf16[4,512,256]{2,1,0:T(8,128)(2,1)}, bf16[3,256,256]{2,1,0:T(8,128)(2,1)S(1)}, f32[3,512]{1,0:T(4,128)S(1)}, f32[3,512]{1,0:T(4,128)S(1)}) custom-call(s32[1]{0:T(128)} %bitcast.at.core_ref, bf16[2,512,512]{2,1,0:T(8,128)(2,1)} %k_ref.2, bf16[2,512,512]{2,1,0:T(8,128)(2,1)} %v_ref.2, ...), custom_call_target="tpu_custom_call" | custom-call | tf_op jit(solution)/shard_map/pallas_call | solution.py:267
  16.8 2.3 %collective-permute-start.1 = (bf16[4,512,256]{2,1,0:T(8,128)(2,1)}, bf16[4,512,256]{2,1,0:T(8,128)(2,1)S(1)}, u32[]{:S(2)}, u32[]{:S(2)}) collective-permute-start(bf16[4,512,256]{2,1,0:T(8,128)(2,1)} %get-tuple-element.41), channel_id=1, source_target_pairs={{0,8},{8,0},{1,9},{9,1},{2,10},{10,2},{3,11},{11,3},{4,12},{12,4},... | collective-permute-start | bytes 3145736 | tf_op jit(solution)/shard_map/ppermute | solution.py:242
  19.1 7.6 %all-to-all-start = ((bf16[32,24,256]{2,1,0:T(8,128)(2,1)}), bf16[32,24,256]{2,1,0:T(8,128)(2,1)S(1)}, u32[]{:S(2)}, u32[]{:S(2)}) async-start(bf16[32,24,256]{2,1,0:T(8,128)(2,1)} %bitcast.1), calls=%async_computation | async-start | bytes 786432 | tf_op jit(solution)/shard_map/all_to_all | solution.py:221
  26.6 2.3 %collective-permute-start.2 = (f32[3,512]{1,0:T(4,128)S(1)}, f32[3,512]{1,0:T(4,128)S(1)}, u32[]{:S(2)}, u32[]{:S(2)}) collective-permute-start(f32[3,512]{1,0:T(4,128)S(1)} %get-tuple-element.42), channel_id=1, source_target_pairs={{0,8},{8,0},{1,9},{9,1},{2,10},{10,2},{3,11},{11,3},{4,12},{12,4},... | collective-permute-start | bytes 18440 | tf_op jit(solution)/shard_map/ppermute | solution.py:242
  28.9 9.8 %all-to-all-done.parts_ref = bf16[32,24,256]{2,1,0:T(8,128)(2,1)S(1)} async-done(((bf16[32,24,256]{2,1,0:T(8,128)(2,1)}), bf16[32,24,256]{2,1,0:T(8,128)(2,1)S(1)}, u32[]{:S(2)}, u32[]{:S(2)}) %all-to-all-start) | async-done | bytes 393248 | tf_op jit(solution)/shard_map/all_to_all | solution.py:221
  38.8 0.1 total.2
  38.9 0.0 collective-permute-done.2.rates_other_ref
  38.9 0.0 copy-start.1
  38.9 0.0 collective-permute-done.1.other_ref
  38.9 18.8 %all_to_all.25 = bf16[32,24,256]{2,1,0:T(8,128)(2,1)S(1)} all-to-all(bf16[32,24,256]{2,1,0:T(8,128)(2,1)S(1)} %total.2), channel_id=1, replica_groups=mesh['x'=4,'z'=8,'c'=2,'y'=8] {'x','z'}, dimensions={0} | all-to-all | bytes 786432 | tf_op jit(solution)/shard_map/all_to_all | solution.py:221
  57.7 0.0 copy-done.1
  57.7 0.0 copy-start.2
  57.7 0.7 copy-done.2
  58.4 2.5 %second.1 = (bf16[768,256]{1,0:T(8,128)(2,1)}, f32[1032,256]{1,0:T(8,128)S(1)}) custom-call(bf16[3,256,256]{2,1,0:T(8,128)(2,1)S(1)} %get-tuple-element.46.init_ref, bf16[768,256]{1,0:T(8,128)(2,1)S(1)} %bitcast.9, bf16[4,512,256]{2,1,0:T(8,128)(2,1)S(1)} %get-tuple-element.48.own_ref, bf16[4,512,256]{2,1,0:T(8,128)(2,1)S(1)} %collective-permute-done.1.other_ref, ...), custom_call_target="tpu_custom_call" | custom-call | tf_op jit(solution)/shard_map/second/pallas_call | solution.py:286
  60.9 18.3 %all_to_all.26.parts_ref = bf16[32,24,256]{2,1,0:T(8,128)(2,1)S(1)} all-to-all(bf16[32,24,256]{2,1,0:T(8,128)(2,1)} %bitcast.10), channel_id=1, replica_groups=mesh['x'=4,'z'=8,'c'=2,'y'=8] {'x','z'}, dimensions={0} | all-to-all | bytes 786432 | tf_op jit(solution)/shard_map/all_to_all | solution.py:221
  79.2 0.8 total.3
  80.0 18.1 %all_to_all.27 = bf16[32,24,256]{2,1,0:T(8,128)(2,1)S(1)} all-to-all(bf16[32,24,256]{2,1,0:T(8,128)(2,1)} %total.3), channel_id=1, replica_groups=mesh['x'=4,'z'=8,'c'=2,'y'=8] {'x','z'}, dimensions={0} | all-to-all | bytes 786432 | tf_op jit(solution)/shard_map/all_to_all | solution.py:221
  98.1 1.1 shard_map.57
  99.2 0.0 copy-start
  99.2 0.8 copy-done
  100.0 12.1 %all-to-all-start.4 = ((bf16[16,64,256]{2,1,0:T(8,128)(2,1)}), bf16[16,64,256]{2,1,0:T(8,128)(2,1)}, u32[]{:S(2)}, u32[]{:S(2)}) async-start(bf16[16,64,256]{2,1,0:T(8,128)(2,1)} %bitcast.7), calls=%async_computation.4 | async-start | bytes 1048576 | tf_op jit(solution)/shard_map/all_to_all | solution.py:221
  112.0 1.4 apply_first.1
  113.5 5.0 %collective-permute-start.3 = (bf16[3,2,64,256]{3,2,1,0:T(8,128)(2,1)S(1)}, bf16[3,2,64,256]{3,2,1,0:T(8,128)(2,1)S(1)}, u32[]{:S(2)}, u32[]{:S(2)}) collective-permute-start(bf16[3,2,64,256]{3,2,1,0:T(8,128)(2,1)S(1)} %get-tuple-element.55), channel_id=1, source_target_pairs={{0,3},{1,4},{2,5},{3,6},{4,7},{5,0},{6,1},{7,2},{8,11},{9,12},{10,... | collective-permute-start | bytes 589832 | tf_op jit(solution)/shard_map/ppermute | solution.py:312
  118.5 3.4 %collective-permute-start.4 = (bf16[2,2,64,256]{3,2,1,0:T(8,128)(2,1)S(1)}, bf16[2,2,64,256]{3,2,1,0:T(8,128)(2,1)S(1)}, u32[]{:S(2)}, u32[]{:S(2)}) collective-permute-start(bf16[2,2,64,256]{3,2,1,0:T(8,128)(2,1)S(1)} %get-tuple-element.56), channel_id=1, source_target_pairs={{0,6},{1,7},{2,0},{3,1},{4,2},{5,3},{6,4},{7,5},{8,14},{9,15},{10,... | collective-permute-start | bytes 393224 | tf_op jit(solution)/shard_map/ppermute | solution.py:312
  121.9 9.6 %collective-permute-done.4.far_behind_ref.refs_2_ = bf16[2,2,64,256]{3,2,1,0:T(8,128)(2,1)S(1)} collective-permute-done((bf16[2,2,64,256]{3,2,1,0:T(8,128)(2,1)S(1)}, bf16[2,2,64,256]{3,2,1,0:T(8,128)(2,1)S(1)}, u32[]{:S(2)}, u32[]{:S(2)}) %collective-permute-start.4) | collective-permute-done | bytes 131104 | tf_op jit(solution)/shard_map/ppermute | solution.py:312
  131.5 9.4 %collective-permute-done.3.far_ahead_ref.refs_1_ = bf16[3,2,64,256]{3,2,1,0:T(8,128)(2,1)S(1)} collective-permute-done((bf16[3,2,64,256]{3,2,1,0:T(8,128)(2,1)S(1)}, bf16[3,2,64,256]{3,2,1,0:T(8,128)(2,1)S(1)}, u32[]{:S(2)}, u32[]{:S(2)}) %collective-permute-start.3) | collective-permute-done | bytes 196640 | tf_op jit(solution)/shard_map/ppermute | solution.py:312
  140.9 1.6 pack.1
  142.5 1.9 %collective-permute-start.6 = (bf16[3,2,64,256]{3,2,1,0:T(8,128)(2,1)}, bf16[3,2,64,256]{3,2,1,0:T(8,128)(2,1)S(1)}, u32[]{:S(2)}, u32[]{:S(2)}) collective-permute-start(bf16[3,2,64,256]{3,2,1,0:T(8,128)(2,1)} %get-tuple-element.60), channel_id=1, source_target_pairs={{0,7},{1,0},{2,1},{3,2},{4,3},{5,4},{6,5},{7,6},{8,15},{9,8},{10,9... | collective-permute-start | bytes 589832 | tf_op jit(solution)/shard_map/ppermute | solution.py:312
  144.4 3.4 %collective-permute-start.5 = (bf16[2,2,64,256]{3,2,1,0:T(8,128)(2,1)}, bf16[2,2,64,256]{3,2,1,0:T(8,128)(2,1)S(1)}, u32[]{:S(2)}, u32[]{:S(2)}) collective-permute-start(bf16[2,2,64,256]{3,2,1,0:T(8,128)(2,1)} %get-tuple-element.59), channel_id=1, source_target_pairs={{0,1},{1,2},{2,3},{3,4},{4,5},{5,6},{6,7},{7,0},{8,9},{9,10},{10,1... | collective-permute-start | bytes 393224 | tf_op jit(solution)/shard_map/ppermute | solution.py:312
  147.8 3.8 %collective-permute-done.5.refs_3_ = bf16[2,2,64,256]{3,2,1,0:T(8,128)(2,1)S(1)} collective-permute-done((bf16[2,2,64,256]{3,2,1,0:T(8,128)(2,1)}, bf16[2,2,64,256]{3,2,1,0:T(8,128)(2,1)S(1)}, u32[]{:S(2)}, u32[]{:S(2)}) %collective-permute-start.5) | collective-permute-done | bytes 131104 | tf_op jit(solution)/shard_map/ppermute | solution.py:312
  151.6 0.0 collective-permute-done.6.refs_4_
  151.6 0.9 collect.1
  152.4 4.5 %collective-permute-start.7 = (bf16[8,64,256]{2,1,0:T(8,128)(2,1)S(1)}, bf16[8,64,256]{2,1,0:T(8,128)(2,1)S(1)}, u32[]{:S(2)}, u32[]{:S(2)}) collective-permute-start(bf16[8,64,256]{2,1,0:T(8,128)(2,1)S(1)} %collect.1), channel_id=1, source_target_pairs={{0,8},{8,0},{1,9},{9,1},{2,10},{10,2},{3,11},{11,3},{4,12},{12,4},... | collective-permute-start | bytes 786440 | tf_op jit(solution)/shard_map/ppermute | solution.py:242
  156.9 1.1 collective-permute-done.7.refs_5_
  158.1 1.7 %assemble_first.1.prev_ref = bf16[2,64,4096]{2,1,0:T(8,128)(2,1)} custom-call(s32[1]{0:T(128)} %bitcast.at.core_ref, s32[1]{0:T(128)} %bitcast.6.row_ref, bf16[1,2,64,256]{3,2,1,0:T(8,128)(2,1)} %get-tuple-element.54.refs_0_, bf16[3,2,64,256]{3,2,1,0:T(8,128)(2,1)S(1)} %collective-permute-done.3.far_ahead_ref.refs_1_, ...), custom_call_target="tpu_custom_call" | custom-call | tf_op jit(solution)/shard_map/assemble_first/pallas_call | solution.py:343
  159.8 0.0 all-to-all-done.4.parts_ref
  159.8 1.8 %assemble_second.1 = bf16[2,64,4096]{2,1,0:T(8,128)(2,1)} custom-call(bf16[16,64,256]{2,1,0:T(8,128)(2,1)} %all-to-all-done.4.parts_ref, bf16[2,64,4096]{2,1,0:T(8,128)(2,1)} %assemble_first.1.prev_ref), custom_call_target="tpu_custom_call", output_to_operand_aliasing={{}: (1, {})} | custom-call | tf_op jit(solution)/shard_map/assemble_second/pallas_call | solution.py:352
Async XLA Ops:
  2.9 10.1 %collective-permute-start = (bf16[768,256]{1,0:T(8,128)(2,1)S(1)}, bf16[768,256]{1,0:T(8,128)(2,1)S(1)}, u32[]{:S(2)}, u32[]{:S(2)}) collective-permute-start(bf16[768,256]{1,0:T(8,128)(2,1)S(1)} %get-tuple-element.34), channel_id=1, source_target_pairs={{0,8},{8,0},{1,9},{9,1},{2,10},{10,2},{3,11},{11,3},{4,12},{12,4},... | collective-permute-start | bytes 1179656 | tf_op jit(solution)/shard_map/ppermute | solution.py:242
  16.8 22.1 %collective-permute-start.1 = (bf16[4,512,256]{2,1,0:T(8,128)(2,1)}, bf16[4,512,256]{2,1,0:T(8,128)(2,1)S(1)}, u32[]{:S(2)}, u32[]{:S(2)}) collective-permute-start(bf16[4,512,256]{2,1,0:T(8,128)(2,1)} %get-tuple-element.41), channel_id=1, source_target_pairs={{0,8},{8,0},{1,9},{9,1},{2,10},{10,2},{3,11},{11,3},{4,12},{12,4},... | collective-permute-start | bytes 3145736 | tf_op jit(solution)/shard_map/ppermute | solution.py:242
  19.1 19.7 %all-to-all-start = ((bf16[32,24,256]{2,1,0:T(8,128)(2,1)}), bf16[32,24,256]{2,1,0:T(8,128)(2,1)S(1)}, u32[]{:S(2)}, u32[]{:S(2)}) async-start(bf16[32,24,256]{2,1,0:T(8,128)(2,1)} %bitcast.1), calls=%async_computation | async-start | bytes 786432 | tf_op jit(solution)/shard_map/all_to_all | solution.py:221
  26.6 12.2 %collective-permute-start.2 = (f32[3,512]{1,0:T(4,128)S(1)}, f32[3,512]{1,0:T(4,128)S(1)}, u32[]{:S(2)}, u32[]{:S(2)}) collective-permute-start(f32[3,512]{1,0:T(4,128)S(1)} %get-tuple-element.42), channel_id=1, source_target_pairs={{0,8},{8,0},{1,9},{9,1},{2,10},{10,2},{3,11},{11,3},{4,12},{12,4},... | collective-permute-start | bytes 18440 | tf_op jit(solution)/shard_map/ppermute | solution.py:242
  38.9 18.8 %copy-start.1 = (f32[3,512]{1,0:T(4,128)}, f32[3,512]{1,0:T(4,128)S(1)}, u32[]{:S(2)}) copy-start(f32[3,512]{1,0:T(4,128)S(1)} %collective-permute-done.2.rates_other_ref) | copy-start | bytes 18436
  57.7 0.7 copy-start.2
  99.2 0.8 copy-start
  100.0 59.8 %all-to-all-start.4 = ((bf16[16,64,256]{2,1,0:T(8,128)(2,1)}), bf16[16,64,256]{2,1,0:T(8,128)(2,1)}, u32[]{:S(2)}, u32[]{:S(2)}) async-start(bf16[16,64,256]{2,1,0:T(8,128)(2,1)} %bitcast.7), calls=%async_computation.4 | async-start | bytes 1048576 | tf_op jit(solution)/shard_map/all_to_all | solution.py:221
  113.5 27.4 %collective-permute-start.3 = (bf16[3,2,64,256]{3,2,1,0:T(8,128)(2,1)S(1)}, bf16[3,2,64,256]{3,2,1,0:T(8,128)(2,1)S(1)}, u32[]{:S(2)}, u32[]{:S(2)}) collective-permute-start(bf16[3,2,64,256]{3,2,1,0:T(8,128)(2,1)S(1)} %get-tuple-element.55), channel_id=1, source_target_pairs={{0,3},{1,4},{2,5},{3,6},{4,7},{5,0},{6,1},{7,2},{8,11},{9,12},{10,... | collective-permute-start | bytes 589832 | tf_op jit(solution)/shard_map/ppermute | solution.py:312
  118.5 13.0 %collective-permute-start.4 = (bf16[2,2,64,256]{3,2,1,0:T(8,128)(2,1)S(1)}, bf16[2,2,64,256]{3,2,1,0:T(8,128)(2,1)S(1)}, u32[]{:S(2)}, u32[]{:S(2)}) collective-permute-start(bf16[2,2,64,256]{3,2,1,0:T(8,128)(2,1)S(1)} %get-tuple-element.56), channel_id=1, source_target_pairs={{0,6},{1,7},{2,0},{3,1},{4,2},{5,3},{6,4},{7,5},{8,14},{9,15},{10,... | collective-permute-start | bytes 393224 | tf_op jit(solution)/shard_map/ppermute | solution.py:312
  142.5 9.1 %collective-permute-start.6 = (bf16[3,2,64,256]{3,2,1,0:T(8,128)(2,1)}, bf16[3,2,64,256]{3,2,1,0:T(8,128)(2,1)S(1)}, u32[]{:S(2)}, u32[]{:S(2)}) collective-permute-start(bf16[3,2,64,256]{3,2,1,0:T(8,128)(2,1)} %get-tuple-element.60), channel_id=1, source_target_pairs={{0,7},{1,0},{2,1},{3,2},{4,3},{5,4},{6,5},{7,6},{8,15},{9,8},{10,9... | collective-permute-start | bytes 589832 | tf_op jit(solution)/shard_map/ppermute | solution.py:312
  144.4 7.1 %collective-permute-start.5 = (bf16[2,2,64,256]{3,2,1,0:T(8,128)(2,1)}, bf16[2,2,64,256]{3,2,1,0:T(8,128)(2,1)S(1)}, u32[]{:S(2)}, u32[]{:S(2)}) collective-permute-start(bf16[2,2,64,256]{3,2,1,0:T(8,128)(2,1)} %get-tuple-element.59), channel_id=1, source_target_pairs={{0,1},{1,2},{2,3},{3,4},{4,5},{5,6},{6,7},{7,0},{8,9},{9,10},{10,1... | collective-permute-start | bytes 393224 | tf_op jit(solution)/shard_map/ppermute | solution.py:312
  152.4 5.7 %collective-permute-start.7 = (bf16[8,64,256]{2,1,0:T(8,128)(2,1)S(1)}, bf16[8,64,256]{2,1,0:T(8,128)(2,1)S(1)}, u32[]{:S(2)}, u32[]{:S(2)}) collective-permute-start(bf16[8,64,256]{2,1,0:T(8,128)(2,1)S(1)} %collect.1), channel_id=1, source_target_pairs={{0,8},{8,0},{1,9},{9,1},{2,10},{10,2},{3,11},{11,3},{4,12},{12,4},... | collective-permute-start | bytes 786440 | tf_op jit(solution)/shard_map/ppermute | solution.py:242

commit v8 on v6

--- a/solution.py
+++ b/solution.py
@@ -292,8 +292,7 @@
         in_specs=[SCALARS, VMEM, VMEM, VMEM],
         out_specs=[VMEM] * len(FIRST_LEVEL),
         out_shape=[
-            (pltpu.HBM if d in ((1,), (-1,)) else jax.ShapeDtypeStruct)((len(d), 2, 64, 256), bf16)
-            for d in FIRST_LEVEL
+            (pltpu.HBM if i > 1 else jax.ShapeDtypeStruct)((n, 2, 64, 256), bf16) for i, n in enumerate((3, 2, 2, 3, 1))
         ],
         scratch_shapes=[pltpu.VMEM((ROWS, 2, 64, 256), bf16)],
         name="apply_first",
@@ -305,8 +304,9 @@
 
     far_ahead = sent(far_ahead, 3)
     far_behind = sent(far_behind, -2)
-    ahead = sent(jnp.concatenate([ahead, far_ahead[2:]]), 1)
-    behind = sent(jnp.concatenate([behind, far_ahead[:1], far_behind[:1]]), -1)
+    ahead = sent(lax.dynamic_update_slice(ahead, far_ahead[2:], (1, 0, 0, 0)), 1)
+    behind = lax.dynamic_update_slice(behind, far_ahead[:1], (1, 0, 0, 0))
+    behind = sent(lax.dynamic_update_slice(behind, far_behind[:1], (2, 0, 0, 0)), -1)
 
     total = scattered(second)
     summed = gathered(total)

time: 139 us -> 152 us (1.094)
  waiting for transfers between devices: 21.8 us -> 31.9 us
  starting transfers between devices: 58.3 us -> 60.9 us
    ppermute x4, waiting for transfers between devices: 9.49 us -> 16.5 us  [sent(): lax.ppermute(array, 'y', [(j, (j + step) % ROWS) for j in range(ROWS)])]
    all_to_all x3, waiting for transfers between devices: 9.83 us -> 12.9 us  [exchange(): return lax.all_to_all(array, axes, split_axis=0, concat_axis=0, tiled=True)]
    dynamic_update_slice x0 -> x2, local copies, waits for them, and re-layouts: none -> 2.16 us  [the longest x1 1.52 us: program(): behind = lax.dynamic_update_slice(behind, far_ahead[:1], (1, 0, 0, 0))]
    slice x2 -> x0, local copies, waits for them, and re-layouts: 1.73 us -> none  [program(): behind = sent(jnp.concatenate([behind, far_ahead[:1], far_behind[:1]]), -1)]
  transfers between devices with their start and end apart: 11 -> 11, of which waited for: 5 -> 6; matrix products, arithmetic and copies ran while one was open for 1% -> 1% of each run, Pallas kernels for 4% -> 4%
where the time goes in v8:
time: 152 us; the launch traced here: 151 us
  starting transfers between devices  60.9 us (40%)
  blocking collectives  37.1 us (24%)
  waiting for transfers between devices  31.9 us (21%)
  Pallas kernels  14.7 us (10%)
  local copies, waits for them, and re-layouts  5.06 us (3%)
    all_to_all x2, blocking collectives, exchange(): return lax.all_to_all(array, axes, split_axis=0, concat_axis=0, tiled=True)  37.1 us
    all_to_all x3, starting transfers between devices, exchange(): return lax.all_to_all(array, axes, split_axis=0, concat_axis=0, tiled=True)  27.3 us
    ppermute x4, starting transfers between devices, swapped(): return lax.ppermute(array, 'c', [(0, 1), (1, 0)])  17.7 us
    ppermute x4, waiting for transfers between devices, sent(): lax.ppermute(array, 'y', [(j, (j + step) % ROWS) for j in range(ROWS)])  16.5 us
    ppermute x4, starting transfers between devices, sent(): lax.ppermute(array, 'y', [(j, (j + step) % ROWS) for j in range(ROWS)])  15.8 us
    all_to_all x3, waiting for transfers between devices, exchange(): return lax.all_to_all(array, axes, split_axis=0, concat_axis=0, tiled=True)  12.9 us
  transfers between devices with their start and end apart: 11, of which 6 were waited for; matrix products, arithmetic and copies ran while one was open for 1% of the time, Pallas kernels for 4%

profile of v8, /device:TPU:1, one launch (start us, length us, event | category | flops | bytes accessed | tf_op | source)
XLA Modules:
  0.0 150.6 jit_solution(1662440695383290316)
XLA Ops:
  0.0 2.9 %shard_map.55 = (bf16[768,256]{1,0:T(8,128)(2,1)S(1)}, f32[768,256]{1,0:T(8,128)S(1)}) custom-call(s32[1]{0:T(128)} %bitcast.at.core_ref, bf16[3,2,256,256]{3,2,1,0:T(8,128)(2,1)} %init_ref.2, bf16[2,512,512]{2,1,0:T(8,128)(2,1)} %k_ref.2, bf16[2,512,512]{2,1,0:T(8,128)(2,1)} %v_ref.2, f32[3,2,2,512]{3,2,1,0:T(2,128)} %rates_ref.2), custom_call_target="tpu_custom_call" | custom-call | tf_op jit(solution)/shard_map/pallas_call | solution.py:242
  2.9 8.8 %collective-permute-start = (bf16[768,256]{1,0:T(8,128)(2,1)S(1)}, bf16[768,256]{1,0:T(8,128)(2,1)S(1)}, u32[]{:S(2)}, u32[]{:S(2)}) collective-permute-start(bf16[768,256]{1,0:T(8,128)(2,1)S(1)} %get-tuple-element.32), channel_id=1, source_target_pairs={{0,8},{8,0},{1,9},{9,1},{2,10},{10,2},{3,11},{11,3},{4,12},{12,4},... | collective-permute-start | bytes 1179656 | tf_op jit(solution)/shard_map/ppermute | solution.py:234
  11.7 1.3 collective-permute-done
  13.0 0.8 add_convert_fusion
  13.8 2.9 %shard_map.56 = (bf16[4,512,256]{2,1,0:T(8,128)(2,1)S(1)}, bf16[4,512,256]{2,1,0:T(8,128)(2,1)}, bf16[3,256,256]{2,1,0:T(8,128)(2,1)S(1)}, f32[3,512]{1,0:T(4,128)S(1)}, f32[3,512]{1,0:T(4,128)S(1)}) custom-call(s32[1]{0:T(128)} %bitcast.at.core_ref, bf16[2,512,512]{2,1,0:T(8,128)(2,1)} %k_ref.2, bf16[2,512,512]{2,1,0:T(8,128)(2,1)} %v_ref.2, ...), custom_call_target="tpu_custom_call" | custom-call | tf_op jit(solution)/shard_map/pallas_call | solution.py:259
  16.8 2.3 %collective-permute-start.1 = (bf16[4,512,256]{2,1,0:T(8,128)(2,1)}, bf16[4,512,256]{2,1,0:T(8,128)(2,1)S(1)}, u32[]{:S(2)}, u32[]{:S(2)}) collective-permute-start(bf16[4,512,256]{2,1,0:T(8,128)(2,1)} %get-tuple-element.39), channel_id=1, source_target_pairs={{0,8},{8,0},{1,9},{9,1},{2,10},{10,2},{3,11},{11,3},{4,12},{12,4},... | collective-permute-start | bytes 3145736 | tf_op jit(solution)/shard_map/ppermute | solution.py:234
  19.1 7.6 %all-to-all-start = ((bf16[32,24,256]{2,1,0:T(8,128)(2,1)}), bf16[32,24,256]{2,1,0:T(8,128)(2,1)S(1)}, u32[]{:S(2)}, u32[]{:S(2)}) async-start(bf16[32,24,256]{2,1,0:T(8,128)(2,1)} %bitcast.1), calls=%async_computation | async-start | bytes 786432 | tf_op jit(solution)/shard_map/all_to_all | solution.py:213
  26.6 2.3 %collective-permute-start.2 = (f32[3,512]{1,0:T(4,128)S(1)}, f32[3,512]{1,0:T(4,128)S(1)}, u32[]{:S(2)}, u32[]{:S(2)}) collective-permute-start(f32[3,512]{1,0:T(4,128)S(1)} %get-tuple-element.40), channel_id=1, source_target_pairs={{0,8},{8,0},{1,9},{9,1},{2,10},{10,2},{3,11},{11,3},{4,12},{12,4},... | collective-permute-start | bytes 18440 | tf_op jit(solution)/shard_map/ppermute | solution.py:234
  28.9 9.8 %all-to-all-done.parts_ref = bf16[32,24,256]{2,1,0:T(8,128)(2,1)S(1)} async-done(((bf16[32,24,256]{2,1,0:T(8,128)(2,1)}), bf16[32,24,256]{2,1,0:T(8,128)(2,1)S(1)}, u32[]{:S(2)}, u32[]{:S(2)}) %all-to-all-start) | async-done | bytes 393248 | tf_op jit(solution)/shard_map/all_to_all | solution.py:213
  38.8 0.1 total.2
  38.9 0.0 collective-permute-done.2.rates_other_ref
  38.9 0.0 copy-start.3
  38.9 0.0 collective-permute-done.1.other_ref
  38.9 18.8 %all_to_all.25 = bf16[32,24,256]{2,1,0:T(8,128)(2,1)S(1)} all-to-all(bf16[32,24,256]{2,1,0:T(8,128)(2,1)S(1)} %total.2), channel_id=1, replica_groups=mesh['x'=4,'z'=8,'c'=2,'y'=8] {'x','z'}, dimensions={0} | all-to-all | bytes 786432 | tf_op jit(solution)/shard_map/all_to_all | solution.py:213
  57.7 0.0 copy-done.3
  57.7 0.0 copy-start.4
  57.7 0.7 copy-done.4
  58.4 2.5 %second.1 = (bf16[768,256]{1,0:T(8,128)(2,1)}, f32[1032,256]{1,0:T(8,128)S(1)}) custom-call(bf16[3,256,256]{2,1,0:T(8,128)(2,1)S(1)} %get-tuple-element.44.init_ref, bf16[768,256]{1,0:T(8,128)(2,1)S(1)} %bitcast.9, bf16[4,512,256]{2,1,0:T(8,128)(2,1)S(1)} %get-tuple-element.46.own_ref, bf16[4,512,256]{2,1,0:T(8,128)(2,1)S(1)} %collective-permute-done.1.other_ref, ...), custom_call_target="tpu_custom_call" | custom-call | tf_op jit(solution)/shard_map/second/pallas_call | solution.py:278
  60.9 18.3 %all_to_all.26.parts_ref = bf16[32,24,256]{2,1,0:T(8,128)(2,1)S(1)} all-to-all(bf16[32,24,256]{2,1,0:T(8,128)(2,1)} %bitcast.10), channel_id=1, replica_groups=mesh['x'=4,'z'=8,'c'=2,'y'=8] {'x','z'}, dimensions={0} | all-to-all | bytes 786432 | tf_op jit(solution)/shard_map/all_to_all | solution.py:213
  79.2 0.1 total.3
  79.2 0.0 copy-start.1
  79.3 0.7 copy-done.1
  80.0 7.6 %all-to-all-start.3 = ((bf16[32,24,256]{2,1,0:T(8,128)(2,1)}), bf16[32,24,256]{2,1,0:T(8,128)(2,1)S(1)}, u32[]{:S(2)}, u32[]{:S(2)}) async-start(bf16[32,24,256]{2,1,0:T(8,128)(2,1)} %copy-done.1), calls=%async_computation.3 | async-start | bytes 786432 | tf_op jit(solution)/shard_map/all_to_all | solution.py:213
  87.6 1.6 %apply_first.1 = (bf16[3,2,64,256]{3,2,1,0:T(8,128)(2,1)}, bf16[2,2,64,256]{3,2,1,0:T(8,128)(2,1)S(1)}, bf16[2,2,64,256]{3,2,1,0:T(8,128)(2,1)}, bf16[3,2,64,256]{3,2,1,0:T(8,128)(2,1)}, bf16[1,2,64,256]{3,2,1,0:T(8,128)(2,1)}) custom-call(s32[1]{0:T(128)} %bitcast.6.row_ref, f32[1032,256]{1,0:T(8,128)S(1)} %get-tuple-element.50.kept_ref, ...), custom_call_target="tpu_custom_call" | custom-call | tf_op jit(solution)/shard_map/apply_first/pallas_call | solution.py:290
  89.2 0.0 copy-start.5
  89.2 0.7 copy-done.5
  89.8 5.2 %collective-permute-start.3 = (bf16[3,2,64,256]{3,2,1,0:T(8,128)(2,1)}, bf16[3,2,64,256]{3,2,1,0:T(8,128)(2,1)}, u32[]{:S(2)}, u32[]{:S(2)}) collective-permute-start(bf16[3,2,64,256]{3,2,1,0:T(8,128)(2,1)} %get-tuple-element.53), channel_id=1, source_target_pairs={{0,3},{1,4},{2,5},{3,6},{4,7},{5,0},{6,1},{7,2},{8,11},{9,12},{10,... | collective-permute-start | bytes 589832 | tf_op jit(solution)/shard_map/ppermute | solution.py:303
  95.0 3.1 %all-to-all-done.3 = bf16[32,24,256]{2,1,0:T(8,128)(2,1)S(1)} async-done(((bf16[32,24,256]{2,1,0:T(8,128)(2,1)}), bf16[32,24,256]{2,1,0:T(8,128)(2,1)S(1)}, u32[]{:S(2)}, u32[]{:S(2)}) %all-to-all-start.3) | async-done | bytes 393248 | tf_op jit(solution)/shard_map/all_to_all | solution.py:213
  98.1 1.1 shard_map.57
  99.2 0.0 copy-start
  99.2 0.8 copy-done
  100.0 12.2 %all-to-all-start.4 = ((bf16[16,64,256]{2,1,0:T(8,128)(2,1)}), bf16[16,64,256]{2,1,0:T(8,128)(2,1)S(1)}, u32[]{:S(2)}, u32[]{:S(2)}) async-start(bf16[16,64,256]{2,1,0:T(8,128)(2,1)} %bitcast.7), calls=%async_computation.4 | async-start | bytes 1048576 | tf_op jit(solution)/shard_map/all_to_all | solution.py:213
  112.2 5.4 %collective-permute-start.4 = (bf16[2,2,64,256]{3,2,1,0:T(8,128)(2,1)}, bf16[2,2,64,256]{3,2,1,0:T(8,128)(2,1)S(1)}, u32[]{:S(2)}, u32[]{:S(2)}) collective-permute-start(bf16[2,2,64,256]{3,2,1,0:T(8,128)(2,1)} %copy-done.5), channel_id=1, source_target_pairs={{0,6},{1,7},{2,0},{3,1},{4,2},{5,3},{6,4},{7,5},{8,14},{9,15},{10,... | collective-permute-start | bytes 393224 | tf_op jit(solution)/shard_map/ppermute | solution.py:303
  117.6 0.0 collective-permute-done.3.refs_1_
  117.6 1.5 %slice_dynamic-update-slice_fusion.1 = (bf16[3,2,64,256]{3,2,1,0:T(8,128)(2,1)}, bf16[2,2,64,256]{3,2,1,0:T(8,128)(2,1)}) fusion(bf16[3,2,64,256]{3,2,1,0:T(8,128)(2,1)} %get-tuple-element.56, bf16[3,2,64,256]{3,2,1,0:T(8,128)(2,1)} %collective-permute-done.3.refs_1_, bf16[2,2,64,256]{3,2,1,0:T(8,128)(2,1)} %get-tuple-element.55), kind=kLoop, calls=%fused_computation.2 | loop fusion | bytes 262144 | tf_op jit(solution)/shard_map/dynamic_update_slice | solution.py:308
  119.1 12.7 %collective-permute-done.4.refs_2_ = bf16[2,2,64,256]{3,2,1,0:T(8,128)(2,1)S(1)} collective-permute-done((bf16[2,2,64,256]{3,2,1,0:T(8,128)(2,1)}, bf16[2,2,64,256]{3,2,1,0:T(8,128)(2,1)S(1)}, u32[]{:S(2)}, u32[]{:S(2)}) %collective-permute-start.4) | collective-permute-done | bytes 131104 | tf_op jit(solution)/shard_map/ppermute | solution.py:303
  131.8 0.6 slice_dynamic-update-slice_fusion
  132.5 1.9 %collective-permute-start.6 = (bf16[3,2,64,256]{3,2,1,0:T(8,128)(2,1)}, bf16[3,2,64,256]{3,2,1,0:T(8,128)(2,1)S(1)}, u32[]{:S(2)}, u32[]{:S(2)}) collective-permute-start(bf16[3,2,64,256]{3,2,1,0:T(8,128)(2,1)} %slice_dynamic-update-slice_fusion), channel_id=1, source_target_pairs={{0,7},{1,0},{2,1},{3,2},{4,3},{5,4},{6,5},{7,6},{8,15},{9,8},{10,9... | collective-permute-start | bytes 589832 | tf_op jit(solution)/shard_map/ppermute | solution.py:303
  134.4 3.4 %collective-permute-start.5 = (bf16[2,2,64,256]{3,2,1,0:T(8,128)(2,1)}, bf16[2,2,64,256]{3,2,1,0:T(8,128)(2,1)S(1)}, u32[]{:S(2)}, u32[]{:S(2)}) collective-permute-start(bf16[2,2,64,256]{3,2,1,0:T(8,128)(2,1)} %get-tuple-element.58), channel_id=1, source_target_pairs={{0,1},{1,2},{2,3},{3,4},{4,5},{5,6},{6,7},{7,0},{8,9},{9,10},{10,1... | collective-permute-start | bytes 393224 | tf_op jit(solution)/shard_map/ppermute | solution.py:303
  137.8 3.8 %collective-permute-done.5.refs_3_ = bf16[2,2,64,256]{3,2,1,0:T(8,128)(2,1)S(1)} collective-permute-done((bf16[2,2,64,256]{3,2,1,0:T(8,128)(2,1)}, bf16[2,2,64,256]{3,2,1,0:T(8,128)(2,1)S(1)}, u32[]{:S(2)}, u32[]{:S(2)}) %collective-permute-start.5) | collective-permute-done | bytes 131104 | tf_op jit(solution)/shard_map/ppermute | solution.py:303
  141.5 0.0 collective-permute-done.6.refs_4_
  141.5 0.0 copy-done.2
  141.5 0.9 collect.1
  142.5 4.4 %collective-permute-start.7 = (bf16[8,64,256]{2,1,0:T(8,128)(2,1)S(1)}, bf16[8,64,256]{2,1,0:T(8,128)(2,1)S(1)}, u32[]{:S(2)}, u32[]{:S(2)}) collective-permute-start(bf16[8,64,256]{2,1,0:T(8,128)(2,1)S(1)} %collect.1), channel_id=1, source_target_pairs={{0,8},{8,0},{1,9},{9,1},{2,10},{10,2},{3,11},{11,3},{4,12},{12,4},... | collective-permute-start | bytes 786440 | tf_op jit(solution)/shard_map/ppermute | solution.py:234
  146.9 1.1 collective-permute-done.7.refs_5_
  148.0 1.8 %assemble_first.1.prev_ref = bf16[2,64,4096]{2,1,0:T(8,128)(2,1)} custom-call(s32[1]{0:T(128)} %bitcast.at.core_ref, s32[1]{0:T(128)} %bitcast.6.row_ref, bf16[1,2,64,256]{3,2,1,0:T(8,128)(2,1)S(1)} %copy-done.2, bf16[3,2,64,256]{3,2,1,0:T(8,128)(2,1)} %collective-permute-done.3.refs_1_, bf16[2,2,64,256]{3,2,1,0:T(8,128)(2,1)S(1)} %collective-permute-done.4.refs_2_, ...), custom_call_target="tpu_custom_call" | custom-call | tf_op jit(solution)/shard_map/assemble_first/pallas_call | solution.py:327
  149.8 0.0 all-to-all-done.4.parts_ref
  149.8 0.8 assemble_second.1
  (1 shorter events, 0.0 us)
Async XLA Ops:
  2.9 10.1 %collective-permute-start = (bf16[768,256]{1,0:T(8,128)(2,1)S(1)}, bf16[768,256]{1,0:T(8,128)(2,1)S(1)}, u32[]{:S(2)}, u32[]{:S(2)}) collective-permute-start(bf16[768,256]{1,0:T(8,128)(2,1)S(1)} %get-tuple-element.32), channel_id=1, source_target_pairs={{0,8},{8,0},{1,9},{9,1},{2,10},{10,2},{3,11},{11,3},{4,12},{12,4},... | collective-permute-start | bytes 1179656 | tf_op jit(solution)/shard_map/ppermute | solution.py:234
  16.8 22.1 %collective-permute-start.1 = (bf16[4,512,256]{2,1,0:T(8,128)(2,1)}, bf16[4,512,256]{2,1,0:T(8,128)(2,1)S(1)}, u32[]{:S(2)}, u32[]{:S(2)}) collective-permute-start(bf16[4,512,256]{2,1,0:T(8,128)(2,1)} %get-tuple-element.39), channel_id=1, source_target_pairs={{0,8},{8,0},{1,9},{9,1},{2,10},{10,2},{3,11},{11,3},{4,12},{12,4},... | collective-permute-start | bytes 3145736 | tf_op jit(solution)/shard_map/ppermute | solution.py:234
  19.1 19.7 %all-to-all-start = ((bf16[32,24,256]{2,1,0:T(8,128)(2,1)}), bf16[32,24,256]{2,1,0:T(8,128)(2,1)S(1)}, u32[]{:S(2)}, u32[]{:S(2)}) async-start(bf16[32,24,256]{2,1,0:T(8,128)(2,1)} %bitcast.1), calls=%async_computation | async-start | bytes 786432 | tf_op jit(solution)/shard_map/all_to_all | solution.py:213
  26.6 12.2 %collective-permute-start.2 = (f32[3,512]{1,0:T(4,128)S(1)}, f32[3,512]{1,0:T(4,128)S(1)}, u32[]{:S(2)}, u32[]{:S(2)}) collective-permute-start(f32[3,512]{1,0:T(4,128)S(1)} %get-tuple-element.40), channel_id=1, source_target_pairs={{0,8},{8,0},{1,9},{9,1},{2,10},{10,2},{3,11},{11,3},{4,12},{12,4},... | collective-permute-start | bytes 18440 | tf_op jit(solution)/shard_map/ppermute | solution.py:234
  38.9 18.8 %copy-start.3 = (f32[3,512]{1,0:T(4,128)}, f32[3,512]{1,0:T(4,128)S(1)}, u32[]{:S(2)}) copy-start(f32[3,512]{1,0:T(4,128)S(1)} %collective-permute-done.2.rates_other_ref) | copy-start | bytes 18436
  57.7 0.7 copy-start.4
  79.2 0.7 copy-start.1
  80.0 18.1 %all-to-all-start.3 = ((bf16[32,24,256]{2,1,0:T(8,128)(2,1)}), bf16[32,24,256]{2,1,0:T(8,128)(2,1)S(1)}, u32[]{:S(2)}, u32[]{:S(2)}) async-start(bf16[32,24,256]{2,1,0:T(8,128)(2,1)} %copy-done.1), calls=%async_computation.3 | async-start | bytes 786432 | tf_op jit(solution)/shard_map/all_to_all | solution.py:213
  89.2 0.7 copy-start.5
  89.8 27.8 %collective-permute-start.3 = (bf16[3,2,64,256]{3,2,1,0:T(8,128)(2,1)}, bf16[3,2,64,256]{3,2,1,0:T(8,128)(2,1)}, u32[]{:S(2)}, u32[]{:S(2)}) collective-permute-start(bf16[3,2,64,256]{3,2,1,0:T(8,128)(2,1)} %get-tuple-element.53), channel_id=1, source_target_pairs={{0,3},{1,4},{2,5},{3,6},{4,7},{5,0},{6,1},{7,2},{8,11},{9,12},{10,... | collective-permute-start | bytes 589832 | tf_op jit(solution)/shard_map/ppermute | solution.py:303
  99.2 0.8 copy-start
  100.0 41.5 %copy-start.2 = (bf16[1,2,64,256]{3,2,1,0:T(8,128)(2,1)S(1)}, bf16[1,2,64,256]{3,2,1,0:T(8,128)(2,1)}, u32[]{:S(2)}) copy-start(bf16[1,2,64,256]{3,2,1,0:T(8,128)(2,1)} %get-tuple-element.52.refs_0_) | copy-start | bytes 196612
  100.0 49.8 %all-to-all-start.4 = ((bf16[16,64,256]{2,1,0:T(8,128)(2,1)}), bf16[16,64,256]{2,1,0:T(8,128)(2,1)S(1)}, u32[]{:S(2)}, u32[]{:S(2)}) async-start(bf16[16,64,256]{2,1,0:T(8,128)(2,1)} %bitcast.7), calls=%async_computation.4 | async-start | bytes 1048576 | tf_op jit(solution)/shard_map/all_to_all | solution.py:213
  112.2 19.6 %collective-permute-start.4 = (bf16[2,2,64,256]{3,2,1,0:T(8,128)(2,1)}, bf16[2,2,64,256]{3,2,1,0:T(8,128)(2,1)S(1)}, u32[]{:S(2)}, u32[]{:S(2)}) collective-permute-start(bf16[2,2,64,256]{3,2,1,0:T(8,128)(2,1)} %copy-done.5), channel_id=1, source_target_pairs={{0,6},{1,7},{2,0},{3,1},{4,2},{5,3},{6,4},{7,5},{8,14},{9,15},{10,... | collective-permute-start | bytes 393224 | tf_op jit(solution)/shard_map/ppermute | solution.py:303
  132.5 9.1 %collective-permute-start.6 = (bf16[3,2,64,256]{3,2,1,0:T(8,128)(2,1)}, bf16[3,2,64,256]{3,2,1,0:T(8,128)(2,1)S(1)}, u32[]{:S(2)}, u32[]{:S(2)}) collective-permute-start(bf16[3,2,64,256]{3,2,1,0:T(8,128)(2,1)} %slice_dynamic-update-slice_fusion), channel_id=1, source_target_pairs={{0,7},{1,0},{2,1},{3,2},{4,3},{5,4},{6,5},{7,6},{8,15},{9,8},{10,9... | collective-permute-start | bytes 589832 | tf_op jit(solution)/shard_map/ppermute | solution.py:303
  134.4 7.1 %collective-permute-start.5 = (bf16[2,2,64,256]{3,2,1,0:T(8,128)(2,1)}, bf16[2,2,64,256]{3,2,1,0:T(8,128)(2,1)S(1)}, u32[]{:S(2)}, u32[]{:S(2)}) collective-permute-start(bf16[2,2,64,256]{3,2,1,0:T(8,128)(2,1)} %get-tuple-element.58), channel_id=1, source_target_pairs={{0,1},{1,2},{2,3},{3,4},{4,5},{5,6},{6,7},{7,0},{8,9},{9,10},{10,1... | collective-permute-start | bytes 393224 | tf_op jit(solution)/shard_map/ppermute | solution.py:303
  142.5 5.5 %collective-permute-start.7 = (bf16[8,64,256]{2,1,0:T(8,128)(2,1)S(1)}, bf16[8,64,256]{2,1,0:T(8,128)(2,1)S(1)}, u32[]{:S(2)}, u32[]{:S(2)}) collective-permute-start(bf16[8,64,256]{2,1,0:T(8,128)(2,1)S(1)} %collect.1), channel_id=1, source_target_pairs={{0,8},{8,0},{1,9},{9,1},{2,10},{10,2},{3,11},{11,3},{4,12},{12,4},... | collective-permute-start | bytes 786440 | tf_op jit(solution)/shard_map/ppermute | solution.py:234

commit v9 on v8

--- a/solution.py
+++ b/solution.py
@@ -136,6 +136,11 @@
         out_ref[:, pl.ds(core, 1)] = applied(q, weights).reshape(ROWS, 1, 64, 256)
 
 
+def total_with_rates_kernel(parts_ref, rates_ref, out_ref, rates_out_ref):
+    rates_out_ref[...] = rates_ref[...]
+    total_kernel(parts_ref, out_ref)
+
+
 def total_kernel(parts_ref, out_ref):
     total = jnp.sum(parts_ref[...].astype(f32), axis=0, keepdims=True)
     out_ref[...] = jnp.broadcast_to(total.astype(bf16), out_ref.shape)
@@ -213,16 +218,19 @@
     return lax.all_to_all(array, axes, split_axis=0, concat_axis=0, tiled=True)
 
 
-def scattered(partial):
+def scattered(partial, rates=None):
     parts = exchange(partial.reshape(32, 24, 256), ("x", "z"))
-    return pl.pallas_call(
-        total_kernel,
-        in_specs=[VMEM],
-        out_specs=VMEM,
-        out_shape=jax.ShapeDtypeStruct((32, 24, 256), bf16),
+    args = [on_chip(parts)] if rates is None else [on_chip(parts), on_chip(rates)]
+    shapes = [jax.ShapeDtypeStruct((32, 24, 256), bf16), jax.ShapeDtypeStruct((3, 512), f32)][: len(args)]
+    result = pl.pallas_call(
+        total_kernel if rates is None else total_with_rates_kernel,
+        in_specs=[VMEM] * len(args),
+        out_specs=[VMEM] * len(args),
+        out_shape=shapes,
         name="total",
         compiler_params=LIMIT,
-    )(on_chip(parts))
+    )(*args)
+    return result[0] if rates is None else result
 
 
 def gathered(total):
@@ -270,7 +278,7 @@
     other = swapped(other)
     rates_other = swapped(rates_other)
 
-    total = scattered(first)
+    total, rates_other = scattered(first, rates_other)
     total, other, rates_other, own, rates_own, init = lax.optimization_barrier(
         (total, other, rates_other, own, rates_own, init)
     )
@@ -314,7 +322,7 @@
         last_kernel, [VMEM, VMEM, VMEM, VMEM], [((ROWS, 2, 64, 256), bf16)]
     )(at, on_chip(kept), summed, on_chip(own), on_chip(other))
     parts = exchange(result.reshape(16, 64, 256), ("y", "c"))
-    got = [on_chip(a) for a in (here, far_ahead, far_behind, ahead, behind)]
+    got = [off_chip(here)] + [on_chip(a) for a in (far_ahead, far_behind, ahead, behind)]
     halves = pl.pallas_call(
         collect_kernel,
         in_specs=[VMEM] * 5,

time: 152 us -> 151 us (level)
  transfers between devices with their start and end apart: 11 -> 11, of which waited for: 6 -> 7; matrix products, arithmetic and copies ran while one was open for 1% -> 1% of each run, Pallas kernels for 4% -> 4%
where the time goes in v9:
time: 151 us; the launch traced here: 150 us
  starting transfers between devices  60.7 us (40%)
  blocking collectives  37.1 us (25%)
  waiting for transfers between devices  31.9 us (21%)
  Pallas kernels  14.8 us (10%)
  local copies, waits for them, and re-layouts  4.37 us (3%)
    all_to_all x2, blocking collectives, exchange(): return lax.all_to_all(array, axes, split_axis=0, concat_axis=0, tiled=True)  37.1 us
    all_to_all x3, starting transfers between devices, exchange(): return lax.all_to_all(array, axes, split_axis=0, concat_axis=0, tiled=True)  27.2 us
    ppermute x4, starting transfers between devices, swapped(): return lax.ppermute(array, 'c', [(0, 1), (1, 0)])  17.7 us
    ppermute x4, waiting for transfers between devices, sent(): lax.ppermute(array, 'y', [(j, (j + step) % ROWS) for j in range(ROWS)])  16.5 us
    ppermute x4, starting transfers between devices, sent(): lax.ppermute(array, 'y', [(j, (j + step) % ROWS) for j in range(ROWS)])  15.9 us
    all_to_all x3, waiting for transfers between devices, exchange(): return lax.all_to_all(array, axes, split_axis=0, concat_axis=0, tiled=True)  12.1 us
    ppermute x4, waiting for transfers between devices, swapped(): return lax.ppermute(array, 'c', [(0, 1), (1, 0)])  3.28 us
  transfers between devices with their start and end apart: 11, of which 7 were waited for; matrix products, arithmetic and copies ran while one was open for 1% of the time, Pallas kernels for 4%

profile of v9, /device:TPU:1, one launch (start us, length us, event | category | flops | bytes accessed | tf_op | source)
XLA Modules:
  0.0 149.8 jit_solution(5491494556733023710)
XLA Ops:
  0.0 2.9 %shard_map.55 = (bf16[768,256]{1,0:T(8,128)(2,1)S(1)}, f32[768,256]{1,0:T(8,128)S(1)}) custom-call(s32[1]{0:T(128)} %bitcast.at.core_ref, bf16[3,2,256,256]{3,2,1,0:T(8,128)(2,1)} %init_ref.2, bf16[2,512,512]{2,1,0:T(8,128)(2,1)} %k_ref.2, bf16[2,512,512]{2,1,0:T(8,128)(2,1)} %v_ref.2, f32[3,2,2,512]{3,2,1,0:T(2,128)} %rates_ref.2), custom_call_target="tpu_custom_call" | custom-call | tf_op jit(solution)/shard_map/pallas_call | solution.py:250
  2.9 8.8 %collective-permute-start = (bf16[768,256]{1,0:T(8,128)(2,1)S(1)}, bf16[768,256]{1,0:T(8,128)(2,1)S(1)}, u32[]{:S(2)}, u32[]{:S(2)}) collective-permute-start(bf16[768,256]{1,0:T(8,128)(2,1)S(1)} %get-tuple-element.34), channel_id=1, source_target_pairs={{0,8},{8,0},{1,9},{9,1},{2,10},{10,2},{3,11},{11,3},{4,12},{12,4},... | collective-permute-start | bytes 1179656 | tf_op jit(solution)/shard_map/ppermute | solution.py:242
  11.7 1.3 collective-permute-done
  13.0 0.8 add_convert_fusion
  13.9 2.9 %shard_map.56 = (bf16[4,512,256]{2,1,0:T(8,128)(2,1)S(1)}, bf16[4,512,256]{2,1,0:T(8,128)(2,1)}, bf16[3,256,256]{2,1,0:T(8,128)(2,1)S(1)}, f32[3,512]{1,0:T(4,128)S(1)}, f32[3,512]{1,0:T(4,128)S(1)}) custom-call(s32[1]{0:T(128)} %bitcast.at.core_ref, bf16[2,512,512]{2,1,0:T(8,128)(2,1)} %k_ref.2, bf16[2,512,512]{2,1,0:T(8,128)(2,1)} %v_ref.2, ...), custom_call_target="tpu_custom_call" | custom-call | tf_op jit(solution)/shard_map/pallas_call | solution.py:267
  16.8 2.3 %collective-permute-start.2 = (bf16[4,512,256]{2,1,0:T(8,128)(2,1)}, bf16[4,512,256]{2,1,0:T(8,128)(2,1)S(1)}, u32[]{:S(2)}, u32[]{:S(2)}) collective-permute-start(bf16[4,512,256]{2,1,0:T(8,128)(2,1)} %get-tuple-element.43), channel_id=1, source_target_pairs={{0,8},{8,0},{1,9},{9,1},{2,10},{10,2},{3,11},{11,3},{4,12},{12,4},... | collective-permute-start | bytes 3145736 | tf_op jit(solution)/shard_map/ppermute | solution.py:242
  19.1 7.6 %all-to-all-start = ((bf16[32,24,256]{2,1,0:T(8,128)(2,1)}), bf16[32,24,256]{2,1,0:T(8,128)(2,1)S(1)}, u32[]{:S(2)}, u32[]{:S(2)}) async-start(bf16[32,24,256]{2,1,0:T(8,128)(2,1)} %bitcast.1), calls=%async_computation | async-start | bytes 786432 | tf_op jit(solution)/shard_map/all_to_all | solution.py:218
  26.6 2.3 %collective-permute-start.1 = (f32[3,512]{1,0:T(4,128)S(1)}, f32[3,512]{1,0:T(4,128)S(1)}, u32[]{:S(2)}, u32[]{:S(2)}) collective-permute-start(f32[3,512]{1,0:T(4,128)S(1)} %get-tuple-element.41), channel_id=1, source_target_pairs={{0,8},{8,0},{1,9},{9,1},{2,10},{10,2},{3,11},{11,3},{4,12},{12,4},... | collective-permute-start | bytes 18440 | tf_op jit(solution)/shard_map/ppermute | solution.py:242
  29.0 0.8 collective-permute-done.1.rates_ref
  29.8 9.0 %all-to-all-done.parts_ref = bf16[32,24,256]{2,1,0:T(8,128)(2,1)S(1)} async-done(((bf16[32,24,256]{2,1,0:T(8,128)(2,1)}), bf16[32,24,256]{2,1,0:T(8,128)(2,1)S(1)}, u32[]{:S(2)}, u32[]{:S(2)}) %all-to-all-start) | async-done | bytes 393248 | tf_op jit(solution)/shard_map/all_to_all | solution.py:218
  38.8 0.1 total.2
  38.9 0.0 collective-permute-done.2.other_ref
  38.9 18.8 %all_to_all.25 = bf16[32,24,256]{2,1,0:T(8,128)(2,1)S(1)} all-to-all(bf16[32,24,256]{2,1,0:T(8,128)(2,1)S(1)} %get-tuple-element.49), channel_id=1, replica_groups=mesh['x'=4,'z'=8,'c'=2,'y'=8] {'x','z'}, dimensions={0} | all-to-all | bytes 786432 | tf_op jit(solution)/shard_map/all_to_all | solution.py:218
  57.7 2.5 %second.1 = (bf16[768,256]{1,0:T(8,128)(2,1)}, f32[1032,256]{1,0:T(8,128)S(1)}) custom-call(bf16[3,256,256]{2,1,0:T(8,128)(2,1)S(1)} %get-tuple-element.48.init_ref, bf16[768,256]{1,0:T(8,128)(2,1)S(1)} %bitcast.9, bf16[4,512,256]{2,1,0:T(8,128)(2,1)S(1)} %get-tuple-element.50.own_ref, bf16[4,512,256]{2,1,0:T(8,128)(2,1)S(1)} %collective-permute-done.2.other_ref, ...), custom_call_target="tpu_custom_call" | custom-call | tf_op jit(solution)/shard_map/second/pallas_call | solution.py:286
  60.2 18.3 %all_to_all.26.parts_ref = bf16[32,24,256]{2,1,0:T(8,128)(2,1)S(1)} all-to-all(bf16[32,24,256]{2,1,0:T(8,128)(2,1)} %bitcast.10), channel_id=1, replica_groups=mesh['x'=4,'z'=8,'c'=2,'y'=8] {'x','z'}, dimensions={0} | all-to-all | bytes 786432 | tf_op jit(solution)/shard_map/all_to_all | solution.py:218
  78.5 0.1 total.3
  78.6 0.0 copy-start.1
  78.6 0.7 copy-done.1
  79.3 7.6 %all-to-all-start.3 = ((bf16[32,24,256]{2,1,0:T(8,128)(2,1)}), bf16[32,24,256]{2,1,0:T(8,128)(2,1)S(1)}, u32[]{:S(2)}, u32[]{:S(2)}) async-start(bf16[32,24,256]{2,1,0:T(8,128)(2,1)} %copy-done.1), calls=%async_computation.3 | async-start | bytes 786432 | tf_op jit(solution)/shard_map/all_to_all | solution.py:218
  86.9 1.6 %apply_first.1 = (bf16[3,2,64,256]{3,2,1,0:T(8,128)(2,1)}, bf16[2,2,64,256]{3,2,1,0:T(8,128)(2,1)S(1)}, bf16[2,2,64,256]{3,2,1,0:T(8,128)(2,1)}, bf16[3,2,64,256]{3,2,1,0:T(8,128)(2,1)}, bf16[1,2,64,256]{3,2,1,0:T(8,128)(2,1)}) custom-call(s32[1]{0:T(128)} %bitcast.6.row_ref, f32[1032,256]{1,0:T(8,128)S(1)} %get-tuple-element.54.kept_ref, ...), custom_call_target="tpu_custom_call" | custom-call | tf_op jit(solution)/shard_map/apply_first/pallas_call | solution.py:298
  88.5 0.0 copy-start.2
  88.5 0.7 copy-done.2
  89.1 5.2 %collective-permute-start.3 = (bf16[3,2,64,256]{3,2,1,0:T(8,128)(2,1)}, bf16[3,2,64,256]{3,2,1,0:T(8,128)(2,1)}, u32[]{:S(2)}, u32[]{:S(2)}) collective-permute-start(bf16[3,2,64,256]{3,2,1,0:T(8,128)(2,1)} %get-tuple-element.57), channel_id=1, source_target_pairs={{0,3},{1,4},{2,5},{3,6},{4,7},{5,0},{6,1},{7,2},{8,11},{9,12},{10,... | collective-permute-start | bytes 589832 | tf_op jit(solution)/shard_map/ppermute | solution.py:311
  94.3 3.1 %all-to-all-done.3 = bf16[32,24,256]{2,1,0:T(8,128)(2,1)S(1)} async-done(((bf16[32,24,256]{2,1,0:T(8,128)(2,1)}), bf16[32,24,256]{2,1,0:T(8,128)(2,1)S(1)}, u32[]{:S(2)}, u32[]{:S(2)}) %all-to-all-start.3) | async-done | bytes 393248 | tf_op jit(solution)/shard_map/all_to_all | solution.py:218
  97.4 1.1 shard_map.57
  98.5 0.0 copy-start
  98.5 0.8 copy-done
  99.3 12.1 %all-to-all-start.4 = ((bf16[16,64,256]{2,1,0:T(8,128)(2,1)}), bf16[16,64,256]{2,1,0:T(8,128)(2,1)S(1)}, u32[]{:S(2)}, u32[]{:S(2)}) async-start(bf16[16,64,256]{2,1,0:T(8,128)(2,1)} %bitcast.7), calls=%async_computation.4 | async-start | bytes 1048576 | tf_op jit(solution)/shard_map/all_to_all | solution.py:218
  111.4 5.4 %collective-permute-start.4 = (bf16[2,2,64,256]{3,2,1,0:T(8,128)(2,1)}, bf16[2,2,64,256]{3,2,1,0:T(8,128)(2,1)S(1)}, u32[]{:S(2)}, u32[]{:S(2)}) collective-permute-start(bf16[2,2,64,256]{3,2,1,0:T(8,128)(2,1)} %copy-done.2), channel_id=1, source_target_pairs={{0,6},{1,7},{2,0},{3,1},{4,2},{5,3},{6,4},{7,5},{8,14},{9,15},{10,... | collective-permute-start | bytes 393224 | tf_op jit(solution)/shard_map/ppermute | solution.py:311
  116.7 0.0 collective-permute-done.3.refs_1_
  116.7 1.5 %slice_dynamic-update-slice_fusion.1 = (bf16[3,2,64,256]{3,2,1,0:T(8,128)(2,1)}, bf16[2,2,64,256]{3,2,1,0:T(8,128)(2,1)}) fusion(bf16[3,2,64,256]{3,2,1,0:T(8,128)(2,1)} %get-tuple-element.60, bf16[3,2,64,256]{3,2,1,0:T(8,128)(2,1)} %collective-permute-done.3.refs_1_, bf16[2,2,64,256]{3,2,1,0:T(8,128)(2,1)} %get-tuple-element.59), kind=kLoop, calls=%fused_computation.2 | loop fusion | bytes 262144 | tf_op jit(solution)/shard_map/dynamic_update_slice | solution.py:316
  118.3 12.7 %collective-permute-done.4.refs_2_ = bf16[2,2,64,256]{3,2,1,0:T(8,128)(2,1)S(1)} collective-permute-done((bf16[2,2,64,256]{3,2,1,0:T(8,128)(2,1)}, bf16[2,2,64,256]{3,2,1,0:T(8,128)(2,1)S(1)}, u32[]{:S(2)}, u32[]{:S(2)}) %collective-permute-start.4) | collective-permute-done | bytes 131104 | tf_op jit(solution)/shard_map/ppermute | solution.py:311
  131.0 0.6 slice_dynamic-update-slice_fusion
  131.6 1.9 %collective-permute-start.6 = (bf16[3,2,64,256]{3,2,1,0:T(8,128)(2,1)}, bf16[3,2,64,256]{3,2,1,0:T(8,128)(2,1)S(1)}, u32[]{:S(2)}, u32[]{:S(2)}) collective-permute-start(bf16[3,2,64,256]{3,2,1,0:T(8,128)(2,1)} %slice_dynamic-update-slice_fusion), channel_id=1, source_target_pairs={{0,7},{1,0},{2,1},{3,2},{4,3},{5,4},{6,5},{7,6},{8,15},{9,8},{10,9... | collective-permute-start | bytes 589832 | tf_op jit(solution)/shard_map/ppermute | solution.py:311
  133.6 3.4 %collective-permute-start.5 = (bf16[2,2,64,256]{3,2,1,0:T(8,128)(2,1)}, bf16[2,2,64,256]{3,2,1,0:T(8,128)(2,1)S(1)}, u32[]{:S(2)}, u32[]{:S(2)}) collective-permute-start(bf16[2,2,64,256]{3,2,1,0:T(8,128)(2,1)} %get-tuple-element.62), channel_id=1, source_target_pairs={{0,1},{1,2},{2,3},{3,4},{4,5},{5,6},{6,7},{7,0},{8,9},{9,10},{10,1... | collective-permute-start | bytes 393224 | tf_op jit(solution)/shard_map/ppermute | solution.py:311
  136.9 3.8 %collective-permute-done.5.refs_3_ = bf16[2,2,64,256]{3,2,1,0:T(8,128)(2,1)S(1)} collective-permute-done((bf16[2,2,64,256]{3,2,1,0:T(8,128)(2,1)}, bf16[2,2,64,256]{3,2,1,0:T(8,128)(2,1)S(1)}, u32[]{:S(2)}, u32[]{:S(2)}) %collective-permute-start.5) | collective-permute-done | bytes 131104 | tf_op jit(solution)/shard_map/ppermute | solution.py:311
  140.7 0.0 collective-permute-done.6.refs_4_
  140.7 1.0 collect.1
  141.7 4.4 %collective-permute-start.7 = (bf16[8,64,256]{2,1,0:T(8,128)(2,1)S(1)}, bf16[8,64,256]{2,1,0:T(8,128)(2,1)S(1)}, u32[]{:S(2)}, u32[]{:S(2)}) collective-permute-start(bf16[8,64,256]{2,1,0:T(8,128)(2,1)S(1)} %collect.1), channel_id=1, source_target_pairs={{0,8},{8,0},{1,9},{9,1},{2,10},{10,2},{3,11},{11,3},{4,12},{12,4},... | collective-permute-start | bytes 786440 | tf_op jit(solution)/shard_map/ppermute | solution.py:242
  146.1 1.1 collective-permute-done.7.refs_5_
  147.2 1.8 %assemble_first.1.prev_ref = bf16[2,64,4096]{2,1,0:T(8,128)(2,1)} custom-call(s32[1]{0:T(128)} %bitcast.at.core_ref, s32[1]{0:T(128)} %bitcast.6.row_ref, bf16[1,2,64,256]{3,2,1,0:T(8,128)(2,1)} %get-tuple-element.56.refs_0_, bf16[3,2,64,256]{3,2,1,0:T(8,128)(2,1)} %collective-permute-done.3.refs_1_, ...), custom_call_target="tpu_custom_call" | custom-call | tf_op jit(solution)/shard_map/assemble_first/pallas_call | solution.py:335
  149.0 0.0 all-to-all-done.4.parts_ref
  149.0 0.8 assemble_second.1
Async XLA Ops:
  2.9 10.1 %collective-permute-start = (bf16[768,256]{1,0:T(8,128)(2,1)S(1)}, bf16[768,256]{1,0:T(8,128)(2,1)S(1)}, u32[]{:S(2)}, u32[]{:S(2)}) collective-permute-start(bf16[768,256]{1,0:T(8,128)(2,1)S(1)} %get-tuple-element.34), channel_id=1, source_target_pairs={{0,8},{8,0},{1,9},{9,1},{2,10},{10,2},{3,11},{11,3},{4,12},{12,4},... | collective-permute-start | bytes 1179656 | tf_op jit(solution)/shard_map/ppermute | solution.py:242
  16.8 22.1 %collective-permute-start.2 = (bf16[4,512,256]{2,1,0:T(8,128)(2,1)}, bf16[4,512,256]{2,1,0:T(8,128)(2,1)S(1)}, u32[]{:S(2)}, u32[]{:S(2)}) collective-permute-start(bf16[4,512,256]{2,1,0:T(8,128)(2,1)} %get-tuple-element.43), channel_id=1, source_target_pairs={{0,8},{8,0},{1,9},{9,1},{2,10},{10,2},{3,11},{11,3},{4,12},{12,4},... | collective-permute-start | bytes 3145736 | tf_op jit(solution)/shard_map/ppermute | solution.py:242
  19.1 19.7 %all-to-all-start = ((bf16[32,24,256]{2,1,0:T(8,128)(2,1)}), bf16[32,24,256]{2,1,0:T(8,128)(2,1)S(1)}, u32[]{:S(2)}, u32[]{:S(2)}) async-start(bf16[32,24,256]{2,1,0:T(8,128)(2,1)} %bitcast.1), calls=%async_computation | async-start | bytes 786432 | tf_op jit(solution)/shard_map/all_to_all | solution.py:218
  26.6 3.1 %collective-permute-start.1 = (f32[3,512]{1,0:T(4,128)S(1)}, f32[3,512]{1,0:T(4,128)S(1)}, u32[]{:S(2)}, u32[]{:S(2)}) collective-permute-start(f32[3,512]{1,0:T(4,128)S(1)} %get-tuple-element.41), channel_id=1, source_target_pairs={{0,8},{8,0},{1,9},{9,1},{2,10},{10,2},{3,11},{11,3},{4,12},{12,4},... | collective-permute-start | bytes 18440 | tf_op jit(solution)/shard_map/ppermute | solution.py:242
  78.6 0.7 copy-start.1
  79.3 18.1 %all-to-all-start.3 = ((bf16[32,24,256]{2,1,0:T(8,128)(2,1)}), bf16[32,24,256]{2,1,0:T(8,128)(2,1)S(1)}, u32[]{:S(2)}, u32[]{:S(2)}) async-start(bf16[32,24,256]{2,1,0:T(8,128)(2,1)} %copy-done.1), calls=%async_computation.3 | async-start | bytes 786432 | tf_op jit(solution)/shard_map/all_to_all | solution.py:218
  88.5 0.7 copy-start.2
  89.1 27.6 %collective-permute-start.3 = (bf16[3,2,64,256]{3,2,1,0:T(8,128)(2,1)}, bf16[3,2,64,256]{3,2,1,0:T(8,128)(2,1)}, u32[]{:S(2)}, u32[]{:S(2)}) collective-permute-start(bf16[3,2,64,256]{3,2,1,0:T(8,128)(2,1)} %get-tuple-element.57), channel_id=1, source_target_pairs={{0,3},{1,4},{2,5},{3,6},{4,7},{5,0},{6,1},{7,2},{8,11},{9,12},{10,... | collective-permute-start | bytes 589832 | tf_op jit(solution)/shard_map/ppermute | solution.py:311
  98.5 0.8 copy-start
  99.3 49.7 %all-to-all-start.4 = ((bf16[16,64,256]{2,1,0:T(8,128)(2,1)}), bf16[16,64,256]{2,1,0:T(8,128)(2,1)S(1)}, u32[]{:S(2)}, u32[]{:S(2)}) async-start(bf16[16,64,256]{2,1,0:T(8,128)(2,1)} %bitcast.7), calls=%async_computation.4 | async-start | bytes 1048576 | tf_op jit(solution)/shard_map/all_to_all | solution.py:218
  111.4 19.6 %collective-permute-start.4 = (bf16[2,2,64,256]{3,2,1,0:T(8,128)(2,1)}, bf16[2,2,64,256]{3,2,1,0:T(8,128)(2,1)S(1)}, u32[]{:S(2)}, u32[]{:S(2)}) collective-permute-start(bf16[2,2,64,256]{3,2,1,0:T(8,128)(2,1)} %copy-done.2), channel_id=1, source_target_pairs={{0,6},{1,7},{2,0},{3,1},{4,2},{5,3},{6,4},{7,5},{8,14},{9,15},{10,... | collective-permute-start | bytes 393224 | tf_op jit(solution)/shard_map/ppermute | solution.py:311
  131.6 9.1 %collective-permute-start.6 = (bf16[3,2,64,256]{3,2,1,0:T(8,128)(2,1)}, bf16[3,2,64,256]{3,2,1,0:T(8,128)(2,1)S(1)}, u32[]{:S(2)}, u32[]{:S(2)}) collective-permute-start(bf16[3,2,64,256]{3,2,1,0:T(8,128)(2,1)} %slice_dynamic-update-slice_fusion), channel_id=1, source_target_pairs={{0,7},{1,0},{2,1},{3,2},{4,3},{5,4},{6,5},{7,6},{8,15},{9,8},{10,9... | collective-permute-start | bytes 589832 | tf_op jit(solution)/shard_map/ppermute | solution.py:311
  133.6 7.1 %collective-permute-start.5 = (bf16[2,2,64,256]{3,2,1,0:T(8,128)(2,1)}, bf16[2,2,64,256]{3,2,1,0:T(8,128)(2,1)S(1)}, u32[]{:S(2)}, u32[]{:S(2)}) collective-permute-start(bf16[2,2,64,256]{3,2,1,0:T(8,128)(2,1)} %get-tuple-element.62), channel_id=1, source_target_pairs={{0,1},{1,2},{2,3},{3,4},{4,5},{5,6},{6,7},{7,0},{8,9},{9,10},{10,1... | collective-permute-start | bytes 393224 | tf_op jit(solution)/shard_map/ppermute | solution.py:311
  141.7 5.5 %collective-permute-start.7 = (bf16[8,64,256]{2,1,0:T(8,128)(2,1)S(1)}, bf16[8,64,256]{2,1,0:T(8,128)(2,1)S(1)}, u32[]{:S(2)}, u32[]{:S(2)}) collective-permute-start(bf16[8,64,256]{2,1,0:T(8,128)(2,1)S(1)} %collect.1), channel_id=1, source_target_pairs={{0,8},{8,0},{1,9},{9,1},{2,10},{10,2},{3,11},{11,3},{4,12},{12,4},... | collective-permute-start | bytes 786440 | tf_op jit(solution)/shard_map/ppermute | solution.py:242

commit v10 on v9

--- a/solution.py
+++ b/solution.py
@@ -24,7 +24,7 @@
     return jnp.mean(w * w, axis=1 if i == 2 else 0, keepdims=True)
 
 
-def gradients(keys, values, rate_gate, rate_up, rate_down, w_gate, w_up, w_down):
+def scaled_errors(keys, values, rate_gate, rate_up, rate_down, w_gate, w_up, w_down):
     gate = dot(w_gate, keys, NT)
     up = dot(w_up, keys, NT)
     err = dot(w_down, values, NT)
@@ -35,11 +35,12 @@
     gate_grad = err * up * sig * (1.0 + gate * (1.0 - sig))
     gate_scaled = (gate_grad * rate_gate).astype(bf16)
     up_scaled = (err * silu * rate_up).astype(bf16)
-    return (
-        dot(gate_scaled, keys, NN),
-        dot(up_scaled, keys, NN),
-        dot(scaled, values, NN),
-    )
+    return gate_scaled, up_scaled, scaled
+
+
+def gradients(keys, values, *rest):
+    gate_scaled, up_scaled, scaled = scaled_errors(keys, values, *rest)
+    return dot(gate_scaled, keys, NN), dot(up_scaled, keys, NN), dot(scaled, values, NN)
 
 
 def updated(state, targets, grad_ref):
@@ -69,7 +70,7 @@
 KEPT = (1032, 256)
 
 
-def second_kernel(init_ref, grad_ref, own_ref, other_ref, rates_own_ref, rates_other_ref, out_ref, kept_ref):
+def second_kernel(init_ref, grad_ref, own_ref, other_ref, rates_own_ref, rates_other_ref, out_ref, kept_ref, scratch, sems):
     init = [init_ref[i].astype(f32) for i in range(3)]
     targets = [jnp.sqrt(row_mean(w, i)) for i, w in enumerate(init)]
     state = updated(init, targets, grad_ref)
@@ -80,10 +81,20 @@
     kept_ref[1024:1025, :] = targets[0]
     kept_ref[1025:1026, :] = targets[1]
     kept_ref[1026:1032, :] = jnp.zeros((6, 256), f32)
-    own = gradients(own_ref[0], own_ref[1], *[rates_own_ref[i : i + 1, :] for i in range(3)], *weights)
-    other = gradients(other_ref[0], other_ref[1], *[rates_other_ref[i : i + 1, :] for i in range(3)], *weights)
+    halves = (
+        (own_ref[0], own_ref[1], [rates_own_ref[i : i + 1, :] for i in range(3)]),
+        (other_ref[0], other_ref[1], [rates_other_ref[i : i + 1, :] for i in range(3)]),
+    )
+    scaled = [scaled_errors(k, v, *rates, *weights) for k, v, rates in halves]
+    copies = []
     for i in range(3):
-        out_ref[256 * i : 256 * (i + 1), :] = (own[i] + other[i]).astype(bf16)
+        rows = slice(256 * i, 256 * (i + 1))
+        grad = sum(dot(scaled[h][i], halves[h][1 if i == 2 else 0], NN) for h in (0, 1))
+        scratch[rows, :] = grad.astype(bf16)
+        copies.append(pltpu.make_async_copy(scratch.at[rows], out_ref.at[rows], sems.at[i]))
+        copies[-1].start()
+    for copy in copies:
+        copy.wait()
 
 
 def state_of(kept_ref):
@@ -128,12 +139,17 @@
             out_ref[i] = scratch[lax.rem(row_ref[0] + ROWS + d, ROWS)]
 
 
-def last_kernel(at, kept_ref, grad_ref, own_ref, other_ref, out_ref):
+def last_kernel(at, kept_ref, grad_ref, own_ref, other_ref, out_ref, scratch, sems):
     targets = [kept_ref[1024:1025, :], kept_ref[1025:1026, :], kept_ref[768:1024, :]]
     state = updated(state_of(kept_ref), targets, grad_ref)
     weights = [w.astype(bf16) for w in state]
-    for q, core in ((own_ref[2], at[0]), (other_ref[2], 1 - at[0])):
-        out_ref[:, pl.ds(core, 1)] = applied(q, weights).reshape(ROWS, 1, 64, 256)
+    copies = []
+    for side, (q, core) in enumerate(((own_ref[2], at[0]), (other_ref[2], 1 - at[0]))):
+        scratch[side] = applied(q, weights).reshape(ROWS, 64, 256)
+        copies.append(pltpu.make_async_copy(scratch.at[side], out_ref.at[:, core], sems.at[side]))
+        copies[-1].start()
+    for copy in copies:
+        copy.wait()
 
 
 def total_with_rates_kernel(parts_ref, rates_ref, out_ref, rates_out_ref):
@@ -286,7 +302,8 @@
     second, kept = pl.pallas_call(
         second_kernel,
         in_specs=[VMEM] * 6,
-        out_specs=[VMEM] * 2,
+        out_specs=[ANY, VMEM],
+        scratch_shapes=[pltpu.VMEM((768, 256), bf16), pltpu.SemaphoreType.DMA((3,))],
         out_shape=[
             pltpu.HBM((768, 256), bf16),
             jax.ShapeDtypeStruct(KEPT, f32),
@@ -318,8 +335,14 @@
 
     total = scattered(second)
     summed = gathered(total)
-    result = call(
-        last_kernel, [VMEM, VMEM, VMEM, VMEM], [((ROWS, 2, 64, 256), bf16)]
+    result = pl.pallas_call(
+        last_kernel,
+        in_specs=[SCALARS] + [VMEM] * 4,
+        out_specs=ANY,
+        out_shape=pltpu.HBM((ROWS, 2, 64, 256), bf16),
+        scratch_shapes=[pltpu.VMEM((2, ROWS, 64, 256), bf16), pltpu.SemaphoreType.DMA((2,))],
+        name="apply_second",
+        compiler_params=LIMIT,
     )(at, on_chip(kept), summed, on_chip(own), on_chip(other))
     parts = exchange(result.reshape(16, 64, 256), ("y", "c"))
     got = [off_chip(here)] + [on_chip(a) for a in (far_ahead, far_behind, ahead, behind)]

time: 151 us -> 151 us (level)
  no operation moved by 1% of the time
where the time goes in v10:
time: 151 us; the launch traced here: 150 us
  starting transfers between devices  60.8 us (40%)
  blocking collectives  37.1 us (25%)
  waiting for transfers between devices  31.9 us (21%)
  Pallas kernels  15.4 us (10%)
  local copies, waits for them, and re-layouts  3.53 us (2%)
    all_to_all x2, blocking collectives, exchange(): return lax.all_to_all(array, axes, split_axis=0, concat_axis=0, tiled=True)  37.1 us
    all_to_all x3, starting transfers between devices, exchange(): return lax.all_to_all(array, axes, split_axis=0, concat_axis=0, tiled=True)  27.2 us
    ppermute x4, starting transfers between devices, swapped(): return lax.ppermute(array, 'c', [(0, 1), (1, 0)])  17.7 us
    ppermute x4, waiting for transfers between devices, sent(): lax.ppermute(array, 'y', [(j, (j + step) % ROWS) for j in range(ROWS)])  16.5 us
    ppermute x4, starting transfers between devices, sent(): lax.ppermute(array, 'y', [(j, (j + step) % ROWS) for j in range(ROWS)])  15.9 us
    all_to_all x3, waiting for transfers between devices, exchange(): return lax.all_to_all(array, axes, split_axis=0, concat_axis=0, tiled=True)  12.1 us
    ppermute x4, waiting for transfers between devices, swapped(): return lax.ppermute(array, 'c', [(0, 1), (1, 0)])  3.28 us
  transfers between devices with their start and end apart: 11, of which 7 were waited for; matrix products, arithmetic and copies ran while one was open for 1% of the time, Pallas kernels for 4%

profile of v10, /device:TPU:1, one launch (start us, length us, event | category | flops | bytes accessed | tf_op | source)
XLA Modules:
  0.0 149.7 jit_solution(1298332054846254049)
XLA Ops:
  0.0 2.9 %shard_map.55 = (bf16[768,256]{1,0:T(8,128)(2,1)S(1)}, f32[768,256]{1,0:T(8,128)S(1)}) custom-call(s32[1]{0:T(128)} %bitcast.at.core_ref, bf16[3,2,256,256]{3,2,1,0:T(8,128)(2,1)} %init_ref.2, bf16[2,512,512]{2,1,0:T(8,128)(2,1)} %k_ref.2, bf16[2,512,512]{2,1,0:T(8,128)(2,1)} %v_ref.2, f32[3,2,2,512]{3,2,1,0:T(2,128)} %rates_ref.2), custom_call_target="tpu_custom_call" | custom-call | tf_op jit(solution)/shard_map/pallas_call | solution.py:266
  2.9 8.8 %collective-permute-start = (bf16[768,256]{1,0:T(8,128)(2,1)S(1)}, bf16[768,256]{1,0:T(8,128)(2,1)S(1)}, u32[]{:S(2)}, u32[]{:S(2)}) collective-permute-start(bf16[768,256]{1,0:T(8,128)(2,1)S(1)} %get-tuple-element.34), channel_id=1, source_target_pairs={{0,8},{8,0},{1,9},{9,1},{2,10},{10,2},{3,11},{11,3},{4,12},{12,4},... | collective-permute-start | bytes 1179656 | tf_op jit(solution)/shard_map/ppermute | solution.py:258
  11.7 1.3 collective-permute-done
  13.0 0.8 add_convert_fusion
  13.9 2.9 %shard_map.56 = (bf16[4,512,256]{2,1,0:T(8,128)(2,1)S(1)}, bf16[4,512,256]{2,1,0:T(8,128)(2,1)}, bf16[3,256,256]{2,1,0:T(8,128)(2,1)S(1)}, f32[3,512]{1,0:T(4,128)S(1)}, f32[3,512]{1,0:T(4,128)S(1)}) custom-call(s32[1]{0:T(128)} %bitcast.at.core_ref, bf16[2,512,512]{2,1,0:T(8,128)(2,1)} %k_ref.2, bf16[2,512,512]{2,1,0:T(8,128)(2,1)} %v_ref.2, ...), custom_call_target="tpu_custom_call" | custom-call | tf_op jit(solution)/shard_map/pallas_call | solution.py:283
  16.8 2.3 %collective-permute-start.2 = (bf16[4,512,256]{2,1,0:T(8,128)(2,1)}, bf16[4,512,256]{2,1,0:T(8,128)(2,1)S(1)}, u32[]{:S(2)}, u32[]{:S(2)}) collective-permute-start(bf16[4,512,256]{2,1,0:T(8,128)(2,1)} %get-tuple-element.43), channel_id=1, source_target_pairs={{0,8},{8,0},{1,9},{9,1},{2,10},{10,2},{3,11},{11,3},{4,12},{12,4},... | collective-permute-start | bytes 3145736 | tf_op jit(solution)/shard_map/ppermute | solution.py:258
  19.1 7.6 %all-to-all-start = ((bf16[32,24,256]{2,1,0:T(8,128)(2,1)}), bf16[32,24,256]{2,1,0:T(8,128)(2,1)S(1)}, u32[]{:S(2)}, u32[]{:S(2)}) async-start(bf16[32,24,256]{2,1,0:T(8,128)(2,1)} %bitcast.1), calls=%async_computation | async-start | bytes 786432 | tf_op jit(solution)/shard_map/all_to_all | solution.py:234
  26.6 2.3 %collective-permute-start.1 = (f32[3,512]{1,0:T(4,128)S(1)}, f32[3,512]{1,0:T(4,128)S(1)}, u32[]{:S(2)}, u32[]{:S(2)}) collective-permute-start(f32[3,512]{1,0:T(4,128)S(1)} %get-tuple-element.41), channel_id=1, source_target_pairs={{0,8},{8,0},{1,9},{9,1},{2,10},{10,2},{3,11},{11,3},{4,12},{12,4},... | collective-permute-start | bytes 18440 | tf_op jit(solution)/shard_map/ppermute | solution.py:258
  29.0 0.8 collective-permute-done.1.rates_ref
  29.8 9.0 %all-to-all-done.parts_ref = bf16[32,24,256]{2,1,0:T(8,128)(2,1)S(1)} async-done(((bf16[32,24,256]{2,1,0:T(8,128)(2,1)}), bf16[32,24,256]{2,1,0:T(8,128)(2,1)S(1)}, u32[]{:S(2)}, u32[]{:S(2)}) %all-to-all-start) | async-done | bytes 393248 | tf_op jit(solution)/shard_map/all_to_all | solution.py:234
  38.8 0.1 total.2
  38.9 0.0 collective-permute-done.2.other_ref
  38.9 18.8 %all_to_all.25 = bf16[32,24,256]{2,1,0:T(8,128)(2,1)S(1)} all-to-all(bf16[32,24,256]{2,1,0:T(8,128)(2,1)S(1)} %get-tuple-element.49), channel_id=1, replica_groups=mesh['x'=4,'z'=8,'c'=2,'y'=8] {'x','z'}, dimensions={0} | all-to-all | bytes 786432 | tf_op jit(solution)/shard_map/all_to_all | solution.py:234
  57.7 2.4 %second.1 = (bf16[768,256]{1,0:T(8,128)(2,1)}, f32[1032,256]{1,0:T(8,128)S(1)}) custom-call(bf16[3,256,256]{2,1,0:T(8,128)(2,1)S(1)} %get-tuple-element.48.init_ref, bf16[768,256]{1,0:T(8,128)(2,1)S(1)} %bitcast.8, bf16[4,512,256]{2,1,0:T(8,128)(2,1)S(1)} %get-tuple-element.50.own_ref, bf16[4,512,256]{2,1,0:T(8,128)(2,1)S(1)} %collective-permute-done.2.other_ref, ...), custom_call_target="tpu_custom_call" | custom-call | tf_op jit(solution)/shard_map/second/pallas_call | solution.py:302
  60.1 18.3 %all_to_all.26.parts_ref = bf16[32,24,256]{2,1,0:T(8,128)(2,1)S(1)} all-to-all(bf16[32,24,256]{2,1,0:T(8,128)(2,1)} %bitcast.10), channel_id=1, replica_groups=mesh['x'=4,'z'=8,'c'=2,'y'=8] {'x','z'}, dimensions={0} | all-to-all | bytes 786432 | tf_op jit(solution)/shard_map/all_to_all | solution.py:234
  78.4 0.1 total.3
  78.5 0.0 copy-start
  78.5 0.7 copy-done
  79.3 7.6 %all-to-all-start.3 = ((bf16[32,24,256]{2,1,0:T(8,128)(2,1)}), bf16[32,24,256]{2,1,0:T(8,128)(2,1)S(1)}, u32[]{:S(2)}, u32[]{:S(2)}) async-start(bf16[32,24,256]{2,1,0:T(8,128)(2,1)} %copy-done), calls=%async_computation.3 | async-start | bytes 786432 | tf_op jit(solution)/shard_map/all_to_all | solution.py:234
  86.8 1.6 %apply_first.1 = (bf16[3,2,64,256]{3,2,1,0:T(8,128)(2,1)}, bf16[2,2,64,256]{3,2,1,0:T(8,128)(2,1)S(1)}, bf16[2,2,64,256]{3,2,1,0:T(8,128)(2,1)}, bf16[3,2,64,256]{3,2,1,0:T(8,128)(2,1)}, bf16[1,2,64,256]{3,2,1,0:T(8,128)(2,1)}) custom-call(s32[1]{0:T(128)} %bitcast.6.row_ref, f32[1032,256]{1,0:T(8,128)S(1)} %get-tuple-element.54.kept_ref, ...), custom_call_target="tpu_custom_call" | custom-call | tf_op jit(solution)/shard_map/apply_first/pallas_call | solution.py:315
  88.4 0.0 copy-start.1
  88.4 0.6 copy-done.1
  89.0 5.2 %collective-permute-start.3 = (bf16[3,2,64,256]{3,2,1,0:T(8,128)(2,1)}, bf16[3,2,64,256]{3,2,1,0:T(8,128)(2,1)}, u32[]{:S(2)}, u32[]{:S(2)}) collective-permute-start(bf16[3,2,64,256]{3,2,1,0:T(8,128)(2,1)} %get-tuple-element.57), channel_id=1, source_target_pairs={{0,3},{1,4},{2,5},{3,6},{4,7},{5,0},{6,1},{7,2},{8,11},{9,12},{10,... | collective-permute-start | bytes 589832 | tf_op jit(solution)/shard_map/ppermute | solution.py:328
  94.3 3.1 %all-to-all-done.3 = bf16[32,24,256]{2,1,0:T(8,128)(2,1)S(1)} async-done(((bf16[32,24,256]{2,1,0:T(8,128)(2,1)}), bf16[32,24,256]{2,1,0:T(8,128)(2,1)S(1)}, u32[]{:S(2)}, u32[]{:S(2)}) %all-to-all-start.3) | async-done | bytes 393248 | tf_op jit(solution)/shard_map/all_to_all | solution.py:234
  97.3 1.8 %apply_second.1 = bf16[8,2,64,256]{3,2,1,0:T(8,128)(2,1)} custom-call(s32[1]{0:T(128)} %bitcast.at.core_ref, f32[1032,256]{1,0:T(8,128)S(1)} %get-tuple-element.54.kept_ref, bf16[768,256]{1,0:T(8,128)(2,1)S(1)} %bitcast.7, bf16[4,512,256]{2,1,0:T(8,128)(2,1)S(1)} %get-tuple-element.50.own_ref, bf16[4,512,256]{2,1,0:T(8,128)(2,1)S(1)} %collective-permute-done.2.other_ref), custom_call_target="tpu_custom_call" | custom-call | tf_op jit(solution)/shard_map/apply_second/pallas_call | solution.py:338
  99.2 12.1 %all-to-all-start.4 = ((bf16[16,64,256]{2,1,0:T(8,128)(2,1)}), bf16[16,64,256]{2,1,0:T(8,128)(2,1)S(1)}, u32[]{:S(2)}, u32[]{:S(2)}) async-start(bf16[16,64,256]{2,1,0:T(8,128)(2,1)} %bitcast.9), calls=%async_computation.4 | async-start | bytes 1048576 | tf_op jit(solution)/shard_map/all_to_all | solution.py:234
  111.3 5.4 %collective-permute-start.4 = (bf16[2,2,64,256]{3,2,1,0:T(8,128)(2,1)}, bf16[2,2,64,256]{3,2,1,0:T(8,128)(2,1)S(1)}, u32[]{:S(2)}, u32[]{:S(2)}) collective-permute-start(bf16[2,2,64,256]{3,2,1,0:T(8,128)(2,1)} %copy-done.1), channel_id=1, source_target_pairs={{0,6},{1,7},{2,0},{3,1},{4,2},{5,3},{6,4},{7,5},{8,14},{9,15},{10,... | collective-permute-start | bytes 393224 | tf_op jit(solution)/shard_map/ppermute | solution.py:328
  116.6 0.0 collective-permute-done.3.refs_1_
  116.6 1.5 %slice_dynamic-update-slice_fusion.1 = (bf16[3,2,64,256]{3,2,1,0:T(8,128)(2,1)}, bf16[2,2,64,256]{3,2,1,0:T(8,128)(2,1)}) fusion(bf16[3,2,64,256]{3,2,1,0:T(8,128)(2,1)} %get-tuple-element.60, bf16[3,2,64,256]{3,2,1,0:T(8,128)(2,1)} %collective-permute-done.3.refs_1_, bf16[2,2,64,256]{3,2,1,0:T(8,128)(2,1)} %get-tuple-element.59), kind=kLoop, calls=%fused_computation.2 | loop fusion | bytes 262144 | tf_op jit(solution)/shard_map/dynamic_update_slice | solution.py:333
  118.2 12.7 %collective-permute-done.4.refs_2_ = bf16[2,2,64,256]{3,2,1,0:T(8,128)(2,1)S(1)} collective-permute-done((bf16[2,2,64,256]{3,2,1,0:T(8,128)(2,1)}, bf16[2,2,64,256]{3,2,1,0:T(8,128)(2,1)S(1)}, u32[]{:S(2)}, u32[]{:S(2)}) %collective-permute-start.4) | collective-permute-done | bytes 131104 | tf_op jit(solution)/shard_map/ppermute | solution.py:328
  130.9 0.6 slice_dynamic-update-slice_fusion
  131.5 1.9 %collective-permute-start.6 = (bf16[3,2,64,256]{3,2,1,0:T(8,128)(2,1)}, bf16[3,2,64,256]{3,2,1,0:T(8,128)(2,1)S(1)}, u32[]{:S(2)}, u32[]{:S(2)}) collective-permute-start(bf16[3,2,64,256]{3,2,1,0:T(8,128)(2,1)} %slice_dynamic-update-slice_fusion), channel_id=1, source_target_pairs={{0,7},{1,0},{2,1},{3,2},{4,3},{5,4},{6,5},{7,6},{8,15},{9,8},{10,9... | collective-permute-start | bytes 589832 | tf_op jit(solution)/shard_map/ppermute | solution.py:328
  133.4 3.4 %collective-permute-start.5 = (bf16[2,2,64,256]{3,2,1,0:T(8,128)(2,1)}, bf16[2,2,64,256]{3,2,1,0:T(8,128)(2,1)S(1)}, u32[]{:S(2)}, u32[]{:S(2)}) collective-permute-start(bf16[2,2,64,256]{3,2,1,0:T(8,128)(2,1)} %get-tuple-element.62), channel_id=1, source_target_pairs={{0,1},{1,2},{2,3},{3,4},{4,5},{5,6},{6,7},{7,0},{8,9},{9,10},{10,1... | collective-permute-start | bytes 393224 | tf_op jit(solution)/shard_map/ppermute | solution.py:328
  136.8 3.8 %collective-permute-done.5.refs_3_ = bf16[2,2,64,256]{3,2,1,0:T(8,128)(2,1)S(1)} collective-permute-done((bf16[2,2,64,256]{3,2,1,0:T(8,128)(2,1)}, bf16[2,2,64,256]{3,2,1,0:T(8,128)(2,1)S(1)}, u32[]{:S(2)}, u32[]{:S(2)}) %collective-permute-start.5) | collective-permute-done | bytes 131104 | tf_op jit(solution)/shard_map/ppermute | solution.py:328
  140.6 0.0 collective-permute-done.6.refs_4_
  140.6 1.0 collect.1
  141.6 4.4 %collective-permute-start.7 = (bf16[8,64,256]{2,1,0:T(8,128)(2,1)S(1)}, bf16[8,64,256]{2,1,0:T(8,128)(2,1)S(1)}, u32[]{:S(2)}, u32[]{:S(2)}) collective-permute-start(bf16[8,64,256]{2,1,0:T(8,128)(2,1)S(1)} %collect.1), channel_id=1, source_target_pairs={{0,8},{8,0},{1,9},{9,1},{2,10},{10,2},{3,11},{11,3},{4,12},{12,4},... | collective-permute-start | bytes 786440 | tf_op jit(solution)/shard_map/ppermute | solution.py:258
  145.9 1.1 collective-permute-done.7.refs_5_
  147.1 1.8 %assemble_first.1.prev_ref = bf16[2,64,4096]{2,1,0:T(8,128)(2,1)} custom-call(s32[1]{0:T(128)} %bitcast.at.core_ref, s32[1]{0:T(128)} %bitcast.6.row_ref, bf16[1,2,64,256]{3,2,1,0:T(8,128)(2,1)} %get-tuple-element.56.refs_0_, bf16[3,2,64,256]{3,2,1,0:T(8,128)(2,1)} %collective-permute-done.3.refs_1_, ...), custom_call_target="tpu_custom_call" | custom-call | tf_op jit(solution)/shard_map/assemble_first/pallas_call | solution.py:358
  148.9 0.0 all-to-all-done.4.parts_ref
  148.9 0.8 assemble_second.1
Async XLA Ops:
  2.9 10.1 %collective-permute-start = (bf16[768,256]{1,0:T(8,128)(2,1)S(1)}, bf16[768,256]{1,0:T(8,128)(2,1)S(1)}, u32[]{:S(2)}, u32[]{:S(2)}) collective-permute-start(bf16[768,256]{1,0:T(8,128)(2,1)S(1)} %get-tuple-element.34), channel_id=1, source_target_pairs={{0,8},{8,0},{1,9},{9,1},{2,10},{10,2},{3,11},{11,3},{4,12},{12,4},... | collective-permute-start | bytes 1179656 | tf_op jit(solution)/shard_map/ppermute | solution.py:258
  16.8 22.1 %collective-permute-start.2 = (bf16[4,512,256]{2,1,0:T(8,128)(2,1)}, bf16[4,512,256]{2,1,0:T(8,128)(2,1)S(1)}, u32[]{:S(2)}, u32[]{:S(2)}) collective-permute-start(bf16[4,512,256]{2,1,0:T(8,128)(2,1)} %get-tuple-element.43), channel_id=1, source_target_pairs={{0,8},{8,0},{1,9},{9,1},{2,10},{10,2},{3,11},{11,3},{4,12},{12,4},... | collective-permute-start | bytes 3145736 | tf_op jit(solution)/shard_map/ppermute | solution.py:258
  19.1 19.7 %all-to-all-start = ((bf16[32,24,256]{2,1,0:T(8,128)(2,1)}), bf16[32,24,256]{2,1,0:T(8,128)(2,1)S(1)}, u32[]{:S(2)}, u32[]{:S(2)}) async-start(bf16[32,24,256]{2,1,0:T(8,128)(2,1)} %bitcast.1), calls=%async_computation | async-start | bytes 786432 | tf_op jit(solution)/shard_map/all_to_all | solution.py:234
  26.6 3.1 %collective-permute-start.1 = (f32[3,512]{1,0:T(4,128)S(1)}, f32[3,512]{1,0:T(4,128)S(1)}, u32[]{:S(2)}, u32[]{:S(2)}) collective-permute-start(f32[3,512]{1,0:T(4,128)S(1)} %get-tuple-element.41), channel_id=1, source_target_pairs={{0,8},{8,0},{1,9},{9,1},{2,10},{10,2},{3,11},{11,3},{4,12},{12,4},... | collective-permute-start | bytes 18440 | tf_op jit(solution)/shard_map/ppermute | solution.py:258
  78.5 0.7 copy-start
  79.3 18.1 %all-to-all-start.3 = ((bf16[32,24,256]{2,1,0:T(8,128)(2,1)}), bf16[32,24,256]{2,1,0:T(8,128)(2,1)S(1)}, u32[]{:S(2)}, u32[]{:S(2)}) async-start(bf16[32,24,256]{2,1,0:T(8,128)(2,1)} %copy-done), calls=%async_computation.3 | async-start | bytes 786432 | tf_op jit(solution)/shard_map/all_to_all | solution.py:234
  88.4 0.7 copy-start.1
  89.0 27.6 %collective-permute-start.3 = (bf16[3,2,64,256]{3,2,1,0:T(8,128)(2,1)}, bf16[3,2,64,256]{3,2,1,0:T(8,128)(2,1)}, u32[]{:S(2)}, u32[]{:S(2)}) collective-permute-start(bf16[3,2,64,256]{3,2,1,0:T(8,128)(2,1)} %get-tuple-element.57), channel_id=1, source_target_pairs={{0,3},{1,4},{2,5},{3,6},{4,7},{5,0},{6,1},{7,2},{8,11},{9,12},{10,... | collective-permute-start | bytes 589832 | tf_op jit(solution)/shard_map/ppermute | solution.py:328
  99.2 49.7 %all-to-all-start.4 = ((bf16[16,64,256]{2,1,0:T(8,128)(2,1)}), bf16[16,64,256]{2,1,0:T(8,128)(2,1)S(1)}, u32[]{:S(2)}, u32[]{:S(2)}) async-start(bf16[16,64,256]{2,1,0:T(8,128)(2,1)} %bitcast.9), calls=%async_computation.4 | async-start | bytes 1048576 | tf_op jit(solution)/shard_map/all_to_all | solution.py:234
  111.3 19.6 %collective-permute-start.4 = (bf16[2,2,64,256]{3,2,1,0:T(8,128)(2,1)}, bf16[2,2,64,256]{3,2,1,0:T(8,128)(2,1)S(1)}, u32[]{:S(2)}, u32[]{:S(2)}) collective-permute-start(bf16[2,2,64,256]{3,2,1,0:T(8,128)(2,1)} %copy-done.1), channel_id=1, source_target_pairs={{0,6},{1,7},{2,0},{3,1},{4,2},{5,3},{6,4},{7,5},{8,14},{9,15},{10,... | collective-permute-start | bytes 393224 | tf_op jit(solution)/shard_map/ppermute | solution.py:328
  131.5 9.1 %collective-permute-start.6 = (bf16[3,2,64,256]{3,2,1,0:T(8,128)(2,1)}, bf16[3,2,64,256]{3,2,1,0:T(8,128)(2,1)S(1)}, u32[]{:S(2)}, u32[]{:S(2)}) collective-permute-start(bf16[3,2,64,256]{3,2,1,0:T(8,128)(2,1)} %slice_dynamic-update-slice_fusion), channel_id=1, source_target_pairs={{0,7},{1,0},{2,1},{3,2},{4,3},{5,4},{6,5},{7,6},{8,15},{9,8},{10,9... | collective-permute-start | bytes 589832 | tf_op jit(solution)/shard_map/ppermute | solution.py:328
  133.4 7.1 %collective-permute-start.5 = (bf16[2,2,64,256]{3,2,1,0:T(8,128)(2,1)}, bf16[2,2,64,256]{3,2,1,0:T(8,128)(2,1)S(1)}, u32[]{:S(2)}, u32[]{:S(2)}) collective-permute-start(bf16[2,2,64,256]{3,2,1,0:T(8,128)(2,1)} %get-tuple-element.62), channel_id=1, source_target_pairs={{0,1},{1,2},{2,3},{3,4},{4,5},{5,6},{6,7},{7,0},{8,9},{9,10},{10,1... | collective-permute-start | bytes 393224 | tf_op jit(solution)/shard_map/ppermute | solution.py:328
  141.6 5.5 %collective-permute-start.7 = (bf16[8,64,256]{2,1,0:T(8,128)(2,1)S(1)}, bf16[8,64,256]{2,1,0:T(8,128)(2,1)S(1)}, u32[]{:S(2)}, u32[]{:S(2)}) collective-permute-start(bf16[8,64,256]{2,1,0:T(8,128)(2,1)S(1)} %collect.1), channel_id=1, source_target_pairs={{0,8},{8,0},{1,9},{9,1},{2,10},{10,2},{3,11},{11,3},{4,12},{12,4},... | collective-permute-start | bytes 786440 | tf_op jit(solution)/shard_map/ppermute | solution.py:258

commit v11 on v9

--- a/solution.py
+++ b/solution.py
@@ -133,7 +133,7 @@
     state = updated(state_of(kept_ref), targets, grad_ref)
     weights = [w.astype(bf16) for w in state]
     for q, core in ((own_ref[2], at[0]), (other_ref[2], 1 - at[0])):
-        out_ref[:, pl.ds(core, 1)] = applied(q, weights).reshape(ROWS, 1, 64, 256)
+        out_ref[core] = applied(q, weights).reshape(ROWS, 64, 256)
 
 
 def total_with_rates_kernel(parts_ref, rates_ref, out_ref, rates_out_ref):
@@ -177,7 +177,7 @@
 def assemble_second_kernel(parts_ref, prev_ref, out_ref):
     rows = pl.ds(pl.program_id(0) * 32, 32)
     for head in range(16):
-        out_ref[0, :, 256 * head : 256 * (head + 1)] = parts_ref[head, rows]
+        out_ref[0, :, 256 * head : 256 * (head + 1)] = parts_ref[ROWS * (head % 2) + head // 2, rows]
 
 
 def whole(shape):
@@ -219,7 +219,7 @@
 
 
 def scattered(partial, rates=None):
-    parts = exchange(partial.reshape(32, 24, 256), ("x", "z"))
+    parts = exchange(partial.reshape(32, 24, 256), ("z", "x"))
     args = [on_chip(parts)] if rates is None else [on_chip(parts), on_chip(rates)]
     shapes = [jax.ShapeDtypeStruct((32, 24, 256), bf16), jax.ShapeDtypeStruct((3, 512), f32)][: len(args)]
     result = pl.pallas_call(
@@ -234,7 +234,7 @@
 
 
 def gathered(total):
-    full = exchange(total, ("x", "z"))
+    full = exchange(total, ("z", "x"))
     return on_chip(full.reshape(768, 256))
 
 
@@ -319,9 +319,9 @@
     total = scattered(second)
     summed = gathered(total)
     result = call(
-        last_kernel, [VMEM, VMEM, VMEM, VMEM], [((ROWS, 2, 64, 256), bf16)]
+        last_kernel, [VMEM, VMEM, VMEM, VMEM], [((2, ROWS, 64, 256), bf16)]
     )(at, on_chip(kept), summed, on_chip(own), on_chip(other))
-    parts = exchange(result.reshape(16, 64, 256), ("y", "c"))
+    parts = exchange(result.reshape(16, 64, 256), ("c", "y"))
     got = [off_chip(here)] + [on_chip(a) for a in (far_ahead, far_behind, ahead, behind)]
     halves = pl.pallas_call(
         collect_kernel,

time: 151 us -> 150 us (level)
  waiting for transfers between devices: 31.9 us -> 36.5 us
  starting transfers between devices: 60.7 us -> 57.2 us
    all_to_all x3, waiting for transfers between devices: 12.1 us -> 16.4 us  [exchange(): return lax.all_to_all(array, axes, split_axis=0, concat_axis=0, tiled=True)]
    all_to_all x3, starting transfers between devices: 27.2 us -> 23.9 us  [exchange(): return lax.all_to_all(array, axes, split_axis=0, concat_axis=0, tiled=True)]
where the time goes in v11:
time: 150 us
  starting transfers between devices  57.2 us (38%)
  waiting for transfers between devices  36.5 us (24%)
  blocking collectives  35.8 us (24%)
  Pallas kernels  14.8 us (10%)
  local copies, waits for them, and re-layouts  4.37 us (3%)
    all_to_all x2, blocking collectives, exchange(): return lax.all_to_all(array, axes, split_axis=0, concat_axis=0, tiled=True)  35.8 us
    all_to_all x3, starting transfers between devices, exchange(): return lax.all_to_all(array, axes, split_axis=0, concat_axis=0, tiled=True)  23.9 us
    ppermute x4, starting transfers between devices, swapped(): return lax.ppermute(array, 'c', [(0, 1), (1, 0)])  17.5 us
    ppermute x4, waiting for transfers between devices, sent(): lax.ppermute(array, 'y', [(j, (j + step) % ROWS) for j in range(ROWS)])  16.9 us
    all_to_all x3, waiting for transfers between devices, exchange(): return lax.all_to_all(array, axes, split_axis=0, concat_axis=0, tiled=True)  16.4 us
    ppermute x4, starting transfers between devices, sent(): lax.ppermute(array, 'y', [(j, (j + step) % ROWS) for j in range(ROWS)])  15.9 us
    ppermute x4, waiting for transfers between devices, swapped(): return lax.ppermute(array, 'c', [(0, 1), (1, 0)])  3.28 us
  transfers between devices with their start and end apart: 11, of which 7 were waited for; matrix products, arithmetic and copies ran while one was open for 1% of the time, Pallas kernels for 4%

profile of v11, /device:TPU:1, one launch (start us, length us, event | category | flops | bytes accessed | tf_op | source)
XLA Modules:
  0.0 149.6 jit_solution(10433667658969655139)
XLA Ops:
  0.0 2.9 %shard_map.55 = (bf16[768,256]{1,0:T(8,128)(2,1)S(1)}, f32[768,256]{1,0:T(8,128)S(1)}) custom-call(s32[1]{0:T(128)} %bitcast.at.core_ref, bf16[3,2,256,256]{3,2,1,0:T(8,128)(2,1)} %init_ref.2, bf16[2,512,512]{2,1,0:T(8,128)(2,1)} %k_ref.2, bf16[2,512,512]{2,1,0:T(8,128)(2,1)} %v_ref.2, f32[3,2,2,512]{3,2,1,0:T(2,128)} %rates_ref.2), custom_call_target="tpu_custom_call" | custom-call | tf_op jit(solution)/shard_map/pallas_call | solution.py:250
  2.9 8.8 %collective-permute-start = (bf16[768,256]{1,0:T(8,128)(2,1)S(1)}, bf16[768,256]{1,0:T(8,128)(2,1)S(1)}, u32[]{:S(2)}, u32[]{:S(2)}) collective-permute-start(bf16[768,256]{1,0:T(8,128)(2,1)S(1)} %get-tuple-element.34), channel_id=1, source_target_pairs={{0,8},{8,0},{1,9},{9,1},{2,10},{10,2},{3,11},{11,3},{4,12},{12,4},... | collective-permute-start | bytes 1179656 | tf_op jit(solution)/shard_map/ppermute | solution.py:242
  11.7 1.3 collective-permute-done
  13.0 0.8 add_convert_fusion
  13.9 2.9 %shard_map.56 = (bf16[4,512,256]{2,1,0:T(8,128)(2,1)S(1)}, bf16[4,512,256]{2,1,0:T(8,128)(2,1)}, bf16[3,256,256]{2,1,0:T(8,128)(2,1)S(1)}, f32[3,512]{1,0:T(4,128)S(1)}, f32[3,512]{1,0:T(4,128)S(1)}) custom-call(s32[1]{0:T(128)} %bitcast.at.core_ref, bf16[2,512,512]{2,1,0:T(8,128)(2,1)} %k_ref.2, bf16[2,512,512]{2,1,0:T(8,128)(2,1)} %v_ref.2, ...), custom_call_target="tpu_custom_call" | custom-call | tf_op jit(solution)/shard_map/pallas_call | solution.py:267
  16.8 2.3 %collective-permute-start.2 = (bf16[4,512,256]{2,1,0:T(8,128)(2,1)}, bf16[4,512,256]{2,1,0:T(8,128)(2,1)S(1)}, u32[]{:S(2)}, u32[]{:S(2)}) collective-permute-start(bf16[4,512,256]{2,1,0:T(8,128)(2,1)} %get-tuple-element.43), channel_id=1, source_target_pairs={{0,8},{8,0},{1,9},{9,1},{2,10},{10,2},{3,11},{11,3},{4,12},{12,4},... | collective-permute-start | bytes 3145736 | tf_op jit(solution)/shard_map/ppermute | solution.py:242
  19.1 7.6 %all-to-all-start = ((bf16[32,24,256]{2,1,0:T(8,128)(2,1)}), bf16[32,24,256]{2,1,0:T(8,128)(2,1)S(1)}, u32[]{:S(2)}, u32[]{:S(2)}) async-start(bf16[32,24,256]{2,1,0:T(8,128)(2,1)} %bitcast.1), calls=%async_computation | async-start | bytes 786432 | tf_op jit(solution)/shard_map/all_to_all | solution.py:218
  26.6 2.3 %collective-permute-start.1 = (f32[3,512]{1,0:T(4,128)S(1)}, f32[3,512]{1,0:T(4,128)S(1)}, u32[]{:S(2)}, u32[]{:S(2)}) collective-permute-start(f32[3,512]{1,0:T(4,128)S(1)} %get-tuple-element.41), channel_id=1, source_target_pairs={{0,8},{8,0},{1,9},{9,1},{2,10},{10,2},{3,11},{11,3},{4,12},{12,4},... | collective-permute-start | bytes 18440 | tf_op jit(solution)/shard_map/ppermute | solution.py:242
  29.0 0.8 collective-permute-done.1.rates_ref
  29.8 11.2 %all-to-all-done.parts_ref = bf16[32,24,256]{2,1,0:T(8,128)(2,1)S(1)} async-done(((bf16[32,24,256]{2,1,0:T(8,128)(2,1)}), bf16[32,24,256]{2,1,0:T(8,128)(2,1)S(1)}, u32[]{:S(2)}, u32[]{:S(2)}) %all-to-all-start) | async-done | bytes 393248 | tf_op jit(solution)/shard_map/all_to_all | solution.py:218
  41.0 0.1 total.2
  41.1 0.0 collective-permute-done.2.other_ref
  41.1 17.1 %all_to_all.25 = bf16[32,24,256]{2,1,0:T(8,128)(2,1)S(1)} all-to-all(bf16[32,24,256]{2,1,0:T(8,128)(2,1)S(1)} %get-tuple-element.49), channel_id=1, replica_groups=mesh['x'=4,'z'=8,'c'=2,'y'=8] {'z','x'}, dimensions={0} | all-to-all | bytes 786432 | tf_op jit(solution)/shard_map/all_to_all | solution.py:218
  58.2 2.5 %second.1 = (bf16[768,256]{1,0:T(8,128)(2,1)}, f32[1032,256]{1,0:T(8,128)S(1)}) custom-call(bf16[3,256,256]{2,1,0:T(8,128)(2,1)S(1)} %get-tuple-element.48.init_ref, bf16[768,256]{1,0:T(8,128)(2,1)S(1)} %bitcast.9, bf16[4,512,256]{2,1,0:T(8,128)(2,1)S(1)} %get-tuple-element.50.own_ref, bf16[4,512,256]{2,1,0:T(8,128)(2,1)S(1)} %collective-permute-done.2.other_ref, ...), custom_call_target="tpu_custom_call" | custom-call | tf_op jit(solution)/shard_map/second/pallas_call | solution.py:286
  60.7 18.6 %all_to_all.26.parts_ref = bf16[32,24,256]{2,1,0:T(8,128)(2,1)S(1)} all-to-all(bf16[32,24,256]{2,1,0:T(8,128)(2,1)} %bitcast.10), channel_id=1, replica_groups=mesh['x'=4,'z'=8,'c'=2,'y'=8] {'z','x'}, dimensions={0} | all-to-all | bytes 786432 | tf_op jit(solution)/shard_map/all_to_all | solution.py:218
  79.4 0.1 total.3
  79.5 0.0 copy-start.1
  79.5 0.7 copy-done.1
  80.2 5.6 %all-to-all-start.3 = ((bf16[32,24,256]{2,1,0:T(8,128)(2,1)}), bf16[32,24,256]{2,1,0:T(8,128)(2,1)S(1)}, u32[]{:S(2)}, u32[]{:S(2)}) async-start(bf16[32,24,256]{2,1,0:T(8,128)(2,1)} %copy-done.1), calls=%async_computation.3 | async-start | bytes 786432 | tf_op jit(solution)/shard_map/all_to_all | solution.py:218
  85.8 1.6 %apply_first.1 = (bf16[3,2,64,256]{3,2,1,0:T(8,128)(2,1)}, bf16[2,2,64,256]{3,2,1,0:T(8,128)(2,1)S(1)}, bf16[2,2,64,256]{3,2,1,0:T(8,128)(2,1)}, bf16[3,2,64,256]{3,2,1,0:T(8,128)(2,1)}, bf16[1,2,64,256]{3,2,1,0:T(8,128)(2,1)}) custom-call(s32[1]{0:T(128)} %bitcast.6.row_ref, f32[1032,256]{1,0:T(8,128)S(1)} %get-tuple-element.54.kept_ref, ...), custom_call_target="tpu_custom_call" | custom-call | tf_op jit(solution)/shard_map/apply_first/pallas_call | solution.py:298
  87.4 0.0 copy-start.2
  87.4 0.7 copy-done.2
  88.0 5.2 %collective-permute-start.3 = (bf16[3,2,64,256]{3,2,1,0:T(8,128)(2,1)}, bf16[3,2,64,256]{3,2,1,0:T(8,128)(2,1)}, u32[]{:S(2)}, u32[]{:S(2)}) collective-permute-start(bf16[3,2,64,256]{3,2,1,0:T(8,128)(2,1)} %get-tuple-element.57), channel_id=1, source_target_pairs={{0,3},{1,4},{2,5},{3,6},{4,7},{5,0},{6,1},{7,2},{8,11},{9,12},{10,... | collective-permute-start | bytes 589832 | tf_op jit(solution)/shard_map/ppermute | solution.py:311
  93.3 5.1 %all-to-all-done.3 = bf16[32,24,256]{2,1,0:T(8,128)(2,1)S(1)} async-done(((bf16[32,24,256]{2,1,0:T(8,128)(2,1)}), bf16[32,24,256]{2,1,0:T(8,128)(2,1)S(1)}, u32[]{:S(2)}, u32[]{:S(2)}) %all-to-all-start.3) | async-done | bytes 393248 | tf_op jit(solution)/shard_map/all_to_all | solution.py:218
  98.4 1.1 shard_map.57
  99.5 0.0 copy-start
  99.5 0.8 copy-done
  100.3 10.7 %all-to-all-start.4 = ((bf16[16,64,256]{2,1,0:T(8,128)(2,1)}), bf16[16,64,256]{2,1,0:T(8,128)(2,1)S(1)}, u32[]{:S(2)}, u32[]{:S(2)}) async-start(bf16[16,64,256]{2,1,0:T(8,128)(2,1)} %bitcast.7), calls=%async_computation.4 | async-start | bytes 1048576 | tf_op jit(solution)/shard_map/all_to_all | solution.py:218
  111.0 5.4 %collective-permute-start.4 = (bf16[2,2,64,256]{3,2,1,0:T(8,128)(2,1)}, bf16[2,2,64,256]{3,2,1,0:T(8,128)(2,1)S(1)}, u32[]{:S(2)}, u32[]{:S(2)}) collective-permute-start(bf16[2,2,64,256]{3,2,1,0:T(8,128)(2,1)} %copy-done.2), channel_id=1, source_target_pairs={{0,6},{1,7},{2,0},{3,1},{4,2},{5,3},{6,4},{7,5},{8,14},{9,15},{10,... | collective-permute-start | bytes 393224 | tf_op jit(solution)/shard_map/ppermute | solution.py:311
  116.4 0.0 collective-permute-done.3.refs_1_
  116.4 1.5 %slice_dynamic-update-slice_fusion.1 = (bf16[3,2,64,256]{3,2,1,0:T(8,128)(2,1)}, bf16[2,2,64,256]{3,2,1,0:T(8,128)(2,1)}) fusion(bf16[3,2,64,256]{3,2,1,0:T(8,128)(2,1)} %get-tuple-element.60, bf16[3,2,64,256]{3,2,1,0:T(8,128)(2,1)} %collective-permute-done.3.refs_1_, bf16[2,2,64,256]{3,2,1,0:T(8,128)(2,1)} %get-tuple-element.59), kind=kLoop, calls=%fused_computation.2 | loop fusion | bytes 262144 | tf_op jit(solution)/shard_map/dynamic_update_slice | solution.py:316
  118.0 13.1 %collective-permute-done.4.refs_2_ = bf16[2,2,64,256]{3,2,1,0:T(8,128)(2,1)S(1)} collective-permute-done((bf16[2,2,64,256]{3,2,1,0:T(8,128)(2,1)}, bf16[2,2,64,256]{3,2,1,0:T(8,128)(2,1)S(1)}, u32[]{:S(2)}, u32[]{:S(2)}) %collective-permute-start.4) | collective-permute-done | bytes 131104 | tf_op jit(solution)/shard_map/ppermute | solution.py:311
  131.1 0.6 slice_dynamic-update-slice_fusion
  131.7 1.9 %collective-permute-start.6 = (bf16[3,2,64,256]{3,2,1,0:T(8,128)(2,1)}, bf16[3,2,64,256]{3,2,1,0:T(8,128)(2,1)S(1)}, u32[]{:S(2)}, u32[]{:S(2)}) collective-permute-start(bf16[3,2,64,256]{3,2,1,0:T(8,128)(2,1)} %slice_dynamic-update-slice_fusion), channel_id=1, source_target_pairs={{0,7},{1,0},{2,1},{3,2},{4,3},{5,4},{6,5},{7,6},{8,15},{9,8},{10,9... | collective-permute-start | bytes 589832 | tf_op jit(solution)/shard_map/ppermute | solution.py:311
  133.6 3.4 %collective-permute-start.5 = (bf16[2,2,64,256]{3,2,1,0:T(8,128)(2,1)}, bf16[2,2,64,256]{3,2,1,0:T(8,128)(2,1)S(1)}, u32[]{:S(2)}, u32[]{:S(2)}) collective-permute-start(bf16[2,2,64,256]{3,2,1,0:T(8,128)(2,1)} %get-tuple-element.62), channel_id=1, source_target_pairs={{0,1},{1,2},{2,3},{3,4},{4,5},{5,6},{6,7},{7,0},{8,9},{9,10},{10,1... | collective-permute-start | bytes 393224 | tf_op jit(solution)/shard_map/ppermute | solution.py:311
  137.0 3.8 %collective-permute-done.5.refs_3_ = bf16[2,2,64,256]{3,2,1,0:T(8,128)(2,1)S(1)} collective-permute-done((bf16[2,2,64,256]{3,2,1,0:T(8,128)(2,1)}, bf16[2,2,64,256]{3,2,1,0:T(8,128)(2,1)S(1)}, u32[]{:S(2)}, u32[]{:S(2)}) %collective-permute-start.5) | collective-permute-done | bytes 131104 | tf_op jit(solution)/shard_map/ppermute | solution.py:311
  140.8 0.0 collective-permute-done.6.refs_4_
  140.8 1.0 collect.1
  141.7 4.1 %collective-permute-start.7 = (bf16[8,64,256]{2,1,0:T(8,128)(2,1)S(1)}, bf16[8,64,256]{2,1,0:T(8,128)(2,1)S(1)}, u32[]{:S(2)}, u32[]{:S(2)}) collective-permute-start(bf16[8,64,256]{2,1,0:T(8,128)(2,1)S(1)} %collect.1), channel_id=1, source_target_pairs={{0,8},{8,0},{1,9},{9,1},{2,10},{10,2},{3,11},{11,3},{4,12},{12,4},... | collective-permute-start | bytes 786440 | tf_op jit(solution)/shard_map/ppermute | solution.py:242
  145.9 1.1 collective-permute-done.7.refs_5_
  147.0 1.8 %assemble_first.1.prev_ref = bf16[2,64,4096]{2,1,0:T(8,128)(2,1)} custom-call(s32[1]{0:T(128)} %bitcast.at.core_ref, s32[1]{0:T(128)} %bitcast.6.row_ref, bf16[1,2,64,256]{3,2,1,0:T(8,128)(2,1)} %get-tuple-element.56.refs_0_, bf16[3,2,64,256]{3,2,1,0:T(8,128)(2,1)} %collective-permute-done.3.refs_1_, ...), custom_call_target="tpu_custom_call" | custom-call | tf_op jit(solution)/shard_map/assemble_first/pallas_call | solution.py:335
  148.8 0.0 all-to-all-done.4.parts_ref
  148.8 0.8 assemble_second.1
Async XLA Ops:
  2.9 10.1 %collective-permute-start = (bf16[768,256]{1,0:T(8,128)(2,1)S(1)}, bf16[768,256]{1,0:T(8,128)(2,1)S(1)}, u32[]{:S(2)}, u32[]{:S(2)}) collective-permute-start(bf16[768,256]{1,0:T(8,128)(2,1)S(1)} %get-tuple-element.34), channel_id=1, source_target_pairs={{0,8},{8,0},{1,9},{9,1},{2,10},{10,2},{3,11},{11,3},{4,12},{12,4},... | collective-permute-start | bytes 1179656 | tf_op jit(solution)/shard_map/ppermute | solution.py:242
  16.8 24.3 %collective-permute-start.2 = (bf16[4,512,256]{2,1,0:T(8,128)(2,1)}, bf16[4,512,256]{2,1,0:T(8,128)(2,1)S(1)}, u32[]{:S(2)}, u32[]{:S(2)}) collective-permute-start(bf16[4,512,256]{2,1,0:T(8,128)(2,1)} %get-tuple-element.43), channel_id=1, source_target_pairs={{0,8},{8,0},{1,9},{9,1},{2,10},{10,2},{3,11},{11,3},{4,12},{12,4},... | collective-permute-start | bytes 3145736 | tf_op jit(solution)/shard_map/ppermute | solution.py:242
  19.1 21.9 %all-to-all-start = ((bf16[32,24,256]{2,1,0:T(8,128)(2,1)}), bf16[32,24,256]{2,1,0:T(8,128)(2,1)S(1)}, u32[]{:S(2)}, u32[]{:S(2)}) async-start(bf16[32,24,256]{2,1,0:T(8,128)(2,1)} %bitcast.1), calls=%async_computation | async-start | bytes 786432 | tf_op jit(solution)/shard_map/all_to_all | solution.py:218
  26.6 3.1 %collective-permute-start.1 = (f32[3,512]{1,0:T(4,128)S(1)}, f32[3,512]{1,0:T(4,128)S(1)}, u32[]{:S(2)}, u32[]{:S(2)}) collective-permute-start(f32[3,512]{1,0:T(4,128)S(1)} %get-tuple-element.41), channel_id=1, source_target_pairs={{0,8},{8,0},{1,9},{9,1},{2,10},{10,2},{3,11},{11,3},{4,12},{12,4},... | collective-permute-start | bytes 18440 | tf_op jit(solution)/shard_map/ppermute | solution.py:242
  79.5 0.7 copy-start.1
  80.2 18.2 %all-to-all-start.3 = ((bf16[32,24,256]{2,1,0:T(8,128)(2,1)}), bf16[32,24,256]{2,1,0:T(8,128)(2,1)S(1)}, u32[]{:S(2)}, u32[]{:S(2)}) async-start(bf16[32,24,256]{2,1,0:T(8,128)(2,1)} %copy-done.1), calls=%async_computation.3 | async-start | bytes 786432 | tf_op jit(solution)/shard_map/all_to_all | solution.py:218
  87.4 0.7 copy-start.2
  88.0 28.4 %collective-permute-start.3 = (bf16[3,2,64,256]{3,2,1,0:T(8,128)(2,1)}, bf16[3,2,64,256]{3,2,1,0:T(8,128)(2,1)}, u32[]{:S(2)}, u32[]{:S(2)}) collective-permute-start(bf16[3,2,64,256]{3,2,1,0:T(8,128)(2,1)} %get-tuple-element.57), channel_id=1, source_target_pairs={{0,3},{1,4},{2,5},{3,6},{4,7},{5,0},{6,1},{7,2},{8,11},{9,12},{10,... | collective-permute-start | bytes 589832 | tf_op jit(solution)/shard_map/ppermute | solution.py:311
  99.5 0.8 copy-start
  100.3 48.5 %all-to-all-start.4 = ((bf16[16,64,256]{2,1,0:T(8,128)(2,1)}), bf16[16,64,256]{2,1,0:T(8,128)(2,1)S(1)}, u32[]{:S(2)}, u32[]{:S(2)}) async-start(bf16[16,64,256]{2,1,0:T(8,128)(2,1)} %bitcast.7), calls=%async_computation.4 | async-start | bytes 1048576 | tf_op jit(solution)/shard_map/all_to_all | solution.py:218
  111.0 20.0 %collective-permute-start.4 = (bf16[2,2,64,256]{3,2,1,0:T(8,128)(2,1)}, bf16[2,2,64,256]{3,2,1,0:T(8,128)(2,1)S(1)}, u32[]{:S(2)}, u32[]{:S(2)}) collective-permute-start(bf16[2,2,64,256]{3,2,1,0:T(8,128)(2,1)} %copy-done.2), channel_id=1, source_target_pairs={{0,6},{1,7},{2,0},{3,1},{4,2},{5,3},{6,4},{7,5},{8,14},{9,15},{10,... | collective-permute-start | bytes 393224 | tf_op jit(solution)/shard_map/ppermute | solution.py:311
  131.7 9.1 %collective-permute-start.6 = (bf16[3,2,64,256]{3,2,1,0:T(8,128)(2,1)}, bf16[3,2,64,256]{3,2,1,0:T(8,128)(2,1)S(1)}, u32[]{:S(2)}, u32[]{:S(2)}) collective-permute-start(bf16[3,2,64,256]{3,2,1,0:T(8,128)(2,1)} %slice_dynamic-update-slice_fusion), channel_id=1, source_target_pairs={{0,7},{1,0},{2,1},{3,2},{4,3},{5,4},{6,5},{7,6},{8,15},{9,8},{10,9... | collective-permute-start | bytes 589832 | tf_op jit(solution)/shard_map/ppermute | solution.py:311
  133.6 7.1 %collective-permute-start.5 = (bf16[2,2,64,256]{3,2,1,0:T(8,128)(2,1)}, bf16[2,2,64,256]{3,2,1,0:T(8,128)(2,1)S(1)}, u32[]{:S(2)}, u32[]{:S(2)}) collective-permute-start(bf16[2,2,64,256]{3,2,1,0:T(8,128)(2,1)} %get-tuple-element.62), channel_id=1, source_target_pairs={{0,1},{1,2},{2,3},{3,4},{4,5},{5,6},{6,7},{7,0},{8,9},{9,10},{10,1... | collective-permute-start | bytes 393224 | tf_op jit(solution)/shard_map/ppermute | solution.py:311
  141.7 5.3 %collective-permute-start.7 = (bf16[8,64,256]{2,1,0:T(8,128)(2,1)S(1)}, bf16[8,64,256]{2,1,0:T(8,128)(2,1)S(1)}, u32[]{:S(2)}, u32[]{:S(2)}) collective-permute-start(bf16[8,64,256]{2,1,0:T(8,128)(2,1)S(1)} %collect.1), channel_id=1, source_target_pairs={{0,8},{8,0},{1,9},{9,1},{2,10},{10,2},{3,11},{11,3},{4,12},{12,4},... | collective-permute-start | bytes 786440 | tf_op jit(solution)/shard_map/ppermute | solution.py:242
